TPU v7x, 32 devices: a whole 2x2x4 slice. The times are simulated.
32 devices in a mesh: dp: 4 (over y, x), expert: 8 (over z, core).
Axes of the slice: x: 2, y: 2, z: 4, core: 2. Of those that a mesh axis runs over, the one named last changes fastest.
Arguments:
- block_input: bfloat16 [6304, 768], P(('dp', 'expert')), may hold values from -12 to 12
- w_qkv: bfloat16 [768, 2304], P('dp'), may hold values from -0.21875 to 0.21875
- b_q: bfloat16 [768], P('dp'), may hold values from -3 to 3
- b_v: bfloat16 [768], P('dp'), may hold values from -3 to 3
- w_proj: bfloat16 [768, 768], P('dp'), may hold values from -1.75 to 1.75
- b_proj: bfloat16 [768], P('dp'), may hold values from -3 to 3
- ln1_gain: bfloat16 [768], P('dp'), may hold values from 0.099609375 to 1.8984375
- ln1_bias: bfloat16 [768], P('dp'), may hold values from -3 to 3
- ln2_gain: bfloat16 [768], P('dp'), may hold values from 0.099609375 to 1.8984375
- ln2_bias: bfloat16 [768], P('dp'), may hold values from -3 to 3
- w_router: bfloat16 [768, 8], P('dp'), may hold values from -0.4375 to 0.4375
- w_in: bfloat16 [8, 768, 3072], P('expert'), may hold values from -0.21875 to 0.21875
- b_in: bfloat16 [8, 3072], P('expert'), may hold values from -3 to 3
- w_out: bfloat16 [8, 3072, 768], P('expert'), may hold values from -0.109375 to 0.109375
- b_out: bfloat16 [8, 768], P('expert'), may hold values from -3 to 3
- routes: int32 [6304, 2], P(('dp', 'expert')), may hold values from 0 to 7, as said below
- slot_index: int32 [6304, 2], P(('dp', 'expert')), may hold values from 0 to 49, as said below
- d_out: bfloat16 [6304, 768], P(('dp', 'expert')), may hold values from -6 to 6
Outputs:
- block_out: bfloat16 [6304, 768], P(('dp', 'expert'))
- grad_input: float32 [6304, 768], P(('dp', 'expert'))
- d_w_qkv: float32 [768, 2304], P('dp')
- d_b_q: float32 [768], P('dp')
- d_b_v: float32 [768], P('dp')
- d_w_proj: float32 [768, 768], P('dp')
- d_b_proj: float32 [768], P('dp')
- d_ln1_gain: float32 [768], P('dp')
- d_ln1_bias: float32 [768], P('dp')
- d_ln2_gain: float32 [768], P('dp')
- d_ln2_bias: float32 [768], P('dp')
- d_w_router: float32 [768, 8], P('dp')
- d_w_in: float32 [8, 768, 3072], P('expert', 'dp')
- d_b_in: float32 [8, 3072], P('expert', 'dp')
- d_w_out: float32 [8, 3072, 768], P('expert', 'dp')
- d_b_out: float32 [8, 768], P('expert', 'dp')
Inputs may be any that keep to these rules, and one draw needn't show every extreme that they name: `routes`: each token names two different experts. slot_index[t, k] is the arrival position of choice k of token t at expert routes[t, k] among the tokens of one device, all first choices in token order before all second choices; 49 marks a choice that arrives beyond capacity and is dropped. In every draw one expert receives more than 49 first choices from every device.
All inputs are finite; a program needn't handle non-finite values.
Results may differ from a plain program's by a relative error of at most 0.012.
The roundings to bfloat16 on the way count: a program that leaves them out, or rounds other values in their place, can miss the bound.
Values may be sent and summed in bfloat16 or wider, within the bound.
No kernel may reach another device: no remote copies, remote signals or barrier semaphores. Data moves between devices by JAX's collectives and lax.ppermute only.
A program may use at most 128 MiB of HBM per device.

v0:
```python
import math

import jax
import jax.numpy as jnp
from jax import lax
from jax.sharding import PartitionSpec as P

HEAD_DIM = 64
SEQ = 197


NORM_EPS = 1e-06
SQRT_HALF = 0.7071067811865476
INV_ROOT_TWO_PI = 0.3989422804014327


def normalize(values):
    center = values - jnp.mean(values, axis=-1, keepdims=True)
    inv_std = lax.rsqrt(jnp.mean(center * center, axis=-1, keepdims=True) + NORM_EPS)
    return (center * inv_std, inv_std)


def norm_back(grad_in, normed, inv_std, gain_vec):
    scaled = grad_in * gain_vec
    mean_plain = jnp.mean(scaled, axis=-1, keepdims=True)
    mean_mixed = jnp.mean(scaled * normed, axis=-1, keepdims=True)
    return inv_std * (scaled - mean_plain - normed * mean_mixed)


def gelu_value(pre_act):
    return 0.5 * pre_act * (1.0 + lax.erf(pre_act * SQRT_HALF))


def gelu_slope(pre_act):
    return 0.5 * (1.0 + lax.erf(pre_act * SQRT_HALF)) + pre_act * INV_ROOT_TWO_PI * jnp.exp(
        -0.5 * pre_act * pre_act
    )


def by_heads(values, images):
    return values.reshape(images, SEQ, values.shape[1] // HEAD_DIM, HEAD_DIM)


def unpack(full_vectors):
    wide_vectors = full_vectors.astype(jnp.float32)
    return tuple((wide_vectors[index] for index in range(7)))


def slot_tables(routes, slot_table, experts, capacity):
    kept_mask = slot_table < capacity
    target = jnp.where(kept_mask, routes * capacity + slot_table, -1).reshape(-1)
    slot_match = target[:, None] == lax.broadcasted_iota(jnp.int32, (1, experts * capacity), 1)
    filled = jnp.any(slot_match, axis=0)
    choice_ids = lax.broadcasted_iota(jnp.int32, (target.shape[0], 1), 0)
    source = jnp.sum(jnp.where(slot_match, choice_ids, 0), axis=0, dtype=jnp.int32)
    return (kept_mask.reshape(-1), jnp.maximum(target, 0), filled, source)


def per_device(
    block_input,
    w_qkv,
    b_q,
    b_v,
    w_proj,
    b_proj,
    ln1_gain,
    ln1_bias,
    ln2_gain,
    ln2_bias,
    w_router,
    w_in,
    b_in,
    w_out,
    b_out,
    routes,
    slot_index,
    d_out,
):
    tokens = block_input.shape[0]
    width = block_input.shape[1]
    images = tokens // SEQ
    local_count = w_in.shape[0]
    hidden_units = w_in.shape[2]
    experts = local_count * lax.axis_size("expert")
    capacity = 2 * tokens // experts
    score_scale = 1.0 / math.sqrt(HEAD_DIM)
    vectors = jnp.stack([b_q, b_v, b_proj, ln1_gain, ln1_bias, ln2_gain, ln2_bias])
    full_qkv, full_proj, full_router, full_vectors = (
        lax.all_gather(w_qkv, "dp", axis=0, tiled=True),
        lax.all_gather(w_proj, "dp", axis=0, tiled=True),
        lax.all_gather(w_router, "dp", axis=0, tiled=True),
        lax.all_gather(vectors, "dp", axis=1, tiled=True),
    )
    bias_q, bias_v, bias_proj, gain_one, bias_one, gain_two, bias_two = unpack(full_vectors)
    resid = block_input.astype(jnp.float32)
    normed_one, inv_one = normalize(resid)
    a_in = (normed_one * gain_one + bias_one).astype(jnp.bfloat16)
    qkv = jnp.dot(a_in, full_qkv, preferred_element_type=jnp.float32)
    queries = (qkv[:, :width] + bias_q).astype(jnp.bfloat16)
    key_vecs = qkv[:, width : 2 * width].astype(jnp.bfloat16)
    values = (qkv[:, 2 * width :] + bias_v).astype(jnp.bfloat16)
    query_heads = by_heads(queries, images)
    key_heads = by_heads(key_vecs, images)
    value_heads = by_heads(values, images)
    scores = (
        jnp.einsum("bqhd,bkhd->bhqk", query_heads, key_heads, preferred_element_type=jnp.float32)
        * score_scale
    )
    row_max = jnp.max(scores, axis=-1, keepdims=True)
    exp_scores = jnp.exp(scores - row_max)
    row_total = jnp.sum(exp_scores, axis=-1, keepdims=True)
    log_total = row_max + jnp.log(row_total)
    probs_low = (exp_scores / row_total).astype(jnp.bfloat16)
    context = (
        jnp.einsum("bhqk,bkhd->bqhd", probs_low, value_heads, preferred_element_type=jnp.float32)
        .reshape(tokens, width)
        .astype(jnp.bfloat16)
    )
    hidden = resid + jnp.dot(context, full_proj, preferred_element_type=jnp.float32) + bias_proj
    normed_two, inv_two = normalize(hidden)
    y_in = (normed_two * gain_two + bias_two).astype(jnp.bfloat16)
    logits = jnp.dot(y_in, full_router, preferred_element_type=jnp.float32)
    route_hot = (routes[:, :, None] == lax.broadcasted_iota(jnp.int32, (1, 1, experts), 2)).astype(
        jnp.float32
    )
    chosen = jnp.sum(logits[:, None, :] * route_hot, axis=-1)
    first_gate = jax.nn.sigmoid(chosen[:, 0] - chosen[:, 1])
    gate_vals = jnp.stack([first_gate, 1.0 - first_gate], axis=1)
    kept_flat, fetch_index, filled, source = slot_tables(routes, slot_index, experts, capacity)
    sent_slots = jnp.where(filled[:, None], y_in[source // 2], 0).reshape(experts, capacity, width)
    bias_in = b_in.astype(jnp.float32)
    bias_out = b_out.astype(jnp.float32)
    received = lax.all_to_all(sent_slots, "expert", split_axis=0, concat_axis=0, tiled=True)
    slot_count = received.shape[1]
    grouped = received.reshape(-1, local_count, slot_count, width)
    pre_act = (
        jnp.einsum("necd,edf->necf", grouped, w_in, preferred_element_type=jnp.float32)
        + bias_in[None, :, None, :]
    )
    activated = gelu_value(pre_act).astype(jnp.bfloat16)
    down_proj = (
        jnp.einsum("necf,efd->necd", activated, w_out, preferred_element_type=jnp.float32)
        + bias_out[None, :, None, :]
    )
    received, pre_all, act_all, expert_out = (
        received,
        pre_act.reshape(-1, slot_count, hidden_units),
        activated.reshape(-1, slot_count, hidden_units),
        down_proj.astype(jnp.bfloat16).reshape(-1, slot_count, width),
    )
    returned = lax.all_to_all(expert_out, "expert", split_axis=0, concat_axis=0, tiled=True)
    picked = jnp.where(
        kept_flat[:, None],
        returned.reshape(experts * capacity, width)[fetch_index].astype(jnp.float32),
        0.0,
    ).reshape(tokens, 2, width)
    block_out = (hidden + jnp.sum(gate_vals[:, :, None] * picked, axis=1)).astype(jnp.bfloat16)
    grad_out = d_out.astype(jnp.float32)
    d_choice = (
        (gate_vals[:, :, None] * grad_out[:, None, :])
        .reshape(2 * tokens, width)
        .astype(jnp.bfloat16)
    )
    d_sent = jnp.where(filled[:, None], d_choice[source], 0).reshape(experts, capacity, width)
    d_gate = jnp.sum(grad_out[:, None, :] * picked, axis=-1)
    d_diff = (d_gate[:, 0] - d_gate[:, 1]) * gate_vals[:, 0] * gate_vals[:, 1]
    d_logits = (d_diff[:, None] * (route_hot[:, 0] - route_hot[:, 1])).astype(jnp.bfloat16)
    d_received = lax.all_to_all(d_sent, "expert", split_axis=0, concat_axis=0, tiled=True)
    grad_rows = d_received.reshape(-1, local_count, capacity, width)
    act_rows = act_all.reshape(-1, local_count, capacity, hidden_units)
    pre_rows = pre_all.reshape(-1, local_count, capacity, hidden_units)
    recv_rows = received.reshape(-1, local_count, capacity, width)
    d_b_out = jnp.sum(grad_rows.astype(jnp.float32), axis=(0, 2))
    d_w_out = jnp.einsum("necf,necd->efd", act_rows, grad_rows, preferred_element_type=jnp.float32)
    d_pre = jnp.einsum(
        "necd,efd->necf", grad_rows, w_out, preferred_element_type=jnp.float32
    ) * gelu_slope(pre_rows)
    d_b_in = jnp.sum(d_pre, axis=(0, 2))
    d_pre_low = d_pre.astype(jnp.bfloat16)
    d_w_in = jnp.einsum("necd,necf->edf", recv_rows, d_pre_low, preferred_element_type=jnp.float32)
    d_expert_in = (
        jnp.einsum("necf,edf->necd", d_pre_low, w_in, preferred_element_type=jnp.float32)
        .astype(jnp.bfloat16)
        .reshape(-1, capacity, width)
    )
    d_returned = lax.all_to_all(d_expert_in, "expert", split_axis=0, concat_axis=0, tiled=True)
    part_w_in, part_w_out, part_b_in, part_b_out = (
        lax.psum_scatter(d_w_in, "dp", scatter_dimension=1, tiled=True),
        lax.psum_scatter(d_w_out, "dp", scatter_dimension=1, tiled=True),
        lax.psum_scatter(d_b_in, "dp", scatter_dimension=1, tiled=True),
        lax.psum_scatter(d_b_out, "dp", scatter_dimension=1, tiled=True),
    )
    full_qkv, full_proj, full_router, full_vectors = (
        lax.all_gather(w_qkv, "dp", axis=0, tiled=True),
        lax.all_gather(w_proj, "dp", axis=0, tiled=True),
        lax.all_gather(w_router, "dp", axis=0, tiled=True),
        lax.all_gather(vectors, "dp", axis=1, tiled=True),
    )
    bias_q, bias_v, bias_proj, gain_one, bias_one, gain_two, bias_two = unpack(full_vectors)
    back_rows = jnp.where(
        kept_flat[:, None],
        d_returned.reshape(experts * capacity, width)[fetch_index].astype(jnp.float32),
        0.0,
    ).reshape(tokens, 2, width)
    d_w_router = jnp.einsum("td,te->de", y_in, d_logits, preferred_element_type=jnp.float32)
    d_y = jnp.sum(back_rows, axis=1) + jnp.einsum(
        "te,de->td", d_logits, full_router, preferred_element_type=jnp.float32
    )
    d_gain_two = jnp.sum(d_y * normed_two, axis=0)
    d_bias_two = jnp.sum(d_y, axis=0)
    d_hidden = grad_out + norm_back(d_y, normed_two, inv_two, gain_two)
    d_b_proj = jnp.sum(d_hidden, axis=0)
    d_hidden_low = d_hidden.astype(jnp.bfloat16)
    d_w_proj = jnp.einsum("td,te->de", context, d_hidden_low, preferred_element_type=jnp.float32)
    d_context = jnp.einsum(
        "te,de->td", d_hidden_low, full_proj, preferred_element_type=jnp.float32
    ).astype(jnp.bfloat16)
    grad_heads = by_heads(d_context, images)
    probs = jnp.exp(
        jnp.einsum("bqhd,bkhd->bhqk", query_heads, key_heads, preferred_element_type=jnp.float32)
        * score_scale
        - log_total
    )
    d_probs = jnp.einsum(
        "bqhd,bkhd->bhqk", grad_heads, value_heads, preferred_element_type=jnp.float32
    )
    d_values = jnp.einsum(
        "bhqk,bqhd->bkhd",
        probs.astype(jnp.bfloat16),
        grad_heads,
        preferred_element_type=jnp.float32,
    ).reshape(tokens, width)
    row_delta = jnp.sum(probs * d_probs, axis=-1, keepdims=True)
    d_scores = (probs * (d_probs - row_delta) * score_scale).astype(jnp.bfloat16)
    d_queries = jnp.einsum(
        "bhqk,bkhd->bqhd", d_scores, key_heads, preferred_element_type=jnp.float32
    ).reshape(tokens, width)
    d_keys = jnp.einsum(
        "bhqk,bqhd->bkhd", d_scores, query_heads, preferred_element_type=jnp.float32
    ).reshape(tokens, width)
    d_b_q = jnp.sum(d_queries, axis=0)
    d_b_v = jnp.sum(d_values, axis=0)
    d_qkv = jnp.concatenate([d_queries, d_keys, d_values], axis=1).astype(jnp.bfloat16)
    d_w_qkv = jnp.einsum("td,te->de", a_in, d_qkv, preferred_element_type=jnp.float32)
    d_a = jnp.einsum("te,de->td", d_qkv, full_qkv, preferred_element_type=jnp.float32)
    d_gain_one = jnp.sum(d_a * normed_one, axis=0)
    d_bias_one = jnp.sum(d_a, axis=0)
    d_input = d_hidden + norm_back(d_a, normed_one, inv_one, gain_one)
    grad_vectors = jnp.stack(
        [d_b_q, d_b_v, d_b_proj, d_gain_one, d_bias_one, d_gain_two, d_bias_two]
    )
    part_qkv, part_proj, part_router, part_vectors = (
        lax.psum_scatter(d_w_qkv, "dp", scatter_dimension=0, tiled=True),
        lax.psum_scatter(d_w_proj, "dp", scatter_dimension=0, tiled=True),
        lax.psum_scatter(d_w_router, "dp", scatter_dimension=0, tiled=True),
        lax.psum_scatter(grad_vectors, "dp", scatter_dimension=1, tiled=True),
    )
    sum_qkv, sum_proj, sum_router, sum_vectors = lax.psum(
        (part_qkv, part_proj, part_router, part_vectors), "expert"
    )
    return (
        block_out,
        d_input,
        sum_qkv,
        sum_vectors[0],
        sum_vectors[1],
        sum_proj,
        sum_vectors[2],
        sum_vectors[3],
        sum_vectors[4],
        sum_vectors[5],
        sum_vectors[6],
        sum_router,
        part_w_in,
        part_b_in,
        part_w_out,
        part_b_out,
    )


def solution(mesh):
    return jax.shard_map(
        per_device,
        mesh=mesh,
        in_specs=(
            P(("dp", "expert"), None),
            P("dp", None),
            P("dp"),
            P("dp"),
            P("dp", None),
            P("dp"),
            P("dp"),
            P("dp"),
            P("dp"),
            P("dp"),
            P("dp", None),
            P("expert", None, None),
            P("expert", None),
            P("expert", None, None),
            P("expert", None),
            P(("dp", "expert"), None),
            P(("dp", "expert"), None),
            P(("dp", "expert"), None),
        ),
        out_specs=(
            P(("dp", "expert"), None),
            P(("dp", "expert"), None),
            P("dp", None),
            P("dp"),
            P("dp"),
            P("dp", None),
            P("dp"),
            P("dp"),
            P("dp"),
            P("dp"),
            P("dp"),
            P("dp", None),
            P("expert", "dp", None),
            P("expert", "dp"),
            P("expert", "dp", None),
            P("expert", "dp"),
        ),
        check_vma=False,
    )
```

profile of v0, /device:TPU:0, one launch (start us, length us, event | category | flops | bytes accessed | tf_op | source)
XLA Modules:
  0.0 757.5 jit_solution(14147222516695071942)
XLA Ops:
  18.7 9.8 %all-gather = bf16[4,192,7]{1,2,0:T(8,128)(2,1)S(1)} all-gather(bf16[1,192,7]{1,2,0:T(8,128)(2,1)S(1)} %bitcast.203), channel_id=1, replica_groups=mesh['dp'=4,'expert'=8] {'dp'}, dimensions={0}, use_global_device_ids=true | all-gather | bytes 13440 | tf_op jit(solution)/shard_map/all_gather | solution.py:92
  29.9 30.1 %all-gather.5.cloned.1.call-done = bf16[768,2304]{1,0:T(8,128)(2,1)} async-done(((bf16[192,2304]{1,0:T(8,128)(2,1)}), bf16[768,2304]{1,0:T(8,128)(2,1)}) %all-gather.5.cloned.1.call-update) | async-done | bytes 3538960 | tf_op jit(solution)/shard_map/all_gather | solution.py:89
  69.3 20.2 %all-gather.7.cloned.1.call-done = bf16[768,768]{1,0:T(8,128)(2,1)} async-done(((bf16[192,768]{1,0:T(8,128)(2,1)}), bf16[768,768]{1,0:T(8,128)(2,1)}) %all-gather.7.cloned.1.call-update) | async-done | bytes 1179664 | tf_op jit(solution)/shard_map/all_gather | solution.py:90
  103.5 18.8 %all-to-all-done = bf16[8,49,768]{2,1,0:T(8,128)(2,1)S(1)} async-done(((bf16[8,49,768]{2,1,0:T(8,128)(2,1)}), bf16[8,49,768]{2,1,0:T(8,128)(2,1)S(1)}, u32[]{:S(2)}, u32[]{:S(2)}) %all-to-all-start) | async-done | bytes 602144 | tf_op jit(solution)/shard_map/all_to_all | solution.py:133
  122.3 7.4 fusion.12
  129.8 7.1 fusion.44
  141.1 8.3 %all-gather.1 = bf16[4,192,8]{1,2,0:T(8,128)(2,1)S(1)} all-gather(bf16[1,192,8]{1,2,0:T(8,128)(2,1)S(1)} %bitcast.211), channel_id=1, replica_groups=mesh['dp'=4,'expert'=8] {'dp'}, dimensions={0}, use_global_device_ids=true | all-gather | bytes 15360 | tf_op jit(solution)/shard_map/all_gather | solution.py:91
  155.2 4.8 all-to-all-done.1
  173.1 21.5 %all_to_all.20 = bf16[8,49,768]{2,1,0:T(8,128)(2,1)S(1)} all-to-all(bf16[8,49,768]{2,1,0:T(8,128)(2,1)S(1)} %broadcast_select_fusion), channel_id=1, replica_groups=mesh['dp'=4,'expert'=8] {'expert'}, dimensions={0} | all-to-all | bytes 1204224 | tf_op jit(solution)/shard_map/all_to_all | solution.py:168
  194.7 7.4 fusion.104
  213.3 16.8 %all-to-all-done.3 = bf16[8,49,768]{2,1,0:T(8,128)(2,1)} async-done(((bf16[8,49,768]{2,1,0:T(8,128)(2,1)}), bf16[8,49,768]{2,1,0:T(8,128)(2,1)}, u32[]{:S(2)}, u32[]{:S(2)}) %all-to-all-start.3) | async-done | bytes 602144 | tf_op jit(solution)/shard_map/all_to_all | solution.py:186
  236.9 7.8 %select_reduce_fusion = (f32[197,768]{1,0:T(8,128)S(1)}, f32[197,768]{1,0:T(8,128)S(1)}) fusion(f32[197,2,768]{2,1,0:T(2,128)} %reshape.385, pred[197,2]{1,0:T(8,128)(4,1)S(1)} %copy-done.27, f32[197,2,768]{2,1,0:T(2,128)} %reshape.384, f32[197,2]{1,0:T(8,128)S(1)} %copy.100), kind=kLoop, calls=%fused_computation.57 | loop fusion | flops 1210368 | bytes 3633074 | tf_op jit(solution)/shard_map/reduce_sum | solution.py:206
  261.5 4.8 fusion.98
  284.6 79.7 %reduce-scatter.17.cloned.1.call-done = f32[192,2304]{1,0:T(8,128)} async-done(((f32[768,2304]{1,0:T(8,128)}), f32[192,2304]{1,0:T(8,128)}) %reduce-scatter.17.cloned.1.call-update) | async-done | bytes 1769488 | tf_op jit(solution)/shard_map/reduce_scatter | solution.py:253
  364.4 6.9 convolution_bitcast_fusion
  372.4 7.0 convolution_bitcast_fusion.1
  379.3 12.0 %reduce-scatter.27.cloned.1.call-done = f32[192,8]{1,0:T(8,128)} async-done(((f32[768,8]{1,0:T(8,128)}), f32[192,8]{1,0:T(8,128)}) %reduce-scatter.27.cloned.1.call-update) | async-done | bytes 6160
  392.3 26.1 %reduce-scatter.31.cloned.1.call-done = f32[192,1]{1,0:T(8,128)} async-done(((f32[768,1]{1,0:T(8,128)}), f32[192,1]{1,0:T(8,128)}) %reduce-scatter.31.cloned.1.call-update) | async-done | bytes 784
  420.0 33.0 %reduce-scatter.29.cloned.1.call-done = f32[768,1]{1,0:T(8,128)} async-done(((f32[3072,1]{1,0:T(8,128)}), f32[768,1]{1,0:T(8,128)}) %reduce-scatter.29.cloned.1.call-update) | async-done | bytes 3088
  455.8 25.0 %reduce-scatter.25.cloned.1.call-done = f32[192,7]{1,0:T(8,128)} async-done(((f32[768,7]{1,0:T(8,128)}), f32[192,7]{1,0:T(8,128)}) %reduce-scatter.25.cloned.1.call-update) | async-done | bytes 5392
  481.7 29.6 %all-reduce = (f32[7,192]{1,0:T(8,128)S(1)}, f32[192,8]{0,1:T(8,128)}) all-reduce(f32[7,192]{1,0:T(8,128)S(1)} %copy.117, f32[192,8]{0,1:T(8,128)S(1)} %copy.119), channel_id=1, replica_groups=mesh['dp'=4,'expert'=8] {'expert'}, use_global_device_ids=true, to_apply=%region_27.28 | all-reduce | flops 2880 | bytes 23040 | tf_op jit(solution)/shard_map/psum | solution.py:258
  511.9 38.6 %all-reduce.4.cloned.1.call-done = (f32[192,2304]{1,0:T(8,128)}, f32[192,768]{1,0:T(8,128)}) async-done(((f32[192,2304]{1,0:T(8,128)}, f32[192,768]{1,0:T(8,128)}), (f32[192,2304]{1,0:T(8,128)}, f32[192,768]{1,0:T(8,128)})) %all-reduce.4.cloned.1.call-update) | async-done | bytes 2359312 | tf_op jit(solution)/shard_map/psum | solution.py:258
  550.5 97.7 %reduce-scatter.23.cloned.1.call-done = f32[1,768,768]{2,1,0:T(8,128)} async-done(((f32[1,3072,768]{2,1,0:T(8,128)}), f32[1,768,768]{2,1,0:T(8,128)}) %reduce-scatter.23.cloned.1.call-update) | async-done | bytes 2359312 | tf_op jit(solution)/shard_map/reduce_scatter | solution.py:189
  648.2 98.8 %reduce-scatter.21.cloned.1.call-done = f32[1,192,3072]{2,1,0:T(8,128)} async-done(((f32[1,768,3072]{2,1,0:T(8,128)}), f32[1,192,3072]{2,1,0:T(8,128)}) %reduce-scatter.21.cloned.1.call-update) | async-done | bytes 2359312 | tf_op jit(solution)/shard_map/reduce_scatter | solution.py:188
  (282 shorter events, 123.4 us)
Async XLA Ops:
  7.2 52.8 %copy-start.2 = (bf16[197,768]{1,0:T(8,128)(2,1)S(1)}, bf16[197,768]{1,0:T(8,128)(2,1)}, u32[]{:S(2)}) copy-start(bf16[197,768]{1,0:T(8,128)(2,1)} %param.18) | copy-start | bytes 907780
  7.2 52.8 %all-gather.5.cloned.1.call-start = ((), (), s32[]{:S(2)}) async-start(), calls=%async_computation.12 | async-start | bytes 4423680 | tf_op jit(solution)/shard_map/all_gather | solution.py:89
  7.9 81.6 %all-gather.7.cloned.1.call-start = ((), (), s32[]{:S(2)}) async-start(), calls=%async_computation.13 | async-start | bytes 1474560 | tf_op jit(solution)/shard_map/all_gather | solution.py:90
  11.7 51.3 %copy-start.42 = (f32[197]{0:T(256)}, f32[197]{0:T(256)S(1)}, u32[]{:S(2)}) copy-start(f32[197]{0:T(256)S(1)} %broadcast_multiply_fusion.5) | copy-start | bytes 2368
  12.9 50.1 %copy-start.46 = (f32[197]{0:T(256)}, f32[197]{0:T(256)S(1)}, u32[]{:S(2)}) copy-start(f32[197]{0:T(256)S(1)} %add_rsqrt_fusion.1) | copy-start | bytes 2368
  29.9 33.1 %copy-start.28 = (f32[768]{0:T(1024)}, f32[768]{0:T(1024)S(1)}, u32[]{:S(2)}) copy-start(f32[768]{0:T(1024)S(1)} %get-tuple-element.32) | copy-start | bytes 9220
  29.9 33.1 %copy-start.30 = (f32[768]{0:T(1024)}, f32[768]{0:T(1024)S(1)}, u32[]{:S(2)}) copy-start(f32[768]{0:T(1024)S(1)} %get-tuple-element.31) | copy-start | bytes 9220
  29.9 61.9 %copy-start.36 = (f32[768]{0:T(1024)}, f32[768]{0:T(1024)S(1)}, u32[]{:S(2)}) copy-start(f32[768]{0:T(1024)S(1)} %get-tuple-element.26) | copy-start | bytes 9220
  98.9 23.5 %all-to-all-start = ((bf16[8,49,768]{2,1,0:T(8,128)(2,1)}), bf16[8,49,768]{2,1,0:T(8,128)(2,1)S(1)}, u32[]{:S(2)}, u32[]{:S(2)}) async-start(bf16[8,49,768]{2,1,0:T(8,128)(2,1)} %broadcast_select_fusion.1), calls=%async_computation | async-start | bytes 1376256 | tf_op jit(solution)/shard_map/all_to_all | solution.py:133
  136.8 23.1 %all-to-all-start.1 = ((bf16[8,49,768]{2,1,0:T(8,128)(2,1)}), bf16[8,49,768]{2,1,0:T(8,128)(2,1)}, u32[]{:S(2)}, u32[]{:S(2)}) async-start(bf16[8,49,768]{2,1,0:T(8,128)(2,1)} %fusion.44), calls=%async_computation.1 | async-start | bytes 1376256 | tf_op jit(solution)/shard_map/all_to_all | solution.py:151
  206.9 23.2 %all-to-all-start.3 = ((bf16[8,49,768]{2,1,0:T(8,128)(2,1)}), bf16[8,49,768]{2,1,0:T(8,128)(2,1)}, u32[]{:S(2)}, u32[]{:S(2)}) async-start(bf16[8,49,768]{2,1,0:T(8,128)(2,1)} %fusion.36), calls=%async_computation.3 | async-start | bytes 1376256 | tf_op jit(solution)/shard_map/all_to_all | solution.py:186
  211.2 73.3 %reduce-scatter.19.cloned.1.call-start = ((), (), s32[]{:S(2)}) async-start(), calls=%async_computation.15 | async-start | bytes 2949120 | tf_op jit(solution)/shard_map/reduce_scatter | solution.py:254
  213.3 31.4 %copy-start.40 = (bf16[197,8]{0,1:T(8,128)(2,1)}, bf16[197,8]{0,1:T(8,128)(2,1)S(1)}, u32[]{:S(2)}) copy-start(bf16[197,8]{0,1:T(8,128)(2,1)S(1)} %fusion.79) | copy-start | bytes 9460
  249.1 115.2 %reduce-scatter.17.cloned.1.call-start = ((), (), s32[]{:S(2)}) async-start(), calls=%async_computation.14 | async-start | bytes 8847360 | tf_op jit(solution)/shard_map/reduce_scatter | solution.py:253
  272.1 119.3 %reduce-scatter.27.cloned.1.call-start = ((), (), s32[]{:S(2)}) async-start(), calls=%async_computation.19 | async-start | bytes 491520
  273.8 144.6 %reduce-scatter.31.cloned.1.call-start = ((), (), s32[]{:S(2)}) async-start(), calls=%async_computation.21 | async-start | bytes 491520
  275.0 178.0 %reduce-scatter.29.cloned.1.call-start = ((), (), s32[]{:S(2)}) async-start(), calls=%async_computation.20 | async-start | bytes 1966080
  276.7 204.1 %reduce-scatter.25.cloned.1.call-start = ((), (), s32[]{:S(2)}) async-start(), calls=%async_computation.18 | async-start | bytes 491520
  280.3 84.0 %copy-start.60 = (f32[1,3072]{1,0:T(1,128)S(1)}, f32[1,3072]{1,0:T(1,128)}, u32[]{:S(2)}) copy-start(f32[1,3072]{1,0:T(1,128)} %copy-done.58) | copy-start | bytes 36868
  281.5 268.9 %all-reduce.4.cloned.1.call-start = ((), (), s32[]{:S(2)}) async-start(), calls=%async_computation.22 | async-start | bytes 4718592 | tf_op jit(solution)/shard_map/psum | solution.py:258
  364.3 283.9 %reduce-scatter.23.cloned.1.call-start = ((), (), s32[]{:S(2)}) async-start(), calls=%async_computation.17 | async-start | bytes 11796480 | tf_op jit(solution)/shard_map/reduce_scatter | solution.py:189
  371.3 375.7 %reduce-scatter.21.cloned.1.call-start = ((), (), s32[]{:S(2)}) async-start(), calls=%async_computation.16 | async-start | bytes 11796480 | tf_op jit(solution)/shard_map/reduce_scatter | solution.py:188
  379.3 75.4 %copy-start.6 = (f32[197,768]{1,0:T(8,128)S(1)}, f32[197,768]{1,0:T(8,128)}, u32[]{:S(2)}) copy-start(f32[197,768]{1,0:T(8,128)} %copy-done.4) | copy-start | bytes 1815556
  550.5 199.3 %copy-start.21 = (f32[192,768]{1,0:T(8,128)S(1)}, f32[192,768]{1,0:T(8,128)}, u32[]{:S(2)}) copy-start(f32[192,768]{1,0:T(8,128)} %get-tuple-element.80) | copy-start | bytes 1769476
  (61 other events, 476.0 us)
Sparse Core Ops, SparseCore 0:
  9.9 50.0 all-gather.4
  61.8 27.7 all-gather.6
  249.2 35.2 reduce-scatter.18
  287.5 76.7 reduce-scatter.16
  366.9 24.3 reduce-scatter.26
  394.0 24.4 reduce-scatter.30
  422.0 30.9 reduce-scatter.28
  456.3 24.3 reduce-scatter.24
  483.2 67.2 all-reduce.3
  554.0 94.1 reduce-scatter.22
  651.9 95.0 reduce-scatter.20
where the time goes:
time: 766 us; the launch traced here: 758 us
  waiting for transfers between devices  506 us (66%)
  matrix products  72.9 us (10%)
  blocking collectives  69.2 us (9%)
  local copies, waits for them, and re-layouts  57.3 us (7%)
  other arithmetic  22.9 us (3%)
  between operations  15.2 us (2%)
  starting transfers between devices  14.1 us (2%)
    reduce_scatter x1, waiting for transfers between devices, per_device(): lax.psum_scatter(d_w_in, 'dp', scatter_dimension=1, tiled=True)  98.8 us
    reduce_scatter x1, waiting for transfers between devices, per_device(): lax.psum_scatter(d_w_out, 'dp', scatter_dimension=1, tiled=True)  97.7 us
    unnamed x15, waiting for transfers between devices  97.7 us
    reduce_scatter x1, waiting for transfers between devices, per_device(): lax.psum_scatter(d_w_qkv, 'dp', scatter_dimension=0, tiled=True)  79.7 us
    psum x1, waiting for transfers between devices, per_device(): lax.psum((part_qkv, part_proj, part_router, part_vectors), 'expert')  38.6 us
    all_gather x1, waiting for transfers between devices, per_device(): lax.all_gather(w_qkv, 'dp', axis=0, tiled=True)  30.1 us
    psum x1, blocking collectives, per_device(): lax.psum((part_qkv, part_proj, part_router, part_vectors), 'expert')  29.6 us
    all_to_all x1, blocking collectives, per_device(): lax.all_to_all(d_sent, 'expert', split_axis=0, concat_axis=0, tiled=True)  21.5 us
  transfers between devices with their start and end apart: 14, of which 14 were waited for; matrix products, arithmetic and copies ran while one was open for 10% of the time, Pallas kernels for 0%

commit v1 on v0

v1 whole, which is shorter than its diff:
```python
import math

import jax
import jax.numpy as jnp
from jax import lax
from jax.experimental import pallas as pl
from jax.experimental.pallas import tpu as pltpu
from jax.sharding import PartitionSpec as P

HEAD_DIM = 64
SEQ = 197


NORM_EPS = 1e-06
SQRT_HALF = 0.7071067811865476
INV_ROOT_TWO_PI = 0.3989422804014327


def normalize(values):
    center = values - jnp.mean(values, axis=-1, keepdims=True)
    inv_std = lax.rsqrt(jnp.mean(center * center, axis=-1, keepdims=True) + NORM_EPS)
    return (center * inv_std, inv_std)


def norm_back(grad_in, normed, inv_std, gain_vec):
    scaled = grad_in * gain_vec
    mean_plain = jnp.mean(scaled, axis=-1, keepdims=True)
    mean_mixed = jnp.mean(scaled * normed, axis=-1, keepdims=True)
    return inv_std * (scaled - mean_plain - normed * mean_mixed)


def gelu_value(pre_act):
    return 0.5 * pre_act * (1.0 + lax.erf(pre_act * SQRT_HALF))


def gelu_slope(pre_act):
    return 0.5 * (1.0 + lax.erf(pre_act * SQRT_HALF)) + pre_act * INV_ROOT_TWO_PI * jnp.exp(
        -0.5 * pre_act * pre_act
    )


def by_heads(values, images):
    return values.reshape(images, SEQ, values.shape[1] // HEAD_DIM, HEAD_DIM)


def swap(values, axis, mask):
    size = lax.axis_size(axis)
    return lax.ppermute(values, axis, [(index, index ^ mask) for index in range(size)])


def place_rows(pieces, starts, rows_out):
    count = len(pieces)

    def body(starts_ref, *refs):
        sems = refs[-1]
        out_ref = refs[count]
        copies = []
        for index in range(count):
            rows = refs[index].shape[0]
            offset = pl.multiple_of(starts_ref[index], 16)
            copies.append(
                pltpu.make_async_copy(
                    refs[index], out_ref.at[pl.ds(offset, rows)], sems.at[index]
                )
            )
        for copy in copies:
            copy.start()
        for copy in copies:
            copy.wait()

    return pl.pallas_call(
        body,
        out_shape=jax.ShapeDtypeStruct((rows_out,) + pieces[0].shape[1:], pieces[0].dtype),
        in_specs=[pl.BlockSpec(memory_space=pltpu.SMEM)]
        + [pl.BlockSpec(memory_space=pl.ANY)] * count,
        out_specs=pl.BlockSpec(memory_space=pl.ANY),
        scratch_shapes=[pltpu.SemaphoreType.DMA((count,))],
        cost_estimate=pl.CostEstimate(
            flops=0,
            bytes_accessed=2 * rows_out * pieces[0].shape[1] * pieces[0].dtype.itemsize,
            transcendentals=0,
        ),
    )(starts, *pieces)


def gather_shared(shard):
    groups = lax.axis_size("dp")
    rows = shard.shape[0]
    if groups != 4:
        return lax.all_gather(shard, "dp", axis=0, tiled=True)
    me = lax.axis_index("dp")
    core = lax.axis_index("expert") % 2
    half = rows // 2
    part = half // 2
    mine = lax.dynamic_slice_in_dim(shard, core * half, half, 0)
    from_one = swap(mine, "dp", 1)
    from_two = swap(mine, "dp", 2)
    far_low = swap(from_one[:part], "dp", 2)
    far_high = swap(from_two[part:], "dp", 1)
    other_one = swap(from_one, "expert", 1)
    other_two = swap(from_two, "expert", 1)
    other_low = swap(far_low, "expert", 1)
    other_high = swap(far_high, "expert", 1)
    base_mine = core * half
    base_other = (1 - core) * half
    one, two, far = (me ^ 1) * rows, (me ^ 2) * rows, (me ^ 3) * rows
    starts = [
        me * rows,
        one + base_mine,
        two + base_mine,
        far + base_mine,
        far + base_mine + part,
        one + base_other,
        two + base_other,
        far + base_other,
        far + base_other + part,
    ]
    pieces = [
        shard,
        from_one,
        from_two,
        far_low,
        far_high,
        other_one,
        other_two,
        other_low,
        other_high,
    ]
    return place_rows(pieces, jnp.stack(starts).astype(jnp.int32), groups * rows)


def gather_rows(rows):
    groups = lax.axis_size("dp")
    if groups != 4:
        return [rows] + [swap(rows, "dp", mask) for mask in range(1, groups)]
    half = rows.shape[0] // 2
    from_one = swap(rows, "dp", 1)
    from_two = swap(rows, "dp", 2)
    return [
        rows,
        from_one,
        from_two,
        swap(from_one[:half], "dp", 2),
        swap(from_two[half:], "dp", 1),
    ]


def exchange(blocks):
    return [blocks[0]] + [swap(blocks[mask], "expert", mask) for mask in range(1, len(blocks))]


def in_order(pieces, me, axis):
    stack = jnp.stack(pieces)
    return jnp.concatenate(
        [
            lax.dynamic_index_in_dim(stack, me ^ index, 0, keepdims=False)
            for index in range(len(pieces))
        ],
        axis=axis,
    )


def reduce_all(partial):
    groups = lax.axis_size("dp")
    layers = lax.axis_size("expert") // 2
    me = lax.axis_index("dp")
    slot = lax.axis_index("expert")
    core, layer = slot % 2, slot // 2
    rows, columns = partial.shape
    half = columns // 2
    keep = lax.dynamic_slice_in_dim(partial, core * half, half, 1)
    give = lax.dynamic_slice_in_dim(partial, (1 - core) * half, half, 1).astype(jnp.bfloat16)
    keep = keep + swap(give, "expert", 1).astype(jnp.float32)
    share = rows // groups
    low = keep.astype(jnp.bfloat16)
    total = lax.dynamic_slice_in_dim(keep, me * share, share, 0)
    for mask in range(1, groups):
        piece = lax.dynamic_slice_in_dim(low, (me ^ mask) * share, share, 0)
        total = total + swap(piece, "dp", mask).astype(jnp.float32)
    part = share // layers
    low = total.astype(jnp.bfloat16)
    done = lax.dynamic_slice_in_dim(total, layer * part, part, 0)
    for mask in range(1, layers):
        piece = lax.dynamic_slice_in_dim(low, (layer ^ mask) * part, part, 0)
        done = done + swap(piece, "expert", 2 * mask).astype(jnp.float32)
    done = done.astype(jnp.bfloat16)
    pieces = [done] + [swap(done, "expert", 2 * mask) for mask in range(1, layers)]
    column = in_order(pieces, layer, 0)
    other = swap(column, "expert", 1)
    return in_order([column, other], core, 1).astype(jnp.float32)


def per_device(
    block_input,
    w_qkv,
    b_q,
    b_v,
    w_proj,
    b_proj,
    ln1_gain,
    ln1_bias,
    ln2_gain,
    ln2_bias,
    w_router,
    w_in,
    b_in,
    w_out,
    b_out,
    routes,
    slot_index,
    d_out,
):
    tokens = block_input.shape[0]
    width = block_input.shape[1]
    images = tokens // SEQ
    hidden_units = w_in.shape[2]
    experts = w_in.shape[0] * lax.axis_size("expert")
    groups = lax.axis_size("dp")
    capacity = 2 * tokens // experts
    slots = -(-(capacity + 1) // 8) * 8
    score_scale = 1.0 / math.sqrt(HEAD_DIM)
    dp_me = lax.axis_index("dp")
    expert_me = lax.axis_index("expert")
    vectors = jnp.stack([b_q, b_v, b_proj, ln1_gain, ln1_bias, ln2_gain, ln2_bias], axis=1)
    side = 128
    side_cols = jnp.concatenate([vectors, w_router], axis=1)
    side_cols = jnp.pad(side_cols, ((0, 0), (0, side - side_cols.shape[1])))
    full_qkv = gather_shared(jnp.concatenate([w_qkv, side_cols], axis=1))
    full_proj = gather_shared(w_proj)
    kept = slot_index < capacity
    target = jnp.where(kept, (routes ^ expert_me) * slots + slot_index, -1)
    slot_ids = lax.broadcasted_iota(jnp.int32, (1, experts * slots), 1)
    hot_first = target[:, :1] == slot_ids
    hot_second = target[:, 1:] == slot_ids
    hot_low = (hot_first | hot_second).astype(jnp.bfloat16)

    def to_slots(values):
        return jnp.einsum(
            "ts,td->sd", hot_low, values, preferred_element_type=jnp.float32
        ).astype(jnp.bfloat16)

    def split(values):
        return list(values.reshape(experts, slots, width))

    grad_slots = jnp.concatenate(exchange(split(to_slots(d_out))), axis=0)
    grad_all = gather_rows(grad_slots)

    side_full = full_qkv[:, 3 * width :]
    wide_vectors = side_full[:, :7].astype(jnp.float32).T
    bias_q, bias_v, bias_proj, gain_one, bias_one, gain_two, bias_two = (
        wide_vectors[index] for index in range(7)
    )
    full_router = side_full[:, 7 : 7 + experts]
    resid = block_input.astype(jnp.float32)
    normed_one, inv_one = normalize(resid)
    a_in = (normed_one * gain_one + bias_one).astype(jnp.bfloat16)
    qkv = jnp.dot(a_in, full_qkv, preferred_element_type=jnp.float32)
    queries = (qkv[:, :width] + bias_q).astype(jnp.bfloat16)
    key_vecs = qkv[:, width : 2 * width].astype(jnp.bfloat16)
    values = (qkv[:, 2 * width : 3 * width] + bias_v).astype(jnp.bfloat16)
    query_heads = by_heads(queries, images)
    key_heads = by_heads(key_vecs, images)
    value_heads = by_heads(values, images)
    scores = (
        jnp.einsum("bqhd,bkhd->bhqk", query_heads, key_heads, preferred_element_type=jnp.float32)
        * score_scale
    )
    row_max = jnp.max(scores, axis=-1, keepdims=True)
    exp_scores = jnp.exp(scores - row_max)
    row_total = jnp.sum(exp_scores, axis=-1, keepdims=True)
    log_total = row_max + jnp.log(row_total)
    probs_low = (exp_scores / row_total).astype(jnp.bfloat16)
    context = (
        jnp.einsum("bhqk,bkhd->bqhd", probs_low, value_heads, preferred_element_type=jnp.float32)
        .reshape(tokens, width)
        .astype(jnp.bfloat16)
    )
    hidden = resid + jnp.dot(context, full_proj, preferred_element_type=jnp.float32) + bias_proj
    normed_two, inv_two = normalize(hidden)
    y_in = (normed_two * gain_two + bias_two).astype(jnp.bfloat16)
    logits = jnp.dot(y_in, full_router, preferred_element_type=jnp.float32)
    route_hot = (routes[:, :, None] == lax.broadcasted_iota(jnp.int32, (1, 1, experts), 2)).astype(
        jnp.float32
    )
    chosen = jnp.sum(logits[:, None, :] * route_hot, axis=-1)
    first_gate = jax.nn.sigmoid(chosen[:, 0] - chosen[:, 1])
    second_gate = 1.0 - first_gate

    slot_gates = jnp.sum(
        jnp.where(hot_first, first_gate[:, None], 0.0)
        + jnp.where(hot_second, second_gate[:, None], 0.0),
        axis=0,
    ).reshape(experts, 1, slots)
    terms = []
    rest = slot_gates
    for _ in range(3):
        term = lax.reduce_precision(rest, 8, 7)
        rest = rest - term
        terms.append(jnp.pad(term, ((0, 0), (0, 0), (0, 128 - slots))))
    gate_row = jnp.pad(
        jnp.concatenate(terms, axis=2), ((0, 0), (0, 0), (0, width - 3 * 128))
    ).astype(jnp.bfloat16)
    row_ids = lax.broadcasted_iota(jnp.int32, (1, slots, 1), 1)
    sent = jnp.where(
        row_ids == capacity, gate_row, to_slots(y_in).reshape(experts, slots, width)
    )
    recv_rows = jnp.concatenate(exchange(list(sent)), axis=0)
    recv_all = gather_rows(recv_rows)

    def gated(rows, grads):
        blocks = rows.shape[0] // slots
        line = rows.reshape(blocks, slots, width)[:, capacity, : 3 * 128].astype(jnp.float32)
        line = line[:, :128] + line[:, 128:256] + line[:, 256:384]
        column = line[:, :slots].reshape(blocks, slots, 1)
        wide = grads.reshape(blocks, slots, width).astype(jnp.float32)
        return (column * wide).astype(jnp.bfloat16).reshape(blocks * slots, width)

    weight_in, weight_out = w_in[0], w_out[0]
    bias_in = b_in[0].astype(jnp.float32)
    bias_out = b_out[0].astype(jnp.float32)
    d_sent = gated(recv_rows, grad_slots)
    pre_act = jnp.dot(recv_rows, weight_in, preferred_element_type=jnp.float32) + bias_in
    activated = gelu_value(pre_act).astype(jnp.bfloat16)
    expert_out = (
        jnp.dot(activated, weight_out, preferred_element_type=jnp.float32) + bias_out
    ).astype(jnp.bfloat16)
    d_pre = jnp.einsum(
        "cd,fd->cf", d_sent, weight_out, preferred_element_type=jnp.float32
    ) * gelu_slope(pre_act)
    d_expert_in = jnp.einsum(
        "cf,df->cd", d_pre.astype(jnp.bfloat16), weight_in, preferred_element_type=jnp.float32
    ).astype(jnp.bfloat16)
    returned = jnp.concatenate(exchange(split(expert_out)), axis=0)
    d_returned = jnp.concatenate(exchange(split(d_expert_in)), axis=0)

    units = hidden_units // groups
    share = width // groups
    rows_all = jnp.concatenate(recv_all, axis=0)
    sent_all = gated(rows_all, jnp.concatenate(grad_all, axis=0))
    my_in = lax.dynamic_slice_in_dim(weight_in, dp_me * units, units, 1)
    my_out = lax.dynamic_slice_in_dim(weight_out, dp_me * units, units, 0)
    my_bias = lax.dynamic_slice_in_dim(bias_in, dp_me * units, units, 0)
    pre_all = jnp.dot(rows_all, my_in, preferred_element_type=jnp.float32) + my_bias
    act_all = gelu_value(pre_all).astype(jnp.bfloat16)
    part_w_out = jnp.einsum("cf,cd->fd", act_all, sent_all, preferred_element_type=jnp.float32)
    d_pre_all = jnp.einsum(
        "cd,fd->cf", sent_all, my_out, preferred_element_type=jnp.float32
    ) * gelu_slope(pre_all)
    part_b_in = jnp.sum(d_pre_all, axis=0)
    d_pre_low = d_pre_all.astype(jnp.bfloat16)
    d_w_in = jnp.einsum("cd,cf->df", rows_all, d_pre_low, preferred_element_type=jnp.float32)
    sum_sent = jnp.sum(sent_all.astype(jnp.float32), axis=0)
    part_b_out = lax.dynamic_slice_in_dim(sum_sent, dp_me * share, share, 0)
    pieces = [lax.dynamic_slice_in_dim(d_w_in, dp_me * share, share, 0)]
    for mask in range(1, groups):
        piece = lax.dynamic_slice_in_dim(d_w_in, (dp_me ^ mask) * share, share, 0)
        pieces.append(swap(piece.astype(jnp.bfloat16), "dp", mask).astype(jnp.float32))
    part_w_in = in_order(pieces, dp_me, 1)

    def from_slots(hot, values):
        return jnp.dot(hot.astype(jnp.bfloat16), values, preferred_element_type=jnp.float32)

    picked_first = from_slots(hot_first, returned)
    picked_second = from_slots(hot_second, returned)
    block_out = (
        hidden + (first_gate[:, None] * picked_first + second_gate[:, None] * picked_second)
    ).astype(jnp.bfloat16)
    grad_out = d_out.astype(jnp.float32)
    d_gate_diff = jnp.sum(grad_out * picked_first, axis=-1) - jnp.sum(
        grad_out * picked_second, axis=-1
    )
    d_diff = d_gate_diff * first_gate * second_gate
    d_logits = (d_diff[:, None] * (route_hot[:, 0] - route_hot[:, 1])).astype(jnp.bfloat16)
    d_w_router = jnp.einsum("td,te->de", y_in, d_logits, preferred_element_type=jnp.float32)
    d_y = from_slots(hot_low, d_returned) + jnp.einsum(
        "te,de->td", d_logits, full_router, preferred_element_type=jnp.float32
    )
    d_gain_two = jnp.sum(d_y * normed_two, axis=0)
    d_bias_two = jnp.sum(d_y, axis=0)
    d_hidden = grad_out + norm_back(d_y, normed_two, inv_two, gain_two)
    d_b_proj = jnp.sum(d_hidden, axis=0)
    d_hidden_low = d_hidden.astype(jnp.bfloat16)
    d_w_proj = jnp.einsum("td,te->de", context, d_hidden_low, preferred_element_type=jnp.float32)
    d_context = jnp.einsum(
        "te,de->td", d_hidden_low, full_proj, preferred_element_type=jnp.float32
    ).astype(jnp.bfloat16)
    early_side = jnp.concatenate(
        [jnp.stack([d_b_proj, d_gain_two, d_bias_two], axis=1), d_w_router], axis=1
    )
    early_side = jnp.pad(early_side, ((0, 0), (0, 256 - early_side.shape[1])))
    early = reduce_all(jnp.concatenate([d_w_proj, early_side], axis=1))
    grad_heads = by_heads(d_context, images)
    probs = jnp.exp(
        jnp.einsum("bqhd,bkhd->bhqk", query_heads, key_heads, preferred_element_type=jnp.float32)
        * score_scale
        - log_total
    )
    d_probs = jnp.einsum(
        "bqhd,bkhd->bhqk", grad_heads, value_heads, preferred_element_type=jnp.float32
    )
    d_values = jnp.einsum(
        "bhqk,bqhd->bkhd",
        probs.astype(jnp.bfloat16),
        grad_heads,
        preferred_element_type=jnp.float32,
    ).reshape(tokens, width)
    row_delta = jnp.sum(probs * d_probs, axis=-1, keepdims=True)
    d_scores = (probs * (d_probs - row_delta) * score_scale).astype(jnp.bfloat16)
    d_queries = jnp.einsum(
        "bhqk,bkhd->bqhd", d_scores, key_heads, preferred_element_type=jnp.float32
    ).reshape(tokens, width)
    d_keys = jnp.einsum(
        "bhqk,bqhd->bkhd", d_scores, query_heads, preferred_element_type=jnp.float32
    ).reshape(tokens, width)
    d_b_q = jnp.sum(d_queries, axis=0)
    d_b_v = jnp.sum(d_values, axis=0)
    d_qkv = jnp.concatenate(
        [d_queries, d_keys, d_values, jnp.zeros((tokens, side), jnp.float32)], axis=1
    ).astype(jnp.bfloat16)
    d_w_qkv = jnp.einsum(
        "td,te->de", a_in, d_qkv[:, : 3 * width], preferred_element_type=jnp.float32
    )
    d_a = jnp.einsum("te,de->td", d_qkv, full_qkv, preferred_element_type=jnp.float32)
    d_gain_one = jnp.sum(d_a * normed_one, axis=0)
    d_bias_one = jnp.sum(d_a, axis=0)
    d_input = d_hidden + norm_back(d_a, normed_one, inv_one, gain_one)
    late_side = jnp.stack([d_b_q, d_b_v, d_gain_one, d_bias_one], axis=1)
    late_side = jnp.pad(late_side, ((0, 0), (0, 256 - late_side.shape[1])))
    late = reduce_all(jnp.concatenate([d_w_qkv, late_side], axis=1))
    return (
        block_out,
        d_input,
        late[:, : 3 * width],
        late[:, 3 * width],
        late[:, 3 * width + 1],
        early[:, :width],
        early[:, width],
        late[:, 3 * width + 2],
        late[:, 3 * width + 3],
        early[:, width + 1],
        early[:, width + 2],
        early[:, width + 3 : width + 3 + experts],
        part_w_in[None],
        part_b_in[None],
        part_w_out[None],
        part_b_out[None],
    )


def solution(mesh):
    return jax.shard_map(
        per_device,
        mesh=mesh,
        in_specs=(
            P(("dp", "expert"), None),
            P("dp", None),
            P("dp"),
            P("dp"),
            P("dp", None),
            P("dp"),
            P("dp"),
            P("dp"),
            P("dp"),
            P("dp"),
            P("dp", None),
            P("expert", None, None),
            P("expert", None),
            P("expert", None, None),
            P("expert", None),
            P(("dp", "expert"), None),
            P(("dp", "expert"), None),
            P(("dp", "expert"), None),
        ),
        out_specs=(
            P(("dp", "expert"), None),
            P(("dp", "expert"), None),
            P("dp", None),
            P("dp"),
            P("dp"),
            P("dp", None),
            P("dp"),
            P("dp"),
            P("dp"),
            P("dp"),
            P("dp"),
            P("dp", None),
            P("expert", "dp", None),
            P("expert", "dp"),
            P("expert", "dp", None),
            P("expert", "dp"),
        ),
        check_vma=False,
    )
```

time: 766 us -> 556 us (0.73)
  waiting for transfers between devices: 506 us -> 157 us
  Pallas kernels: 0 us -> 153 us
  blocking collectives: 69.2 us -> 0 us
  starting transfers between devices: 14.1 us -> 75 us
  between operations: 15.2 us -> 2.7 us
    reduce_scatter x4 -> x0, waiting for transfers between devices: 279 us -> none  [the longest x1 98.8 us: per_device(): lax.psum_scatter(d_w_in, 'dp', scatter_dimension=1, tiled=True)]
    ppermute x0 -> x77, waiting for transfers between devices: none -> 157 us  [swap(): lax.ppermute(values, axis, [(index, index ^ mask) for index in range(size)])]
    pallas_call x0 -> x2, Pallas kernels: none -> 153 us  [place_rows(): pl.pallas_call(body, out_shape=jax.ShapeDtypeStruct((rows_out,) + pieces[...]
    unnamed x15 -> x0, waiting for transfers between devices: 97.7 us -> none
    ppermute x0 -> x77, starting transfers between devices: none -> 75 us  [swap(): lax.ppermute(values, axis, [(index, index ^ mask) for index in range(size)])]
    all_gather x2 -> x0, waiting for transfers between devices: 50.3 us -> none  [the longest x1 30.1 us: per_device(): lax.all_gather(w_qkv, 'dp', axis=0, tiled=True)]
    all_to_all x3 -> x0, waiting for transfers between devices: 40.3 us -> none  [the longest x1 18.8 us: per_device(): lax.all_to_all(sent_slots, 'expert', split_axis=0, concat_axis=0, tiled=T...]
    psum x1 -> x0, waiting for transfers between devices: 38.6 us -> none  [per_device(): lax.psum((part_qkv, part_proj, part_router, part_vectors), 'expert')]
  transfers between devices with their start and end apart: 14 -> 77, of which waited for: 14 -> 37; matrix products, arithmetic and copies ran while one was open for 10% -> 27% of each run, Pallas kernels for 0% -> 28%
where the time goes in v1:
time: 556 us; the launch traced here: 546 us
  waiting for transfers between devices  157 us (28%)
  Pallas kernels  153 us (28%)
  matrix products  78.6 us (14%)
  starting transfers between devices  75 us (13%)
  local copies, waits for them, and re-layouts  50.9 us (9%)
  other arithmetic  30.1 us (5%)
    ppermute x77, waiting for transfers between devices, swap(): lax.ppermute(values, axis, [(index, index ^ mask) for index in range(size)])  157 us
    pallas_call x2, Pallas kernels, place_rows(): pl.pallas_call(body, out_shape=jax.ShapeDtypeStruct((rows_out,) + pieces[...  153 us
    ppermute x77, starting transfers between devices, swap(): lax.ppermute(values, axis, [(index, index ^ mask) for index in range(size)])  75 us
    unnamed x229, local copies, waits for them, and re-layouts  24.9 us
  transfers between devices with their start and end apart: 77, of which 37 were waited for; matrix products, arithmetic and copies ran while one was open for 27% of the time, Pallas kernels for 28%

profile of v1, /device:TPU:0, one launch (start us, length us, event | category | flops | bytes accessed | tf_op | source)
XLA Modules:
  0.0 546.3 jit_solution(18189890881914266456)
XLA Ops:
  33.9 6.2 %collective-permute-done.34 = bf16[56,768]{1,0:T(8,128)(2,1)S(1)} collective-permute-done((bf16[56,768]{1,0:T(8,128)(2,1)S(1)}, bf16[56,768]{1,0:T(8,128)(2,1)S(1)}, u32[]{:S(2)}, u32[]{:S(2)}) %collective-permute-start.34) | collective-permute-done | bytes 86048 | tf_op jit(solution)/shard_map/ppermute | solution.py:48
  56.9 15.0 %collective-permute-done.11.refs_4_ = bf16[48,768]{1,0:T(8,128)(2,1)S(1)} collective-permute-done((bf16[48,768]{1,0:T(8,128)(2,1)S(1)}, bf16[48,768]{1,0:T(8,128)(2,1)S(1)}, u32[]{:S(2)}, u32[]{:S(2)}) %collective-permute-start.11) | collective-permute-done | bytes 73760 | tf_op jit(solution)/shard_map/ppermute | solution.py:48
  81.5 37.6 %shard_map.298 = bf16[768,768]{1,0:T(8,128)(2,1)} custom-call(s32[9]{0:T(128)} %stack.166.starts_ref, bf16[192,768]{1,0:T(8,128)(2,1)} %refs_0_.1, bf16[96,768]{1,0:T(8,128)(2,1)} %copy-done.29, bf16[96,768]{1,0:T(8,128)(2,1)} %copy-done.30, bf16[48,768]{1,0:T(8,128)(2,1)} %copy-done.43, bf16[48,768]{1,0:T(8,128)(2,1)} %copy-done.44, ...), custom_call_target="tpu_custom_call" | custom-call | bytes 2359296 | tf_op jit(solution)/shard_map/pallas_call | solution.py:71
  126.2 115.0 %shard_map.297 = bf16[768,2432]{1,0:T(8,128)(2,1)} custom-call(s32[9]{0:T(128)} %stack.166.starts_ref, bf16[192,2432]{1,0:T(8,128)(2,1)} %copy-done.7, bf16[96,2432]{1,0:T(8,128)(2,1)} %copy-done.21, bf16[96,2432]{1,0:T(8,128)(2,1)} %copy-done.22, bf16[48,2432]{1,0:T(8,128)(2,1)} %collective-permute-done.2.refs_3_, ...), custom_call_target="tpu_custom_call" | custom-call | bytes 7471104 | tf_op jit(solution)/shard_map/pallas_call | solution.py:71
  278.2 5.2 fusion.16
  290.1 6.5 %fusion.5 = bf16[448,3072]{1,0:T(8,128)(2,1)S(1)} fusion(f32[448,3072]{1,0:T(8,128)} %copy-done.8, bf16[1,3072,768]{2,1,0:T(8,128)(2,1)} %param.31, f32[3072]{0:T(1024)} %bitcast.240, bf16[448,768]{1,0:T(8,128)(2,1)} %get-tuple-element.193, f32[448]{0:T(512)} %mul.360), kind=kOutput, calls=%fused_computation.9 | convolution fusion | flops 2130100224 | bytes 13678336 | tf_op jit(solution)/shard_map/cd,fd->cf/dot_general | solution.py:327
  296.6 4.8 fusion.45
  314.6 4.8 collective-permute-done.26
  319.5 6.2 %collective-permute-done.27 = bf16[56,768]{1,0:T(8,128)(2,1)S(1)} collective-permute-done((bf16[56,768]{1,0:T(8,128)(2,1)S(1)}, bf16[56,768]{1,0:T(8,128)(2,1)S(1)}, u32[]{:S(2)}, u32[]{:S(2)}) %collective-permute-start.27) | collective-permute-done | bytes 86048 | tf_op jit(solution)/shard_map/ppermute | solution.py:48
  327.6 4.4 collective-permute-done.28
  332.0 5.7 %collective-permute-done.29 = bf16[56,768]{1,0:T(8,128)(2,1)S(1)} collective-permute-done((bf16[56,768]{1,0:T(8,128)(2,1)S(1)}, bf16[56,768]{1,0:T(8,128)(2,1)S(1)}, u32[]{:S(2)}, u32[]{:S(2)}) %collective-permute-start.29) | collective-permute-done | bytes 86048 | tf_op jit(solution)/shard_map/ppermute | solution.py:48
  339.4 4.9 collective-permute-done.38
  344.3 4.7 collective-permute-done.39
  349.6 6.3 %collective-permute-done.40 = bf16[56,768]{1,0:T(8,128)(2,1)S(1)} collective-permute-done((bf16[56,768]{1,0:T(8,128)(2,1)S(1)}, bf16[56,768]{1,0:T(8,128)(2,1)S(1)}, u32[]{:S(2)}, u32[]{:S(2)}) %collective-permute-start.40) | collective-permute-done | bytes 86048 | tf_op jit(solution)/shard_map/ppermute | solution.py:48
  355.9 6.5 %collective-permute-done.41 = bf16[56,768]{1,0:T(8,128)(2,1)S(1)} collective-permute-done((bf16[56,768]{1,0:T(8,128)(2,1)S(1)}, bf16[56,768]{1,0:T(8,128)(2,1)S(1)}, u32[]{:S(2)}, u32[]{:S(2)}) %collective-permute-start.41) | collective-permute-done | bytes 86048 | tf_op jit(solution)/shard_map/ppermute | solution.py:48
  364.2 4.5 collective-permute-done.42
  369.5 5.3 collective-permute-done.43
  385.6 4.5 fusion.52
  390.1 4.6 fusion.163
  431.8 7.0 %fusion.71 = f32[1792,768]{1,0:T(8,128)} fusion(bf16[1792,768]{1,0:T(8,128)(2,1)S(1)} %constant_dynamic-update-slice_fusion.32, bf16[1,768,3072]{2,1,0:T(8,128)(2,1)} %param.29, s32[]{:T(128)S(6)} %select_n.157), kind=kOutput, calls=%fused_computation.89 | convolution fusion | flops 2113929216 | bytes 9437188 | tf_op jit(solution)/shard_map/dot_general | solution.py:343
  439.0 7.4 %fusion.172 = (f32[768]{0:T(1024)S(1)}, bf16[1792,768]{1,0:T(8,128)(2,1)S(1)}) fusion(f32[1792,768]{1,0:T(8,128)} %fusion.71, f32[768]{0:T(1024)S(1)} %copy-done.89, bf16[1,3072,768]{2,1,0:T(8,128)(2,1)} %param.31, s32[]{:T(128)S(6)} %select_n.157, bf16[1792,768]{1,0:T(8,128)(2,1)} %constant_dynamic-update-slice_fusion.44, f32[1792]{0:T(1024)S(1)} %mul.401), kind=kOutput, calls=%fused_computation.373 | convolution fusion | flops 2134572288 | bytes 12203012 | tf_op jit(solution)/shard_map/cd,fd->cf/dot_general | solution.py:346
  446.4 6.1 %fusion.38 = f32[1,768,768]{2,1,0:T(8,128)} fusion(f32[1792,768]{1,0:T(8,128)S(1)} %copy-done.93, f32[768]{0:T(1024)S(1)} %copy-done.89, bf16[1792,768]{1,0:T(8,128)(2,1)} %constant_dynamic-update-slice_fusion.44, f32[1792]{0:T(1024)S(1)} %mul.401), kind=kOutput, calls=%fused_computation.55 | convolution fusion | flops 2126315520 | bytes 10627072 | tf_op jit(solution)/shard_map/cf,cd->fd/dot_general | solution.py:345
  491.8 11.4 %collective-permute-done.47 = bf16[192,1280]{1,0:T(8,128)(2,1)S(1)} collective-permute-done((bf16[192,1280]{1,0:T(8,128)(2,1)S(1)}, bf16[192,1280]{1,0:T(8,128)(2,1)S(1)}, u32[]{:S(2)}, u32[]{:S(2)}) %collective-permute-start.47) | collective-permute-done | bytes 491552 | tf_op jit(solution)/shard_map/ppermute | solution.py:48
  503.2 10.1 %collective-permute-done.46 = bf16[192,1280]{1,0:T(8,128)(2,1)S(1)} collective-permute-done((bf16[192,1280]{1,0:T(8,128)(2,1)S(1)}, bf16[192,1280]{1,0:T(8,128)(2,1)S(1)}, u32[]{:S(2)}, u32[]{:S(2)}) %collective-permute-start.46) | collective-permute-done | bytes 491552 | tf_op jit(solution)/shard_map/ppermute | solution.py:48
  (523 shorter events, 249.1 us)
Async XLA Ops:
  7.7 49.2 %collective-permute-start = (bf16[96,2432]{1,0:T(8,128)(2,1)S(1)}, bf16[96,2432]{1,0:T(8,128)(2,1)S(1)}, u32[]{:S(2)}, u32[]{:S(2)}) collective-permute-start(bf16[96,2432]{1,0:T(8,128)(2,1)S(1)} %constant_dynamic-slice_fusion.14), channel_id=1, source_target_pairs={{0,8},{8,0},{16,24},{24,16},{1,9},{9,1},{17,25},{25,17},{2,10},{10... | collective-permute-start | bytes 1400840 | tf_op jit(solution)/shard_map/ppermute | solution.py:48
  10.7 63.1 %collective-permute-start.1 = (bf16[96,2432]{1,0:T(8,128)(2,1)S(1)}, bf16[96,2432]{1,0:T(8,128)(2,1)S(1)}, u32[]{:S(2)}, u32[]{:S(2)}) collective-permute-start(bf16[96,2432]{1,0:T(8,128)(2,1)S(1)} %constant_dynamic-slice_fusion.14), channel_id=1, source_target_pairs={{0,16},{8,24},{16,0},{24,8},{1,17},{9,25},{17,1},{25,9},{2,18},{10... | collective-permute-start | bytes 1400840 | tf_op jit(solution)/shard_map/ppermute | solution.py:48
  12.2 35.5 %collective-permute-start.8 = (bf16[96,768]{1,0:T(8,128)(2,1)S(1)}, bf16[96,768]{1,0:T(8,128)(2,1)S(1)}, u32[]{:S(2)}, u32[]{:S(2)}) collective-permute-start(bf16[96,768]{1,0:T(8,128)(2,1)S(1)} %constant_dynamic-slice_fusion.13), channel_id=1, source_target_pairs={{0,8},{8,0},{16,24},{24,16},{1,9},{9,1},{17,25},{25,17},{2,10},{10... | collective-permute-start | bytes 442376 | tf_op jit(solution)/shard_map/ppermute | solution.py:48
  12.8 41.9 %collective-permute-start.9 = (bf16[96,768]{1,0:T(8,128)(2,1)S(1)}, bf16[96,768]{1,0:T(8,128)(2,1)S(1)}, u32[]{:S(2)}, u32[]{:S(2)}) collective-permute-start(bf16[96,768]{1,0:T(8,128)(2,1)S(1)} %constant_dynamic-slice_fusion.13), channel_id=1, source_target_pairs={{0,16},{8,24},{16,0},{24,8},{1,17},{9,25},{17,1},{25,9},{2,18},{10... | collective-permute-start | bytes 442376 | tf_op jit(solution)/shard_map/ppermute | solution.py:48
  53.2 66.5 %collective-permute-start.70 = (bf16[448,768]{1,0:T(8,128)(2,1)}, bf16[448,768]{1,0:T(8,128)(2,1)S(1)}, u32[]{:S(2)}, u32[]{:S(2)}) collective-permute-start(bf16[448,768]{1,0:T(8,128)(2,1)} %get-tuple-element.193), channel_id=1, source_target_pairs={{0,8},{8,0},{16,24},{24,16},{1,9},{9,1},{17,25},{25,17},{2,10},{10... | collective-permute-start | bytes 2064392 | tf_op jit(solution)/shard_map/ppermute | solution.py:48
  54.7 65.8 %collective-permute-start.71 = (bf16[448,768]{1,0:T(8,128)(2,1)}, bf16[448,768]{1,0:T(8,128)(2,1)S(1)}, u32[]{:S(2)}, u32[]{:S(2)}) collective-permute-start(bf16[448,768]{1,0:T(8,128)(2,1)} %get-tuple-element.193), channel_id=1, source_target_pairs={{0,16},{8,24},{16,0},{24,8},{1,17},{9,25},{17,1},{25,9},{2,18},{10... | collective-permute-start | bytes 2064392 | tf_op jit(solution)/shard_map/ppermute | solution.py:48
  56.3 15.7 %collective-permute-start.11 = (bf16[48,768]{1,0:T(8,128)(2,1)S(1)}, bf16[48,768]{1,0:T(8,128)(2,1)S(1)}, u32[]{:S(2)}, u32[]{:S(2)}) collective-permute-start(bf16[48,768]{1,0:T(8,128)(2,1)S(1)} %slice.225), channel_id=1, source_target_pairs={{0,8},{8,0},{16,24},{24,16},{1,9},{9,1},{17,25},{25,17},{2,10},{10... | collective-permute-start | bytes 221192 | tf_op jit(solution)/shard_map/ppermute | solution.py:48
  56.9 15.1 %collective-permute-start.12 = (bf16[96,768]{1,0:T(8,128)(2,1)S(1)}, bf16[96,768]{1,0:T(8,128)(2,1)S(1)}, u32[]{:S(2)}, u32[]{:S(2)}) collective-permute-start(bf16[96,768]{1,0:T(8,128)(2,1)S(1)} %collective-permute-done.8.refs_1_), channel_id=1, source_target_pairs={{0,1},{1,0},{2,3},{3,2},{4,5},{5,4},{6,7},{7,6},{8,9},{9,8},{10,11... | collective-permute-start | bytes 442376 | tf_op jit(solution)/shard_map/ppermute | solution.py:48
  76.4 42.8 %collective-permute-start.3 = (bf16[48,2432]{1,0:T(8,128)(2,1)}, bf16[48,2432]{1,0:T(8,128)(2,1)}, u32[]{:S(2)}, u32[]{:S(2)}) collective-permute-start(bf16[48,2432]{1,0:T(8,128)(2,1)} %slice.215), channel_id=1, source_target_pairs={{0,8},{8,0},{16,24},{24,16},{1,9},{9,1},{17,25},{25,17},{2,10},{10... | collective-permute-start | bytes 700424 | tf_op jit(solution)/shard_map/ppermute | solution.py:48
  80.3 43.6 %collective-permute-start.4 = (bf16[96,2432]{1,0:T(8,128)(2,1)S(1)}, bf16[96,2432]{1,0:T(8,128)(2,1)S(1)}, u32[]{:S(2)}, u32[]{:S(2)}) collective-permute-start(bf16[96,2432]{1,0:T(8,128)(2,1)S(1)} %collective-permute-done.refs_1_), channel_id=1, source_target_pairs={{0,1},{1,0},{2,3},{3,2},{4,5},{5,4},{6,7},{7,6},{8,9},{9,8},{10,11... | collective-permute-start | bytes 1400840 | tf_op jit(solution)/shard_map/ppermute | solution.py:48
  81.0 44.4 %collective-permute-start.5 = (bf16[96,2432]{1,0:T(8,128)(2,1)S(1)}, bf16[96,2432]{1,0:T(8,128)(2,1)S(1)}, u32[]{:S(2)}, u32[]{:S(2)}) collective-permute-start(bf16[96,2432]{1,0:T(8,128)(2,1)S(1)} %collective-permute-done.1.refs_2_), channel_id=1, source_target_pairs={{0,1},{1,0},{2,3},{3,2},{4,5},{5,4},{6,7},{7,6},{8,9},{9,8},{10,11... | collective-permute-start | bytes 1400840 | tf_op jit(solution)/shard_map/ppermute | solution.py:48
  120.6 292.0 %collective-permute-start.72 = (bf16[224,768]{1,0:T(8,128)(2,1)}, bf16[224,768]{1,0:T(8,128)(2,1)}, u32[]{:S(2)}, u32[]{:S(2)}) collective-permute-start(bf16[224,768]{1,0:T(8,128)(2,1)} %slice.251), channel_id=1, source_target_pairs={{0,16},{8,24},{16,0},{24,8},{1,17},{9,25},{17,1},{25,9},{2,18},{10... | collective-permute-start | bytes 1032200 | tf_op jit(solution)/shard_map/ppermute | solution.py:48
  123.9 292.4 %collective-permute-start.73 = (bf16[224,768]{1,0:T(8,128)(2,1)}, bf16[224,768]{1,0:T(8,128)(2,1)}, u32[]{:S(2)}, u32[]{:S(2)}) collective-permute-start(bf16[224,768]{1,0:T(8,128)(2,1)} %slice.252), channel_id=1, source_target_pairs={{0,8},{8,0},{16,24},{24,16},{1,9},{9,1},{17,25},{25,17},{2,10},{10... | collective-permute-start | bytes 1032200 | tf_op jit(solution)/shard_map/ppermute | solution.py:48
  276.3 141.7 %collective-permute-start.66 = (bf16[448,768]{1,0:T(8,128)(2,1)}, bf16[448,768]{1,0:T(8,128)(2,1)}, u32[]{:S(2)}, u32[]{:S(2)}) collective-permute-start(bf16[448,768]{1,0:T(8,128)(2,1)} %get-tuple-element.207), channel_id=1, source_target_pairs={{0,8},{8,0},{16,24},{24,16},{1,9},{9,1},{17,25},{25,17},{2,10},{10... | collective-permute-start | bytes 2064392 | tf_op jit(solution)/shard_map/ppermute | solution.py:48
  276.9 142.9 %collective-permute-start.67 = (bf16[448,768]{1,0:T(8,128)(2,1)}, bf16[448,768]{1,0:T(8,128)(2,1)}, u32[]{:S(2)}, u32[]{:S(2)}) collective-permute-start(bf16[448,768]{1,0:T(8,128)(2,1)} %get-tuple-element.207), channel_id=1, source_target_pairs={{0,16},{8,24},{16,0},{24,8},{1,17},{9,25},{17,1},{25,9},{2,18},{10... | collective-permute-start | bytes 2064392 | tf_op jit(solution)/shard_map/ppermute | solution.py:48
  405.3 19.3 %collective-permute-start.55 = (bf16[768,512]{0,1:T(8,128)(2,1)S(1)}, bf16[768,512]{0,1:T(8,128)(2,1)S(1)}, u32[]{:S(2)}, u32[]{:S(2)}) collective-permute-start(bf16[768,512]{0,1:T(8,128)(2,1)S(1)} %fusion.40), channel_id=1, source_target_pairs={{0,1},{1,0},{2,3},{3,2},{4,5},{5,4},{6,7},{7,6},{8,9},{9,8},{10,11... | collective-permute-start | bytes 2359304 | tf_op jit(solution)/shard_map/ppermute | solution.py:48
  412.6 72.3 %collective-permute-start.44 = (bf16[768,1280]{1,0:T(8,128)(2,1)}, bf16[768,1280]{1,0:T(8,128)(2,1)}, u32[]{:S(2)}, u32[]{:S(2)}) collective-permute-start(bf16[768,1280]{1,0:T(8,128)(2,1)} %dynamic-slice_convert_fusion), channel_id=1, source_target_pairs={{0,1},{1,0},{2,3},{3,2},{4,5},{5,4},{6,7},{7,6},{8,9},{9,8},{10,11... | collective-permute-start | bytes 5898248 | tf_op jit(solution)/shard_map/ppermute | solution.py:48
  426.7 30.7 %collective-permute-start.58 = (bf16[192,512]{0,1:T(8,128)(2,1)S(1)}, bf16[192,512]{0,1:T(8,128)(2,1)S(1)}, u32[]{:S(2)}, u32[]{:S(2)}) collective-permute-start(bf16[192,512]{0,1:T(8,128)(2,1)S(1)} %get-tuple-element.129), channel_id=1, source_target_pairs={{0,24},{8,16},{16,8},{24,0},{1,25},{9,17},{17,9},{25,1},{2,26},{10... | collective-permute-start | bytes 589832 | tf_op jit(solution)/shard_map/ppermute | solution.py:48
  428.0 29.3 %collective-permute-start.57 = (bf16[192,512]{0,1:T(8,128)(2,1)S(1)}, bf16[192,512]{0,1:T(8,128)(2,1)S(1)}, u32[]{:S(2)}, u32[]{:S(2)}) collective-permute-start(bf16[192,512]{0,1:T(8,128)(2,1)S(1)} %get-tuple-element.130), channel_id=1, source_target_pairs={{0,16},{8,24},{16,0},{24,8},{1,17},{9,25},{17,1},{25,9},{2,18},{10... | collective-permute-start | bytes 589832 | tf_op jit(solution)/shard_map/ppermute | solution.py:48
  429.2 28.2 %collective-permute-start.56 = (bf16[192,512]{0,1:T(8,128)(2,1)S(1)}, bf16[192,512]{0,1:T(8,128)(2,1)S(1)}, u32[]{:S(2)}, u32[]{:S(2)}) collective-permute-start(bf16[192,512]{0,1:T(8,128)(2,1)S(1)} %get-tuple-element.128), channel_id=1, source_target_pairs={{0,8},{8,0},{16,24},{24,16},{1,9},{9,1},{17,25},{25,17},{2,10},{10... | collective-permute-start | bytes 589832 | tf_op jit(solution)/shard_map/ppermute | solution.py:48
  484.7 55.9 %collective-permute-start.65 = (bf16[192,512]{1,0:T(8,128)(2,1)S(1)}, bf16[192,512]{1,0:T(8,128)(2,1)S(1)}, u32[]{:S(2)}, u32[]{:S(2)}) collective-permute-start(bf16[192,512]{1,0:T(8,128)(2,1)S(1)} %get-tuple-element.186), channel_id=1, source_target_pairs={{0,1},{1,0},{2,3},{3,2},{4,5},{5,4},{6,7},{7,6},{8,9},{9,8},{10,11... | collective-permute-start | bytes 589832 | tf_op jit(solution)/shard_map/ppermute | solution.py:48
  488.1 15.0 %collective-permute-start.47 = (bf16[192,1280]{1,0:T(8,128)(2,1)S(1)}, bf16[192,1280]{1,0:T(8,128)(2,1)S(1)}, u32[]{:S(2)}, u32[]{:S(2)}) collective-permute-start(bf16[192,1280]{1,0:T(8,128)(2,1)S(1)} %get-tuple-element.121), channel_id=1, source_target_pairs={{0,24},{8,16},{16,8},{24,0},{1,25},{9,17},{17,9},{25,1},{2,26},{10... | collective-permute-start | bytes 1474568 | tf_op jit(solution)/shard_map/ppermute | solution.py:48
  489.5 23.7 %collective-permute-start.46 = (bf16[192,1280]{1,0:T(8,128)(2,1)S(1)}, bf16[192,1280]{1,0:T(8,128)(2,1)S(1)}, u32[]{:S(2)}, u32[]{:S(2)}) collective-permute-start(bf16[192,1280]{1,0:T(8,128)(2,1)S(1)} %get-tuple-element.122), channel_id=1, source_target_pairs={{0,16},{8,24},{16,0},{24,8},{1,17},{9,25},{17,1},{25,9},{2,18},{10... | collective-permute-start | bytes 1474568 | tf_op jit(solution)/shard_map/ppermute | solution.py:48
  490.2 23.1 %collective-permute-start.45 = (bf16[192,1280]{1,0:T(8,128)(2,1)S(1)}, bf16[192,1280]{1,0:T(8,128)(2,1)S(1)}, u32[]{:S(2)}, u32[]{:S(2)}) collective-permute-start(bf16[192,1280]{1,0:T(8,128)(2,1)S(1)} %get-tuple-element.120), channel_id=1, source_target_pairs={{0,8},{8,0},{16,24},{24,16},{1,9},{9,1},{17,25},{25,17},{2,10},{10... | collective-permute-start | bytes 1474568 | tf_op jit(solution)/shard_map/ppermute | solution.py:48
  (149 other events, 1513.2 us)

commit v2 on v0

v2 whole, which is shorter than its diff:
```python
import functools
import math

import jax
import jax.numpy as jnp
from jax import lax
from jax.experimental import pallas as pl
from jax.experimental.pallas import tpu as pltpu
from jax.sharding import PartitionSpec as P

HEAD_DIM = 64
SEQ = 197


NORM_EPS = 1e-06
SQRT_HALF = 0.7071067811865476
INV_ROOT_TWO_PI = 0.3989422804014327


def normalize(values):
    center = values - jnp.mean(values, axis=-1, keepdims=True)
    inv_std = lax.rsqrt(jnp.mean(center * center, axis=-1, keepdims=True) + NORM_EPS)
    return (center * inv_std, inv_std)


def norm_back(grad_in, normed, inv_std, gain_vec):
    scaled = grad_in * gain_vec
    mean_plain = jnp.mean(scaled, axis=-1, keepdims=True)
    mean_mixed = jnp.mean(scaled * normed, axis=-1, keepdims=True)
    return inv_std * (scaled - mean_plain - normed * mean_mixed)


def gelu_value(pre_act):
    return 0.5 * pre_act * (1.0 + lax.erf(pre_act * SQRT_HALF))


def gelu_slope(pre_act):
    return 0.5 * (1.0 + lax.erf(pre_act * SQRT_HALF)) + pre_act * INV_ROOT_TWO_PI * jnp.exp(
        -0.5 * pre_act * pre_act
    )


def swap(values, axis, mask):
    size = lax.axis_size(axis)
    return lax.ppermute(values, axis, [(index, index ^ mask) for index in range(size)])


def gather_shared(shard):
    groups = lax.axis_size("dp")
    rows = shard.shape[0]
    if groups != 4:
        return [lax.all_gather(shard, "dp", axis=0, tiled=True)], [jnp.int32(0)]
    me = lax.axis_index("dp")
    core = lax.axis_index("expert") % 2
    half = rows // 2
    part = half // 2
    mine = lax.dynamic_slice_in_dim(shard, core * half, half, 0)
    from_one = swap(mine, "dp", 1)
    from_two = swap(mine, "dp", 2)
    far_low = swap(from_one[:part], "dp", 2)
    far_high = swap(from_two[part:], "dp", 1)
    other_one = swap(from_one, "expert", 1)
    other_two = swap(from_two, "expert", 1)
    other_low = swap(far_low, "expert", 1)
    other_high = swap(far_high, "expert", 1)
    base = core * half
    other = half - base
    one, two, far = (me ^ 1) * rows, (me ^ 2) * rows, (me ^ 3) * rows
    starts = [me * rows, one + base, two + base, far + base, far + base + part]
    starts += [one + other, two + other, far + other, far + other + part]
    pieces = [shard, from_one, from_two, far_low, far_high]
    pieces += [other_one, other_two, other_low, other_high]
    return pieces, starts


def gather_rows(rows):
    groups = lax.axis_size("dp")
    if groups != 4:
        return [rows] + [swap(rows, "dp", mask) for mask in range(1, groups)]
    half = rows.shape[0] // 2
    from_one = swap(rows, "dp", 1)
    from_two = swap(rows, "dp", 2)
    return [
        rows,
        from_one,
        from_two,
        swap(from_one[:half], "dp", 2),
        swap(from_two[half:], "dp", 1),
    ]


def exchange(blocks):
    return [blocks[0]] + [swap(blocks[mask], "expert", mask) for mask in range(1, len(blocks))]


def in_order(pieces, me, axis):
    stack = jnp.stack(pieces)
    return jnp.concatenate(
        [
            lax.dynamic_index_in_dim(stack, me ^ index, 0, keepdims=False)
            for index in range(len(pieces))
        ],
        axis=axis,
    )


VMEM = pl.BlockSpec(memory_space=pltpu.VMEM)
SMEM = pl.BlockSpec(memory_space=pltpu.SMEM)
NARROW = jnp.bfloat16
WIDE = jnp.float32
MIB = 1024 * 1024


def like(shape, dtype):
    return jax.ShapeDtypeStruct(shape, dtype)


def run(body, outs, operands, flops, moved, mib, scalars=0, scratch=(), name=None):
    return pl.pallas_call(
        body,
        out_shape=outs,
        in_specs=[SMEM] * scalars + [VMEM] * (len(operands) - scalars),
        out_specs=jax.tree.map(lambda _: VMEM, outs),
        scratch_shapes=list(scratch),
        compiler_params=pltpu.CompilerParams(vmem_limit_bytes=mib * MIB),
        cost_estimate=pl.CostEstimate(flops=flops, bytes_accessed=moved, transcendentals=0),
        name=name,
    )(*operands)


def mm(left, right):
    return jnp.dot(left, right, preferred_element_type=WIDE)


def mm_rows(left, right):
    return lax.dot_general(left, right, (((1,), (1,)), ((), ())), preferred_element_type=WIDE)


def mm_cols(left, right):
    return lax.dot_general(left, right, (((0,), (0,)), ((), ())), preferred_element_type=WIDE)


def head_masks(rows):
    lanes = lax.broadcasted_iota(jnp.int32, (rows, 2 * HEAD_DIM), 1)
    return [lanes < HEAD_DIM, lanes >= HEAD_DIM]


def join_body(count, *refs):
    out_ref, wide_ref = refs[count], refs[count + 1]
    at = 0
    for ref in refs[:count]:
        wide_ref[at : at + ref.shape[0], :] = ref[...].astype(WIDE)
        at += ref.shape[0]
    out_ref[...] = wide_ref[...].astype(NARROW)


def join(pieces):
    rows = sum(piece.shape[0] for piece in pieces)
    columns = pieces[0].shape[1]
    return run(
        functools.partial(join_body, len(pieces)),
        like((rows, columns), NARROW),
        pieces,
        rows * columns,
        4 * rows * columns,
        16,
        scratch=[pltpu.VMEM((rows, columns), WIDE)],
        name="join",
    )


def slot_rows(targets, total, tokens):
    ids = lax.broadcasted_iota(jnp.int32, (total, tokens), 0)
    return ids == targets[0:1, :], ids == targets[1:2, :]


def grad_slots_body(experts, d_ref, routes_ref, targets_ref, *outs):
    tokens, width = d_ref.shape
    slots = outs[0].shape[0]
    first, second = slot_rows(targets_ref[...], experts * slots, tokens)
    first, second = first.astype(NARROW), second.astype(NARROW)
    rows = mm(first + second, d_ref[...]).astype(NARROW)
    lanes = lax.broadcasted_iota(jnp.int32, (tokens, 128), 1)
    other_first = (lanes == routes_ref[:, 1:2]).astype(NARROW)
    other_second = (lanes == routes_ref[:, 0:1]).astype(NARROW)
    marks = (mm(first, other_first) + mm(second, other_second)).astype(NARROW)
    for index, out in enumerate(outs):
        out[:, :width] = rows[index * slots : (index + 1) * slots, :]
        out[:, width:] = marks[index * slots : (index + 1) * slots, :]


def attend_body(count, parts, *refs):
    starts_ref, x_ref, columns_ref = refs[0], refs[1], refs[2]
    pieces = refs[3 : 3 + count]
    full_ref, vec_ref, a_ref, qkv_ref, ctx_ref, lse_ref, asel_ref, csel_ref = refs[3 + count :]
    for index, piece in enumerate(pieces):
        rows = piece.shape[0]
        at = starts_ref[index] if count > 1 else 0
        if count > 1:
            at = pl.multiple_of(at, 16)
        full_ref[pl.ds(at, rows), :] = piece[...]
    tokens, width = x_ref.shape
    side = jnp.transpose(full_ref[:, 3 * width :].astype(WIDE))
    vec_ref[...] = side[: vec_ref.shape[0], :]
    bias_q, bias_v = vec_ref[0:1, :], vec_ref[1:2, :]
    gain, bias = vec_ref[3:4, :], vec_ref[4:5, :]
    normed, _ = normalize(x_ref[...].astype(WIDE))
    a_ref[...] = (normed * gain + bias).astype(NARROW)
    a_in = a_ref[...]
    qkv_ref[:, :width] = (mm(a_in, full_ref[:, :width]) + bias_q).astype(NARROW)
    qkv_ref[:, width : 2 * width] = mm(a_in, full_ref[:, width : 2 * width]).astype(NARROW)
    qkv_ref[:, 2 * width :] = (
        mm(a_in, full_ref[:, 2 * width : 3 * width]) + bias_v
    ).astype(NARROW)
    masks = head_masks(tokens)
    lanes = lax.broadcasted_iota(jnp.int32, (tokens, 128), 1)
    lse_all = jnp.zeros((tokens, 128), WIDE)
    pair = 2 * HEAD_DIM
    for group in range(width // pair):
        at = group * pair
        query = qkv_ref[:, at : at + pair]
        keys = qkv_ref[:, width + at : width + at + pair]
        values = qkv_ref[:, 2 * width + at : 2 * width + at + pair]
        outs = []
        for index in range(2):
            scores = mm_rows(jnp.where(masks[index], query, 0), keys) * (
                1.0 / math.sqrt(HEAD_DIM)
            )
            top = jnp.max(scores, axis=-1, keepdims=True)
            exps = jnp.exp(scores - top)
            total = jnp.sum(exps, axis=-1, keepdims=True)
            lse_all = jnp.where(lanes == 2 * group + index, top + jnp.log(total), lse_all)
            outs.append(mm((exps / total).astype(NARROW), values))
        ctx_ref[:, at : at + pair] = jnp.where(masks[0], outs[0], outs[1]).astype(NARROW)
    lse_ref[...] = lse_all
    ids = lax.broadcasted_iota(jnp.int32, (width, columns_ref.shape[1]), 0)
    hot = (ids == columns_ref[0:1, :]).astype(NARROW)
    asel_ref[...] = mm(a_in, hot).astype(NARROW)
    csel_ref[...] = mm(ctx_ref[...], hot).astype(NARROW)


def middle_body(count, experts, *refs):
    starts_ref, ctx_ref, x_ref, vec_ref, targets_ref = refs[:5]
    pieces = refs[5 : 5 + count]
    full_ref, hidden_ref, y_ref = refs[5 + count : 8 + count]
    outs = refs[8 + count :]
    for index, piece in enumerate(pieces):
        rows = piece.shape[0]
        at = starts_ref[index] if count > 1 else 0
        if count > 1:
            at = pl.multiple_of(at, 16)
        full_ref[pl.ds(at, rows), :] = piece[...]
    hidden = x_ref[...].astype(WIDE) + mm(ctx_ref[...], full_ref[...]) + vec_ref[2:3, :]
    hidden_ref[...] = hidden
    normed, _ = normalize(hidden)
    y_in = (normed * vec_ref[5:6, :] + vec_ref[6:7, :]).astype(NARROW)
    y_ref[...] = y_in
    slots = outs[0].shape[0]
    first, second = slot_rows(targets_ref[...], experts * slots, x_ref.shape[0])
    rows = mm((first | second).astype(NARROW), y_in).astype(NARROW)
    for index, out in enumerate(outs):
        out[...] = rows[index * slots : (index + 1) * slots, :]


def slot_gates(rows, marks, router, mine):
    logits = mm_rows(rows, router)
    lanes = lax.broadcasted_iota(jnp.int32, logits.shape, 1)
    own = jnp.sum(jnp.where(lanes == mine, logits, 0.0), axis=-1, keepdims=True)
    other = jnp.sum(
        marks[:, : logits.shape[1]].astype(WIDE) * logits, axis=-1, keepdims=True
    )
    return 1.0 / (1.0 + jnp.exp(other - own))


def gelu_parts(pre_act):
    half = 0.5 * (1.0 + lax.erf(pre_act * SQRT_HALF))
    slope = half + pre_act * INV_ROOT_TWO_PI * jnp.exp(-0.5 * pre_act * pre_act)
    return pre_act * half, slope


def expert_body(experts, me_ref, rows_ref, marked_ref, vec_ref, in_ref, bin_ref, out_ref, bout_ref, *refs):
    fresh = refs[:experts]
    back = refs[experts : 2 * experts]
    sent_ref, acc_ref, dacc_ref = refs[2 * experts :]
    step = pl.program_id(0)
    width = rows_ref.shape[1]

    @pl.when(step == 0)
    def _():
        router = vec_ref[8:32, :].astype(NARROW)
        gate = slot_gates(rows_ref[...], marked_ref[:, width:], router, me_ref[0])
        sent_ref[...] = (gate * marked_ref[:, :width].astype(WIDE)).astype(NARROW)
        acc_ref[...] = jnp.zeros_like(acc_ref)
        dacc_ref[...] = jnp.zeros_like(dacc_ref)

    weight_in, weight_out = in_ref[...], out_ref[...]
    pre_act = mm(rows_ref[...], weight_in) + bin_ref[...].astype(WIDE)
    act, slope = gelu_parts(pre_act)
    acc_ref[...] += mm(act.astype(NARROW), weight_out)
    d_pre = mm_rows(sent_ref[...], weight_out) * slope
    dacc_ref[...] += mm_rows(d_pre.astype(NARROW), weight_in)

    @pl.when(step == pl.num_programs(0) - 1)
    def _():
        bias = bout_ref[...].astype(WIDE)
        slots = fresh[0].shape[0]
        for index in range(experts):
            at = index * slots
            fresh[index][...] = (acc_ref[at : at + slots, :] + bias).astype(NARROW)
            back[index][...] = dacc_ref[at : at + slots, :].astype(NARROW)


def expert(me, rows, marked, vec, weight_in, b_in, weight_out, b_out, experts, slots, chunk):
    total, width = rows.shape
    hidden_units = weight_in.shape[1]
    whole = lambda array: pl.BlockSpec(array.shape, lambda step: (0, 0))
    block = like((slots, width), NARROW)
    return pl.pallas_call(
        functools.partial(expert_body, experts),
        grid=(hidden_units // chunk,),
        out_shape=[block] * (2 * experts),
        in_specs=[
            SMEM,
            whole(rows),
            whole(marked),
            whole(vec),
            pl.BlockSpec((width, chunk), lambda step: (0, step)),
            pl.BlockSpec((1, chunk), lambda step: (0, step)),
            pl.BlockSpec((chunk, width), lambda step: (step, 0)),
            whole(b_out),
        ],
        out_specs=[pl.BlockSpec((slots, width), lambda step: (0, 0))] * (2 * experts),
        scratch_shapes=[
            pltpu.VMEM((total, width), NARROW),
            pltpu.VMEM((total, width), WIDE),
            pltpu.VMEM((total, width), WIDE),
        ],
        compiler_params=pltpu.CompilerParams(vmem_limit_bytes=32 * MIB),
        cost_estimate=pl.CostEstimate(
            flops=8 * total * width * hidden_units,
            bytes_accessed=4 * width * hidden_units,
            transcendentals=0,
        ),
        name="expert",
    )(me, rows, marked, vec, weight_in, b_in, weight_out, b_out)


def weights_body(count, me_ref, vec_ref, in_ref, bin_ref, out_ref, *refs):
    rows_in, marked_in = refs[:count], refs[count : 2 * count]
    dout_ref, din_ref, dbin_ref, dbout_ref, rows_ref, sent_ref = refs[2 * count :]
    width = in_ref.shape[0]

    @pl.when(pl.program_id(0) == 0)
    def _():
        router = vec_ref[8:32, :].astype(NARROW)
        at = 0
        total = jnp.zeros((1, width), WIDE)
        for rows, marked in zip(rows_in, marked_in):
            size = rows.shape[0]
            gate = slot_gates(rows[...], marked[:, width:], router, me_ref[0])
            sent = (gate * marked[:, :width].astype(WIDE)).astype(NARROW)
            rows_ref[at : at + size, :] = rows[...]
            sent_ref[at : at + size, :] = sent
            total += jnp.sum(sent.astype(WIDE), axis=0, keepdims=True)
            at += size
        dbout_ref[...] = total

    pre_act = mm(rows_ref[...], in_ref[...]) + bin_ref[...].astype(WIDE)
    act, slope = gelu_parts(pre_act)
    dout_ref[...] = mm_cols(act.astype(NARROW), sent_ref[...])
    d_pre = mm_rows(sent_ref[...], out_ref[...]) * slope
    dbin_ref[...] = jnp.sum(d_pre, axis=0, keepdims=True)
    din_ref[...] = mm_cols(rows_ref[...], d_pre.astype(NARROW))


def expert_weights(me, vec, my_in, my_bias, my_out, rows, marked, chunk):
    count = len(rows)
    width, units = my_in.shape
    total = sum(piece.shape[0] for piece in rows)
    whole = lambda array: pl.BlockSpec(array.shape, lambda step: (0, 0))
    return pl.pallas_call(
        functools.partial(weights_body, count),
        grid=(units // chunk,),
        out_shape=[
            like((units, width), WIDE),
            like((width, units), WIDE),
            like((1, units), WIDE),
            like((1, width), WIDE),
        ],
        in_specs=[
            SMEM,
            whole(vec),
            pl.BlockSpec((width, chunk), lambda step: (0, step)),
            pl.BlockSpec((1, chunk), lambda step: (0, step)),
            pl.BlockSpec((chunk, width), lambda step: (step, 0)),
        ]
        + [whole(piece) for piece in rows + marked],
        out_specs=[
            pl.BlockSpec((chunk, width), lambda step: (step, 0)),
            pl.BlockSpec((width, chunk), lambda step: (0, step)),
            pl.BlockSpec((1, chunk), lambda step: (0, step)),
            pl.BlockSpec((1, width), lambda step: (0, 0)),
        ],
        scratch_shapes=[
            pltpu.VMEM((total, width), NARROW),
            pltpu.VMEM((total, width), NARROW),
        ],
        compiler_params=pltpu.CompilerParams(vmem_limit_bytes=(36 if count < 8 else 60) * MIB),
        cost_estimate=pl.CostEstimate(
            flops=8 * total * width * units,
            bytes_accessed=16 * total * width,
            transcendentals=0,
        ),
        name="expert_weights",
    )(me, vec, my_in, my_bias, my_out, *rows, *marked)


def combine_body(experts, *refs):
    hidden_ref, y_ref, d_ref, vec_ref, full_ref, routes_ref, targets_ref = refs[:7]
    fresh = refs[7 : 7 + experts]
    back = refs[7 + experts : 7 + 2 * experts]
    out_ref, dh_ref, dhlow_ref, dctx_ref, sums_ref, ret_ref, dret_ref = refs[7 + 2 * experts :]
    tokens, width = hidden_ref.shape
    slots = fresh[0].shape[0]
    for index in range(experts):
        at = index * slots
        ret_ref[at : at + slots, :] = fresh[index][...].astype(WIDE)
        dret_ref[at : at + slots, :] = back[index][...].astype(WIDE)
    lanes = lax.broadcasted_iota(jnp.int32, (tokens, experts * slots), 1)
    first = lanes == targets_ref[:, 0:1]
    second = lanes == targets_ref[:, 1:2]
    returned = ret_ref[...].astype(NARROW)
    picked_first = mm(first.astype(NARROW), returned)
    picked_second = mm(second.astype(NARROW), returned)
    router = vec_ref[8:32, :].astype(NARROW)
    y_in = y_ref[...]
    logits = mm_rows(y_in, router)
    names = lax.broadcasted_iota(jnp.int32, logits.shape, 1)
    hot_first = (names == routes_ref[:, 0:1]).astype(WIDE)
    hot_second = (names == routes_ref[:, 1:2]).astype(WIDE)
    chosen_first = jnp.sum(logits * hot_first, axis=-1, keepdims=True)
    chosen_second = jnp.sum(logits * hot_second, axis=-1, keepdims=True)
    gate_first = 1.0 / (1.0 + jnp.exp(chosen_second - chosen_first))
    gate_second = 1.0 - gate_first
    hidden = hidden_ref[...]
    out_ref[...] = (
        hidden + (gate_first * picked_first + gate_second * picked_second)
    ).astype(NARROW)
    grad = d_ref[...].astype(WIDE)
    d_gate = jnp.sum(grad * picked_first, axis=-1, keepdims=True) - jnp.sum(
        grad * picked_second, axis=-1, keepdims=True
    )
    d_diff = d_gate * gate_first * gate_second
    d_logits = (d_diff * (hot_first - hot_second)).astype(NARROW)
    sums_ref[8:32, :] = mm_cols(d_logits, y_in)
    d_y = mm((first | second).astype(NARROW), dret_ref[...].astype(NARROW)) + mm(
        d_logits, router
    )
    normed, inv_std = normalize(hidden)
    d_hidden = grad + norm_back(d_y, normed, inv_std, vec_ref[5:6, :])
    sums_ref[0:8, :] = jnp.zeros((8, width), WIDE)
    sums_ref[0:1, :] = jnp.sum(d_hidden, axis=0, keepdims=True)
    sums_ref[1:2, :] = jnp.sum(d_y * normed, axis=0, keepdims=True)
    sums_ref[2:3, :] = jnp.sum(d_y, axis=0, keepdims=True)
    dh_ref[...] = d_hidden
    low = d_hidden.astype(NARROW)
    dhlow_ref[...] = low
    dctx_ref[...] = mm_rows(low, full_ref[...]).astype(NARROW)


def attend_back_body(start, qkv_ref, dctx_ref, lse_ref, out_ref, sums_ref):
    tokens = qkv_ref.shape[0]
    width = dctx_ref.shape[1]
    columns = out_ref.shape[1] // 3
    masks = head_masks(tokens)
    lanes = lax.broadcasted_iota(jnp.int32, (tokens, 128), 1)
    pair = 2 * HEAD_DIM
    scale = 1.0 / math.sqrt(HEAD_DIM)
    sums_ref[...] = jnp.zeros_like(sums_ref)
    for group in range(columns // pair):
        to = group * pair
        at = start + to
        query = qkv_ref[:, at : at + pair]
        keys = qkv_ref[:, width + at : width + at + pair]
        values = qkv_ref[:, 2 * width + at : 2 * width + at + pair]
        grads = dctx_ref[:, at : at + pair]
        d_query = d_keys = d_values = None
        for index in range(2):
            zero = jnp.zeros_like(query)
            query_h = jnp.where(masks[index], query, zero)
            keys_h = jnp.where(masks[index], keys, zero)
            grads_h = jnp.where(masks[index], grads, zero)
            head = (start + to) // HEAD_DIM + index
            lse = jnp.sum(jnp.where(lanes == head, lse_ref[...], 0.0), axis=-1, keepdims=True)
            probs = jnp.exp(mm_rows(query_h, keys) * scale - lse)
            d_probs = mm_rows(grads_h, values)
            delta = jnp.sum(probs * d_probs, axis=-1, keepdims=True)
            d_scores = (probs * (d_probs - delta) * scale).astype(NARROW)
            new_values = mm_cols(probs.astype(NARROW), grads_h)
            new_query = mm(d_scores, keys_h)
            new_keys = mm_cols(d_scores, query_h)
            d_values = new_values if d_values is None else d_values + new_values
            d_query = new_query if d_query is None else d_query + new_query
            d_keys = new_keys if d_keys is None else d_keys + new_keys
        out_ref[:, to : to + pair] = d_query.astype(NARROW)
        out_ref[:, columns + to : columns + to + pair] = d_keys.astype(NARROW)
        out_ref[:, 2 * columns + to : 2 * columns + to + pair] = d_values.astype(NARROW)
        sums_ref[0:1, to : to + pair] = jnp.sum(d_query, axis=0, keepdims=True)
        sums_ref[1:2, to : to + pair] = jnp.sum(d_values, axis=0, keepdims=True)


def finish_body(low_ref, high_ref, full_ref, x_ref, vec_ref, dh_ref, dx_ref, sums_ref):
    width = x_ref.shape[1]
    columns = low_ref.shape[1] // 3
    d_a = None
    for half, ref in enumerate((low_ref, high_ref)):
        for third in range(3):
            at = third * width + half * columns
            new = mm_rows(
                ref[:, third * columns : (third + 1) * columns], full_ref[:, at : at + columns]
            )
            d_a = new if d_a is None else d_a + new
    normed, inv_std = normalize(x_ref[...].astype(WIDE))
    sums_ref[...] = jnp.zeros_like(sums_ref)
    sums_ref[0:1, :] = jnp.sum(d_a * normed, axis=0, keepdims=True)
    sums_ref[1:2, :] = jnp.sum(d_a, axis=0, keepdims=True)
    dx_ref[...] = dh_ref[...] + norm_back(d_a, normed, inv_std, vec_ref[3:4, :])


def outer_body(groups, left_ref, left_other_ref, right_ref, right_other_ref, own_ref, *outs):
    rows = own_ref.shape[0]
    total = mm_cols(left_ref[...], right_ref[...]) + mm_cols(
        left_other_ref[...], right_other_ref[...]
    )
    own_ref[...] = total[:rows, :]
    for index in range(1, groups):
        outs[index - 1][...] = total[index * rows : (index + 1) * rows, :].astype(NARROW)


def outer(left, left_other, right, right_other, groups):
    tokens, rows = left.shape
    columns = right.shape[1]
    block = rows // groups
    return run(
        functools.partial(outer_body, groups),
        [like((block, columns), WIDE)] + [like((block, columns), NARROW)] * (groups - 1),
        [left, left_other, right, right_other],
        4 * tokens * rows * columns,
        6 * rows * columns,
        24,
        name="outer",
    )


def reduce_blocks(own, others):
    layers = lax.axis_size("expert") // 2
    total = own
    for mask, block in enumerate(others, 1):
        total = total + swap(block, "dp", mask).astype(WIDE)
    part = own.shape[0] // layers
    done = total[:part]
    low = total.astype(NARROW)
    for mask in range(1, layers):
        piece = swap(low[mask * part : (mask + 1) * part], "expert", 2 * mask)
        done = done + piece.astype(WIDE)
    done = done.astype(NARROW)
    return jnp.concatenate(
        [done] + [swap(done, "expert", 2 * mask) for mask in range(1, layers)], axis=0
    )


def expert_weights_plain(me, vec, my_in, my_bias, my_out, rows, marked):
    rows, marked = jnp.concatenate(rows, axis=0), jnp.concatenate(marked, axis=0)
    width = rows.shape[1]
    gate = slot_gates(rows, marked[:, width:], vec[8:32].astype(NARROW), me)
    sent = (gate * marked[:, :width].astype(WIDE)).astype(NARROW)
    act, slope = gelu_parts(mm(rows, my_in) + my_bias.astype(WIDE))
    d_pre = mm_rows(sent, my_out) * slope
    return (
        mm_cols(act.astype(NARROW), sent),
        mm_cols(rows, d_pre.astype(NARROW)),
        jnp.sum(d_pre, axis=0, keepdims=True),
        jnp.sum(sent.astype(WIDE), axis=0, keepdims=True),
    )


def per_device(
    block_input,
    w_qkv,
    b_q,
    b_v,
    w_proj,
    b_proj,
    ln1_gain,
    ln1_bias,
    ln2_gain,
    ln2_bias,
    w_router,
    w_in,
    b_in,
    w_out,
    b_out,
    routes,
    slot_index,
    d_out,
):
    tokens, width = block_input.shape
    hidden_units = w_in.shape[2]
    experts = w_in.shape[0] * lax.axis_size("expert")
    groups = lax.axis_size("dp")
    layers = lax.axis_size("expert") // 2
    capacity = 2 * tokens // experts
    slots = -(-capacity // 8) * 8
    dp_me = lax.axis_index("dp")
    expert_me = lax.axis_index("expert")
    core, layer = expert_me % 2, expert_me // 2
    vectors = jnp.stack([b_q, b_v, b_proj, ln1_gain, ln1_bias, ln2_gain, ln2_bias], axis=1)
    side_cols = jnp.concatenate([vectors, jnp.zeros_like(vectors[:, :1]), w_router], axis=1)
    side_cols = jnp.pad(side_cols, ((0, 0), (0, 128 - side_cols.shape[1])))
    qkv_pieces, qkv_starts = gather_shared(jnp.concatenate([w_qkv, side_cols], axis=1))
    proj_pieces, proj_starts = gather_shared(w_proj)
    starts = jnp.stack(qkv_starts).astype(jnp.int32)
    me = expert_me.reshape(1).astype(jnp.int32)
    targets = jnp.where(slot_index < capacity, (routes ^ expert_me) * slots + slot_index, -1)
    targets_row = targets.T
    share = width // groups
    part = share // (2 * layers)
    order = jnp.arange(width // 2, dtype=jnp.int32)
    group_of = order // (share // 2)
    layer_of = order // part % layers
    spot = (group_of ^ dp_me) * share + (layer_of ^ layer) * part + order % part
    chosen_columns = jnp.concatenate(
        [spot + core * (share // 2), spot + (1 - core) * (share // 2)]
    )[None].astype(jnp.int32)

    total = experts * slots
    marked_blocks = run(
        functools.partial(grad_slots_body, experts),
        [like((slots, width + 128), NARROW)] * experts,
        [d_out, routes, targets_row],
        2 * total * tokens * width,
        4 * total * width,
        16,
        name="grad_slots",
    )
    marked = join(exchange(marked_blocks))
    marked_all = gather_rows(marked)

    count = len(qkv_pieces)
    wide = w_qkv.shape[1] + 128
    full_qkv, vec, a_in, qkv, context, log_total, a_sel, ctx_sel = run(
        functools.partial(attend_body, count, part),
        [
            like((width, wide), NARROW),
            like((32, width), WIDE),
            like((tokens, width), NARROW),
            like((tokens, 3 * width), NARROW),
            like((tokens, width), NARROW),
            like((tokens, 128), WIDE),
            like((tokens, width), NARROW),
            like((tokens, width), NARROW),
        ],
        [starts, block_input, chosen_columns] + qkv_pieces,
        10 * tokens * width * width,
        4 * width * wide,
        40,
        scalars=1,
        name="attend",
    )
    half = width // 2
    a_keep, ctx_keep = a_sel[:, :half], ctx_sel[:, :half]
    a_other = swap(a_sel[:, half:], "expert", 1)
    ctx_other = swap(ctx_sel[:, half:], "expert", 1)
    middle = run(
        functools.partial(middle_body, count, experts),
        [
            like((width, width), NARROW),
            like((tokens, width), WIDE),
            like((tokens, width), NARROW),
        ]
        + [like((slots, width), NARROW)] * experts,
        [jnp.stack(proj_starts).astype(jnp.int32), context, block_input, vec, targets_row]
        + proj_pieces,
        4 * tokens * width * width,
        4 * width * width,
        24,
        scalars=1,
        name="middle",
    )
    full_proj, hidden, y_in = middle[:3]
    rows = join(exchange(middle[3:]))
    rows_all = gather_rows(rows)
    weight_in, weight_out = w_in[0], w_out[0]
    results = expert(
        me, rows, marked, vec, weight_in, b_in, weight_out, b_out, experts, slots, 512
    )
    d_returned = exchange(results[experts:])
    returned = exchange(results[:experts])

    units = hidden_units // groups
    my_in = lax.dynamic_slice_in_dim(weight_in, dp_me * units, units, 1)
    my_out = lax.dynamic_slice_in_dim(weight_out, dp_me * units, units, 0)
    my_bias = lax.dynamic_slice_in_dim(b_in, dp_me * units, units, 1)
    if groups == 4:
        part_w_out, d_w_in, part_b_in, sum_sent = expert_weights(
            me, vec, my_in, my_bias, my_out, rows_all, marked_all, 256
        )
    else:
        part_w_out, d_w_in, part_b_in, sum_sent = expert_weights_plain(
            expert_me, vec, my_in, my_bias, my_out, rows_all, marked_all
        )
    part_b_out = lax.dynamic_slice_in_dim(sum_sent[0], dp_me * share, share, 0)
    pieces = [lax.dynamic_slice_in_dim(d_w_in, dp_me * share, share, 0)]
    for mask in range(1, groups):
        piece = lax.dynamic_slice_in_dim(d_w_in, (dp_me ^ mask) * share, share, 0)
        pieces.append(swap(piece.astype(NARROW), "dp", mask).astype(WIDE))
    part_w_in = in_order(pieces, dp_me, 1)

    block_out, d_hidden, d_hidden_low, d_context, early_sums = run(
        functools.partial(combine_body, experts),
        [
            like((tokens, width), NARROW),
            like((tokens, width), WIDE),
            like((tokens, width), NARROW),
            like((tokens, width), NARROW),
            like((32, width), WIDE),
        ],
        [hidden, y_in, d_out, vec, full_proj, routes, targets] + returned + d_returned,
        6 * tokens * total * width + 2 * tokens * width * width,
        4 * width * width,
        24,
        scratch=[pltpu.VMEM((total, width), WIDE)] * 2,
        name="combine",
    )
    hidden_other = swap(d_hidden_low, "expert", 1)
    proj_blocks = outer(ctx_keep, ctx_other, d_hidden_low, hidden_other, groups)
    proj_sum = reduce_blocks(proj_blocks[0], proj_blocks[1:])

    def back(start):
        return run(
            functools.partial(attend_back_body, start),
            [like((tokens, 3 * half), NARROW), like((8, half), WIDE)],
            [qkv, d_context, log_total],
            16 * tokens * 256 * width,
            8 * tokens * width,
            24,
            name="attend_back",
        )

    d_low, low_sums = back(0)
    low_other = swap(d_low, "expert", 1)
    d_high, high_sums = back(half)
    high_other = swap(d_high, "expert", 1)
    low_blocks = outer(a_keep, a_other, d_low, low_other, groups)
    low_sum = reduce_blocks(low_blocks[0], low_blocks[1:])
    high_blocks = outer(a_keep, a_other, d_high, high_other, groups)
    high_sum = reduce_blocks(high_blocks[0], high_blocks[1:])
    d_input, late_sums = run(
        finish_body,
        [like((tokens, width), WIDE), like((8, width), WIDE)],
        [d_low, d_high, full_qkv, block_input, vec, d_hidden],
        6 * tokens * width * width,
        6 * width * width,
        24,
        name="finish",
    )
    sums = jnp.concatenate(
        [
            early_sums[:3],
            jnp.concatenate([low_sums[:2], high_sums[:2]], axis=1),
            late_sums[:2],
            jnp.zeros((1, width), WIDE),
            early_sums[8 : 8 + experts],
        ],
        axis=0,
    )
    vector_sum = lax.dynamic_slice_in_dim(sums, dp_me * share, share, 1)
    for mask in range(1, groups):
        piece = lax.dynamic_slice_in_dim(sums, (dp_me ^ mask) * share, share, 1)
        vector_sum = vector_sum + swap(piece, "dp", mask)
    for mask in range(layers.bit_length() - 1):
        vector_sum = vector_sum + swap(vector_sum, "expert", 2 << mask)
    vector_sum = vector_sum + swap(vector_sum, "expert", 1)

    gathered = jnp.concatenate([proj_sum, low_sum, high_sum], axis=1)
    gathered = jnp.concatenate([gathered, swap(gathered, "expert", 1)], axis=0)
    place = jnp.arange(share // 2, dtype=jnp.int32)
    place = (place // part ^ layer) * part + place % part
    place = jnp.concatenate([place + core * (share // 2), place + (1 - core) * (share // 2)])
    hot = (jnp.arange(share, dtype=jnp.int32)[:, None] == place[None, :]).astype(NARROW)
    ordered = jnp.dot(hot, gathered, preferred_element_type=WIDE)
    third = half
    columns = [
        ordered[:, width + side * 3 * third + index * third :][:, :third]
        for index in range(3)
        for side in range(2)
    ]
    return (
        block_out,
        d_input,
        jnp.concatenate(columns, axis=1),
        vector_sum[3],
        vector_sum[4],
        ordered[:, :width],
        vector_sum[0],
        vector_sum[5],
        vector_sum[6],
        vector_sum[1],
        vector_sum[2],
        vector_sum[8 : 8 + experts].T,
        part_w_in[None],
        part_b_in,
        part_w_out[None],
        part_b_out[None],
    )


def solution(mesh):
    return jax.shard_map(
        per_device,
        mesh=mesh,
        in_specs=(
            P(("dp", "expert"), None),
            P("dp", None),
            P("dp"),
            P("dp"),
            P("dp", None),
            P("dp"),
            P("dp"),
            P("dp"),
            P("dp"),
            P("dp"),
            P("dp", None),
            P("expert", None, None),
            P("expert", None),
            P("expert", None, None),
            P("expert", None),
            P(("dp", "expert"), None),
            P(("dp", "expert"), None),
            P(("dp", "expert"), None),
        ),
        out_specs=(
            P(("dp", "expert"), None),
            P(("dp", "expert"), None),
            P("dp", None),
            P("dp"),
            P("dp"),
            P("dp", None),
            P("dp"),
            P("dp"),
            P("dp"),
            P("dp"),
            P("dp"),
            P("dp", None),
            P("expert", "dp", None),
            P("expert", "dp"),
            P("expert", "dp", None),
            P("expert", "dp"),
        ),
        check_vma=False,
    )
```

time: 766 us -> 309 us (0.40)
  waiting for transfers between devices: 506 us -> 97.8 us
  starting transfers between devices: 14.1 us -> 109 us
  matrix products: 72.9 us -> 0.47 us
  blocking collectives: 69.2 us -> 0 us
  Pallas kernels: 0 us -> 50.1 us
  other arithmetic: 22.9 us -> 3.95 us
  between operations: 15.2 us -> 1.57 us
  local copies, waits for them, and re-layouts: 57.3 us -> 44.8 us
    reduce_scatter x4 -> x0, waiting for transfers between devices: 279 us -> none  [the longest x1 98.8 us: per_device(): lax.psum_scatter(d_w_in, 'dp', scatter_dimension=1, tiled=True)]
    ppermute x0 -> x94, starting transfers between devices: none -> 109 us  [swap(): lax.ppermute(values, axis, [(index, index ^ mask) for index in range(size)])]
    ppermute x0 -> x94, waiting for transfers between devices: none -> 97.8 us  [swap(): lax.ppermute(values, axis, [(index, index ^ mask) for index in range(size)])]
    unnamed x15 -> x0, waiting for transfers between devices: 97.7 us -> none
    dot_general x20 -> x1, matrix products: 71.8 us -> 0.47 us  [per_device(): ordered = jnp.dot(hot, gathered, preferred_element_type=WIDE)]
    all_gather x2 -> x0, waiting for transfers between devices: 50.3 us -> none  [the longest x1 30.1 us: per_device(): lax.all_gather(w_qkv, 'dp', axis=0, tiled=True)]
    pallas_call x0 -> x14, Pallas kernels: none -> 50.1 us  [the longest x12 20.2 us: run(): pl.pallas_call(body, out_shape=outs, in_specs=[SMEM] * scalars + [VMEM] *...]
    all_to_all x3 -> x0, waiting for transfers between devices: 40.3 us -> none  [the longest x1 18.8 us: per_device(): lax.all_to_all(sent_slots, 'expert', split_axis=0, concat_axis=0, tiled=T...]
  transfers between devices with their start and end apart: 14 -> 94, of which waited for: 14 -> 31; matrix products, arithmetic and copies ran while one was open for 10% -> 4% of each run, Pallas kernels for 0% -> 12%
where the time goes in v2:
time: 309 us; the launch traced here: 308 us
  starting transfers between devices  109 us (35%)
  waiting for transfers between devices  97.8 us (32%)
  Pallas kernels  50.1 us (16%)
  local copies, waits for them, and re-layouts  44.8 us (14%)
  other arithmetic  3.95 us (1%)
    ppermute x94, starting transfers between devices, swap(): lax.ppermute(values, axis, [(index, index ^ mask) for index in range(size)])  109 us
    ppermute x94, waiting for transfers between devices, swap(): lax.ppermute(values, axis, [(index, index ^ mask) for index in range(size)])  97.8 us
    unnamed x128, local copies, waits for them, and re-layouts  27.1 us
    pallas_call x12, Pallas kernels, run(): pl.pallas_call(body, out_shape=outs, in_specs=[SMEM] * scalars + [VMEM] *...  20.2 us
    pallas_call x1, Pallas kernels, expert_weights(): pl.pallas_call(functools.partial(weights_body, count), grid=(units // chu...  17.2 us
    pallas_call x1, Pallas kernels, expert(): pl.pallas_call(functools.partial(expert_body, experts), grid=(hidden_unit...  12.7 us
  transfers between devices with their start and end apart: 94, of which 31 were waited for; matrix products, arithmetic and copies ran while one was open for 4% of the time, Pallas kernels for 12%

profile of v2, /device:TPU:0, one launch (start us, length us, event | category | flops | bytes accessed | tf_op | source)
XLA Modules:
  0.0 308.0 jit_solution(203986574138087714)
XLA Ops:
  8.3 2.9 collective-permute-start
  17.5 5.5 %collective-permute-done.refs_4_ = bf16[96,2432]{1,0:T(8,128)(2,1)} collective-permute-done((bf16[96,2432]{1,0:T(8,128)(2,1)}, bf16[96,2432]{1,0:T(8,128)(2,1)}, u32[]{:S(2)}, u32[]{:S(2)}) %collective-permute-start) | collective-permute-done | bytes 466976 | tf_op jit(solution)/shard_map/ppermute | solution.py:45
  31.4 5.8 %collective-permute-done.10.refs_8_ = bf16[48,768]{1,0:T(8,128)(2,1)} collective-permute-done((bf16[48,768]{1,0:T(8,128)(2,1)S(1)}, bf16[48,768]{1,0:T(8,128)(2,1)}, u32[]{:S(2)}, u32[]{:S(2)}) %collective-permute-start.10) | collective-permute-done | bytes 73760 | tf_op jit(solution)/shard_map/ppermute | solution.py:45
  38.7 3.0 collective-permute-done.11.refs_9_
  50.8 5.3 %attend.1 = (bf16[768,2432]{1,0:T(8,128)(2,1)S(1)}, f32[32,768]{1,0:T(8,128)S(1)}, bf16[197,768]{1,0:T(8,128)(2,1)}, bf16[197,2304]{1,0:T(8,128)(2,1)S(1)}, bf16...) custom-call(s32[9]{0:T(128)S(1)} %stack.94.refs_0_, ...), custom_call_target="tpu_custom_call" | custom-call | flops 1161953280 | bytes 7471104 | tf_op jit(solution)/shard_map/attend/pallas_call | solution.py:119
  67.3 4.4 %collective-permute-done.27.refs_5_ = bf16[56,896]{1,0:T(8,128)(2,1)S(1)} collective-permute-done((bf16[56,896]{1,0:T(8,128)(2,1)S(1)}, bf16[56,896]{1,0:T(8,128)(2,1)S(1)}, u32[]{:S(2)}, u32[]{:S(2)}) %collective-permute-start.27) | collective-permute-done | bytes 100384 | tf_op jit(solution)/shard_map/ppermute | solution.py:45
  75.2 3.4 %collective-permute-start.21 = (bf16[56,768]{1,0:T(8,128)(2,1)S(1)}, bf16[56,768]{1,0:T(8,128)(2,1)S(1)}, u32[]{:S(2)}, u32[]{:S(2)}) collective-permute-start(bf16[56,768]{1,0:T(8,128)(2,1)S(1)} %get-tuple-element.96), channel_id=1, source_target_pairs={{0,6},{1,7},{2,4},{3,5},{4,2},{5,3},{6,0},{7,1},{8,14},{9,15},{10,... | collective-permute-start | bytes 258056 | tf_op jit(solution)/shard_map/ppermute | solution.py:45
  78.9 6.6 %collective-permute-done.19.refs_4_ = bf16[56,768]{1,0:T(8,128)(2,1)S(1)} collective-permute-done((bf16[56,768]{1,0:T(8,128)(2,1)S(1)}, bf16[56,768]{1,0:T(8,128)(2,1)S(1)}, u32[]{:S(2)}, u32[]{:S(2)}) %collective-permute-start.19) | collective-permute-done | bytes 86048 | tf_op jit(solution)/shard_map/ppermute | solution.py:45
  91.5 12.7 %expert.1 = (bf16[56,768]{1,0:T(8,128)(2,1)S(1)}, bf16[56,768]{1,0:T(8,128)(2,1)}, bf16[56,768]{1,0:T(8,128)(2,1)}, bf16[56,768]{1,0:T(8,128)(2,1)S(1)}, bf16[56...) custom-call(s32[1]{0:T(128)} %bitcast.10.me_ref, ...), custom_call_target="tpu_custom_call" | custom-call | flops 8455716864 | bytes 9437184 | tf_op jit(solution)/shard_map/expert/pallas_call | solution.py:318
  107.8 4.0 %collective-permute-start.31 = (bf16[56,768]{1,0:T(8,128)(2,1)}, bf16[56,768]{1,0:T(8,128)(2,1)S(1)}, u32[]{:S(2)}, u32[]{:S(2)}) collective-permute-start(bf16[56,768]{1,0:T(8,128)(2,1)} %get-tuple-element.108), channel_id=1, source_target_pairs={{0,2},{1,3},{2,0},{3,1},{4,6},{5,7},{6,4},{7,5},{8,10},{9,11},{10,... | collective-permute-start | bytes 258056 | tf_op jit(solution)/shard_map/ppermute | solution.py:45
  122.0 2.8 dynamic-slice_bitcast_fusion
  127.0 3.4 %collective-permute-start.40 = (bf16[56,768]{1,0:T(8,128)(2,1)}, bf16[56,768]{1,0:T(8,128)(2,1)S(1)}, u32[]{:S(2)}, u32[]{:S(2)}) collective-permute-start(bf16[56,768]{1,0:T(8,128)(2,1)} %copy-done.51), channel_id=1, source_target_pairs={{0,4},{1,5},{2,6},{3,7},{4,0},{5,1},{6,2},{7,3},{8,12},{9,13},{10,... | collective-permute-start | bytes 258056 | tf_op jit(solution)/shard_map/ppermute | solution.py:45
  136.7 3.9 %collective-permute-done.40.refs_19_ = bf16[56,768]{1,0:T(8,128)(2,1)S(1)} collective-permute-done((bf16[56,768]{1,0:T(8,128)(2,1)}, bf16[56,768]{1,0:T(8,128)(2,1)S(1)}, u32[]{:S(2)}, u32[]{:S(2)}) %collective-permute-start.40) | collective-permute-done | bytes 86048 | tf_op jit(solution)/shard_map/ppermute | solution.py:45
  149.1 3.7 %combine.1 = (bf16[197,768]{1,0:T(8,128)(2,1)}, f32[197,768]{1,0:T(8,128)S(1)}, bf16[197,768]{1,0:T(8,128)(2,1)S(1)}, bf16[197,768]{1,0:T(8,128)(2,1)S(1)}, f32[32,768]{1,0:T(8,128)S(1)}) custom-call(f32[197,768]{1,0:T(8,128)S(1)} %copy-done.8, bf16[197,768]{1,0:T(8,128)(2,1)S(1)} %copy-done.22, bf16[197,768]{1,0:T(8,128)(2,1)S(1)} %copy-done.20, ...), custom_call_target="tpu_custom_call" | custom-call | flops 639074304 | bytes 2359296 | tf_op jit(solution)/shard_map/combine/pallas_call | solution.py:119
  166.4 4.3 %collective-permute-start.80 = (f32[16,192]{1,0:T(8,128)S(1)}, f32[16,192]{1,0:T(8,128)S(1)}, u32[]{:S(2)}, u32[]{:S(2)}) collective-permute-start(f32[16,192]{1,0:T(8,128)S(1)} %add_add_fusion), channel_id=1, source_target_pairs={{0,2},{1,3},{2,0},{3,1},{4,6},{5,7},{6,4},{7,5},{8,10},{9,11},{10,... | collective-permute-start | bytes 36872 | tf_op jit(solution)/shard_map/ppermute | solution.py:45
  184.1 15.5 %collective-permute-done.48 = bf16[96,768]{1,0:T(8,128)(2,1)S(1)} collective-permute-done((bf16[96,768]{1,0:T(8,128)(2,1)S(1)}, bf16[96,768]{1,0:T(8,128)(2,1)S(1)}, u32[]{:S(2)}, u32[]{:S(2)}) %collective-permute-start.48) | collective-permute-done | bytes 147488 | tf_op jit(solution)/shard_map/ppermute | solution.py:45
  212.3 10.5 %collective-permute-done.84.refs_2_ = bf16[448,768]{1,0:T(8,128)(2,1)S(1)} collective-permute-done((bf16[448,768]{1,0:T(8,128)(2,1)S(1)}, bf16[448,768]{1,0:T(8,128)(2,1)S(1)}, u32[]{:S(2)}, u32[]{:S(2)}) %collective-permute-start.84) | collective-permute-done | bytes 688160 | tf_op jit(solution)/shard_map/ppermute | solution.py:45
  225.9 4.0 %collective-permute-done.68 = bf16[96,1152]{1,0:T(8,128)(2,1)S(1)} collective-permute-done((bf16[96,1152]{1,0:T(8,128)(2,1)S(1)}, bf16[96,1152]{1,0:T(8,128)(2,1)S(1)}, u32[]{:S(2)}, u32[]{:S(2)}) %collective-permute-start.68) | collective-permute-done | bytes 221216 | tf_op jit(solution)/shard_map/ppermute | solution.py:45
  232.1 4.9 %collective-permute-done.59 = bf16[96,1152]{1,0:T(8,128)(2,1)S(1)} collective-permute-done((bf16[96,1152]{1,0:T(8,128)(2,1)S(1)}, bf16[96,1152]{1,0:T(8,128)(2,1)S(1)}, u32[]{:S(2)}, u32[]{:S(2)}) %collective-permute-start.59) | collective-permute-done | bytes 221216 | tf_op jit(solution)/shard_map/ppermute | solution.py:45
  238.9 4.0 %collective-permute-done.58 = bf16[96,1152]{1,0:T(8,128)(2,1)S(1)} collective-permute-done((bf16[96,1152]{1,0:T(8,128)(2,1)S(1)}, bf16[96,1152]{1,0:T(8,128)(2,1)S(1)}, u32[]{:S(2)}, u32[]{:S(2)}) %collective-permute-start.58) | collective-permute-done | bytes 221216 | tf_op jit(solution)/shard_map/ppermute | solution.py:45
  259.9 2.9 collective-permute-done.85.refs_3_
  264.8 17.2 %expert_weights.1 = (f32[768,768]{1,0:T(8,128)}, f32[768,768]{1,0:T(8,128)S(1)}, f32[1,768]{1,0:T(1,128)}, f32[1,768]{1,0:T(1,128)S(1)}) custom-call(s32[1]{0:T(128)} %bitcast.10.me_ref, f32[32,768]{1,0:T(8,128)S(1)} %get-tuple-element.86.refs_3_.vec_ref, bf16[768,768]{1,0:T(8,128)(2,1)S(1)} %copy-done.3, ...), custom_call_target="tpu_custom_call" | custom-call | flops 8455716864 | bytes 22020096 | tf_op jit(solution)/shard_map/expert_weights/pallas_call | solution.py:381
  294.2 3.0 collective-permute-done.93
  297.2 5.7 %collective-permute-done.92 = bf16[192,768]{1,0:T(8,128)(2,1)S(1)} collective-permute-done((bf16[192,768]{1,0:T(8,128)(2,1)S(1)}, bf16[192,768]{1,0:T(8,128)(2,1)S(1)}, u32[]{:S(2)}, u32[]{:S(2)}) %collective-permute-start.92) | collective-permute-done | bytes 294944 | tf_op jit(solution)/shard_map/ppermute | solution.py:45
  (382 shorter events, 167.0 us)
Async XLA Ops:
  11.2 14.9 %collective-permute-start.1 = (bf16[96,2432]{1,0:T(8,128)(2,1)}, bf16[96,2432]{1,0:T(8,128)(2,1)}, u32[]{:S(2)}, u32[]{:S(2)}) collective-permute-start(bf16[96,2432]{1,0:T(8,128)(2,1)} %constant_dynamic-slice_fusion.6), channel_id=1, source_target_pairs={{0,16},{8,24},{16,0},{24,8},{1,17},{9,25},{17,1},{25,9},{2,18},{10... | collective-permute-start | bytes 1400840 | tf_op jit(solution)/shard_map/ppermute | solution.py:45
  26.2 17.4 %collective-permute-start.4 = (bf16[96,2432]{1,0:T(8,128)(2,1)}, bf16[96,2432]{1,0:T(8,128)(2,1)S(1)}, u32[]{:S(2)}, u32[]{:S(2)}) collective-permute-start(bf16[96,2432]{1,0:T(8,128)(2,1)} %collective-permute-done.refs_4_), channel_id=1, source_target_pairs={{0,1},{1,0},{2,3},{3,2},{4,5},{5,4},{6,7},{7,6},{8,9},{9,8},{10,11... | collective-permute-start | bytes 1400840 | tf_op jit(solution)/shard_map/ppermute | solution.py:45
  27.2 18.5 %collective-permute-start.5 = (bf16[96,2432]{1,0:T(8,128)(2,1)}, bf16[96,2432]{1,0:T(8,128)(2,1)}, u32[]{:S(2)}, u32[]{:S(2)}) collective-permute-start(bf16[96,2432]{1,0:T(8,128)(2,1)} %collective-permute-done.1.refs_5_), channel_id=1, source_target_pairs={{0,1},{1,0},{2,3},{3,2},{4,5},{5,4},{6,7},{7,6},{8,9},{9,8},{10,11... | collective-permute-start | bytes 1400840 | tf_op jit(solution)/shard_map/ppermute | solution.py:45
  43.1 16.1 %collective-permute-start.13 = (bf16[96,768]{1,0:T(8,128)(2,1)S(1)}, bf16[96,768]{1,0:T(8,128)(2,1)}, u32[]{:S(2)}, u32[]{:S(2)}) collective-permute-start(bf16[96,768]{1,0:T(8,128)(2,1)S(1)} %collective-permute-done.9.refs_7_), channel_id=1, source_target_pairs={{0,1},{1,0},{2,3},{3,2},{4,5},{5,4},{6,7},{7,6},{8,9},{9,8},{10,11... | collective-permute-start | bytes 442376 | tf_op jit(solution)/shard_map/ppermute | solution.py:45
  44.3 22.5 %collective-permute-start.25 = (bf16[56,896]{1,0:T(8,128)(2,1)}, bf16[56,896]{1,0:T(8,128)(2,1)S(1)}, u32[]{:S(2)}, u32[]{:S(2)}) collective-permute-start(bf16[56,896]{1,0:T(8,128)(2,1)} %copy-done.47), channel_id=1, source_target_pairs={{0,3},{1,2},{2,1},{3,0},{4,7},{5,6},{6,5},{7,4},{8,11},{9,10},{10,... | collective-permute-start | bytes 301064 | tf_op jit(solution)/shard_map/ppermute | solution.py:45
  45.7 21.6 %collective-permute-start.26 = (bf16[56,896]{1,0:T(8,128)(2,1)}, bf16[56,896]{1,0:T(8,128)(2,1)S(1)}, u32[]{:S(2)}, u32[]{:S(2)}) collective-permute-start(bf16[56,896]{1,0:T(8,128)(2,1)} %copy-done.46), channel_id=1, source_target_pairs={{0,4},{1,5},{2,6},{3,7},{4,0},{5,1},{6,2},{7,3},{8,12},{9,13},{10,... | collective-permute-start | bytes 301064 | tf_op jit(solution)/shard_map/ppermute | solution.py:45
  135.2 35.6 %collective-permute-start.87 = (bf16[448,896]{1,0:T(8,128)(2,1)S(1)}, bf16[448,896]{1,0:T(8,128)(2,1)}, u32[]{:S(2)}, u32[]{:S(2)}) collective-permute-start(bf16[448,896]{1,0:T(8,128)(2,1)S(1)} %join.3.marked_ref.refs_5_), channel_id=1, source_target_pairs={{0,8},{8,0},{16,24},{24,16},{1,9},{9,1},{17,25},{25,17},{2,10},{10... | collective-permute-start | bytes 2408456 | tf_op jit(solution)/shard_map/ppermute | solution.py:45
  140.7 31.3 %collective-permute-start.88 = (bf16[448,896]{1,0:T(8,128)(2,1)S(1)}, bf16[448,896]{1,0:T(8,128)(2,1)}, u32[]{:S(2)}, u32[]{:S(2)}) collective-permute-start(bf16[448,896]{1,0:T(8,128)(2,1)S(1)} %join.3.marked_ref.refs_5_), channel_id=1, source_target_pairs={{0,16},{8,24},{16,0},{24,8},{1,17},{9,25},{17,1},{25,9},{2,18},{10... | collective-permute-start | bytes 2408456 | tf_op jit(solution)/shard_map/ppermute | solution.py:45
  174.9 27.2 %collective-permute-start.55 = (bf16[197,384]{1,0:T(8,128)(2,1)S(1)}, bf16[197,384]{1,0:T(8,128)(2,1)S(1)}, u32[]{:S(2)}, u32[]{:S(2)}) collective-permute-start(bf16[197,384]{1,0:T(8,128)(2,1)S(1)} %get-tuple-element.169), channel_id=1, source_target_pairs={{0,1},{1,0},{2,3},{3,2},{4,5},{5,4},{6,7},{7,6},{8,9},{9,8},{10,11... | collective-permute-start | bytes 453896 | tf_op jit(solution)/shard_map/ppermute | solution.py:45
  178.3 33.4 %collective-permute-start.83 = (bf16[448,768]{1,0:T(8,128)(2,1)S(1)}, bf16[448,768]{1,0:T(8,128)(2,1)S(1)}, u32[]{:S(2)}, u32[]{:S(2)}) collective-permute-start(bf16[448,768]{1,0:T(8,128)(2,1)S(1)} %join.2.rows_ref.refs_0_), channel_id=1, source_target_pairs={{0,8},{8,0},{16,24},{24,16},{1,9},{9,1},{17,25},{25,17},{2,10},{10... | collective-permute-start | bytes 2064392 | tf_op jit(solution)/shard_map/ppermute | solution.py:45
  180.0 19.7 %collective-permute-start.48 = (bf16[96,768]{1,0:T(8,128)(2,1)S(1)}, bf16[96,768]{1,0:T(8,128)(2,1)S(1)}, u32[]{:S(2)}, u32[]{:S(2)}) collective-permute-start(bf16[96,768]{1,0:T(8,128)(2,1)S(1)} %get-tuple-element.136), channel_id=1, source_target_pairs={{0,24},{8,16},{16,8},{24,0},{1,25},{9,17},{17,9},{25,1},{2,26},{10... | collective-permute-start | bytes 442376 | tf_op jit(solution)/shard_map/ppermute | solution.py:45
  181.5 19.8 %collective-permute-start.47 = (bf16[96,768]{1,0:T(8,128)(2,1)S(1)}, bf16[96,768]{1,0:T(8,128)(2,1)S(1)}, u32[]{:S(2)}, u32[]{:S(2)}) collective-permute-start(bf16[96,768]{1,0:T(8,128)(2,1)S(1)} %get-tuple-element.135), channel_id=1, source_target_pairs={{0,16},{8,24},{16,0},{24,8},{1,17},{9,25},{17,1},{25,9},{2,18},{10... | collective-permute-start | bytes 442376 | tf_op jit(solution)/shard_map/ppermute | solution.py:45
  183.0 19.1 %collective-permute-start.46 = (bf16[96,768]{1,0:T(8,128)(2,1)S(1)}, bf16[96,768]{1,0:T(8,128)(2,1)S(1)}, u32[]{:S(2)}, u32[]{:S(2)}) collective-permute-start(bf16[96,768]{1,0:T(8,128)(2,1)S(1)} %get-tuple-element.134), channel_id=1, source_target_pairs={{0,8},{8,0},{16,24},{24,16},{1,9},{9,1},{17,25},{25,17},{2,10},{10... | collective-permute-start | bytes 442376 | tf_op jit(solution)/shard_map/ppermute | solution.py:45
  199.7 23.1 %collective-permute-start.84 = (bf16[448,768]{1,0:T(8,128)(2,1)S(1)}, bf16[448,768]{1,0:T(8,128)(2,1)S(1)}, u32[]{:S(2)}, u32[]{:S(2)}) collective-permute-start(bf16[448,768]{1,0:T(8,128)(2,1)S(1)} %join.2.rows_ref.refs_0_), channel_id=1, source_target_pairs={{0,16},{8,24},{16,0},{24,8},{1,17},{9,25},{17,1},{25,9},{2,18},{10... | collective-permute-start | bytes 2064392 | tf_op jit(solution)/shard_map/ppermute | solution.py:45
  208.2 15.2 %collective-permute-start.69 = (bf16[96,1152]{1,0:T(8,128)(2,1)S(1)}, bf16[96,1152]{1,0:T(8,128)(2,1)S(1)}, u32[]{:S(2)}, u32[]{:S(2)}) collective-permute-start(bf16[96,1152]{1,0:T(8,128)(2,1)S(1)} %get-tuple-element.145), channel_id=1, source_target_pairs={{0,24},{8,16},{16,8},{24,0},{1,25},{9,17},{17,9},{25,1},{2,26},{10... | collective-permute-start | bytes 663560 | tf_op jit(solution)/shard_map/ppermute | solution.py:45
  209.6 20.3 %collective-permute-start.68 = (bf16[96,1152]{1,0:T(8,128)(2,1)S(1)}, bf16[96,1152]{1,0:T(8,128)(2,1)S(1)}, u32[]{:S(2)}, u32[]{:S(2)}) collective-permute-start(bf16[96,1152]{1,0:T(8,128)(2,1)S(1)} %get-tuple-element.144), channel_id=1, source_target_pairs={{0,16},{8,24},{16,0},{24,8},{1,17},{9,25},{17,1},{25,9},{2,18},{10... | collective-permute-start | bytes 663560 | tf_op jit(solution)/shard_map/ppermute | solution.py:45
  210.2 21.3 %collective-permute-start.67 = (bf16[96,1152]{1,0:T(8,128)(2,1)S(1)}, bf16[96,1152]{1,0:T(8,128)(2,1)S(1)}, u32[]{:S(2)}, u32[]{:S(2)}) collective-permute-start(bf16[96,1152]{1,0:T(8,128)(2,1)S(1)} %get-tuple-element.143), channel_id=1, source_target_pairs={{0,8},{8,0},{16,24},{24,16},{1,9},{9,1},{17,25},{25,17},{2,10},{10... | collective-permute-start | bytes 663560 | tf_op jit(solution)/shard_map/ppermute | solution.py:45
  211.7 45.6 %collective-permute-start.89 = (bf16[224,896]{1,0:T(8,128)(2,1)S(1)}, bf16[224,896]{1,0:T(8,128)(2,1)S(1)}, u32[]{:S(2)}, u32[]{:S(2)}) collective-permute-start(bf16[224,896]{1,0:T(8,128)(2,1)S(1)} %slice.219), channel_id=1, source_target_pairs={{0,16},{8,24},{16,0},{24,8},{1,17},{9,25},{17,1},{25,9},{2,18},{10... | collective-permute-start | bytes 1204232 | tf_op jit(solution)/shard_map/ppermute | solution.py:45
  222.8 34.9 %collective-permute-start.90 = (bf16[224,896]{1,0:T(8,128)(2,1)S(1)}, bf16[224,896]{1,0:T(8,128)(2,1)S(1)}, u32[]{:S(2)}, u32[]{:S(2)}) collective-permute-start(bf16[224,896]{1,0:T(8,128)(2,1)S(1)} %slice.220), channel_id=1, source_target_pairs={{0,8},{8,0},{16,24},{24,16},{1,9},{9,1},{17,25},{25,17},{2,10},{10... | collective-permute-start | bytes 1204232 | tf_op jit(solution)/shard_map/ppermute | solution.py:45
  252.0 30.0 %collective-permute-start.54 = (bf16[24,768]{1,0:T(8,128)(2,1)S(1)}, bf16[24,768]{1,0:T(8,128)(2,1)S(1)}, u32[]{:S(2)}, u32[]{:S(2)}) collective-permute-start(bf16[24,768]{1,0:T(8,128)(2,1)S(1)} %fusion.37), channel_id=1, source_target_pairs={{0,6},{1,7},{2,4},{3,5},{4,2},{5,3},{6,0},{7,1},{8,14},{9,15},{10,... | collective-permute-start | bytes 110600 | tf_op jit(solution)/shard_map/ppermute | solution.py:45
  257.4 27.1 %collective-permute-start.53 = (bf16[24,768]{1,0:T(8,128)(2,1)S(1)}, bf16[24,768]{1,0:T(8,128)(2,1)S(1)}, u32[]{:S(2)}, u32[]{:S(2)}) collective-permute-start(bf16[24,768]{1,0:T(8,128)(2,1)S(1)} %fusion.37), channel_id=1, source_target_pairs={{0,4},{1,5},{2,6},{3,7},{4,0},{5,1},{6,2},{7,3},{8,12},{9,13},{10,... | collective-permute-start | bytes 110600 | tf_op jit(solution)/shard_map/ppermute | solution.py:45
  257.7 28.7 %collective-permute-start.52 = (bf16[24,768]{1,0:T(8,128)(2,1)S(1)}, bf16[24,768]{1,0:T(8,128)(2,1)S(1)}, u32[]{:S(2)}, u32[]{:S(2)}) collective-permute-start(bf16[24,768]{1,0:T(8,128)(2,1)S(1)} %fusion.37), channel_id=1, source_target_pairs={{0,2},{1,3},{2,0},{3,1},{4,6},{5,7},{6,4},{7,5},{8,10},{9,11},{10,... | collective-permute-start | bytes 110600 | tf_op jit(solution)/shard_map/ppermute | solution.py:45
  262.9 23.5 %collective-permute-start.75 = (bf16[24,1152]{1,0:T(8,128)(2,1)S(1)}, bf16[24,1152]{1,0:T(8,128)(2,1)S(1)}, u32[]{:S(2)}, u32[]{:S(2)}) collective-permute-start(bf16[24,1152]{1,0:T(8,128)(2,1)S(1)} %fusion.30), channel_id=1, source_target_pairs={{0,6},{1,7},{2,4},{3,5},{4,2},{5,3},{6,0},{7,1},{8,14},{9,15},{10,... | collective-permute-start | bytes 165896 | tf_op jit(solution)/shard_map/ppermute | solution.py:45
  264.8 24.2 %collective-permute-start.74 = (bf16[24,1152]{1,0:T(8,128)(2,1)S(1)}, bf16[24,1152]{1,0:T(8,128)(2,1)S(1)}, u32[]{:S(2)}, u32[]{:S(2)}) collective-permute-start(bf16[24,1152]{1,0:T(8,128)(2,1)S(1)} %fusion.30), channel_id=1, source_target_pairs={{0,4},{1,5},{2,6},{3,7},{4,0},{5,1},{6,2},{7,3},{8,12},{9,13},{10,... | collective-permute-start | bytes 165896 | tf_op jit(solution)/shard_map/ppermute | solution.py:45
  (131 other events, 1112.0 us)

commit v3 on v2

v3 whole, which is shorter than its diff:
```python
import functools
import math

import jax
import jax.numpy as jnp
from jax import lax
from jax.experimental import pallas as pl
from jax.experimental.pallas import tpu as pltpu
from jax.sharding import PartitionSpec as P

HEAD_DIM = 64
SEQ = 197


NORM_EPS = 1e-06
SQRT_HALF = 0.7071067811865476
INV_ROOT_TWO_PI = 0.3989422804014327


def normalize(values):
    center = values - jnp.mean(values, axis=-1, keepdims=True)
    inv_std = lax.rsqrt(jnp.mean(center * center, axis=-1, keepdims=True) + NORM_EPS)
    return (center * inv_std, inv_std)


def norm_back(grad_in, normed, inv_std, gain_vec):
    scaled = grad_in * gain_vec
    mean_plain = jnp.mean(scaled, axis=-1, keepdims=True)
    mean_mixed = jnp.mean(scaled * normed, axis=-1, keepdims=True)
    return inv_std * (scaled - mean_plain - normed * mean_mixed)


def gelu_value(pre_act):
    return 0.5 * pre_act * (1.0 + lax.erf(pre_act * SQRT_HALF))


def gelu_slope(pre_act):
    return 0.5 * (1.0 + lax.erf(pre_act * SQRT_HALF)) + pre_act * INV_ROOT_TWO_PI * jnp.exp(
        -0.5 * pre_act * pre_act
    )


def swap(values, axis, mask):
    size = lax.axis_size(axis)
    return lax.ppermute(values, axis, [(index, index ^ mask) for index in range(size)])


def gather_shared(shard, mine):
    groups = lax.axis_size("dp")
    rows = shard.shape[0]
    if groups != 4:
        return [lax.all_gather(shard, "dp", axis=0, tiled=True)], [jnp.int32(0)]
    me = lax.axis_index("dp")
    core = lax.axis_index("expert") % 2
    half = rows // 2
    part = half // 2
    from_one = swap(mine, "dp", 1)
    from_two = swap(mine, "dp", 2)
    far_low = swap(from_one[:part], "dp", 2)
    far_high = swap(from_two[part:], "dp", 1)
    other_one = swap(from_one, "expert", 1)
    other_two = swap(from_two, "expert", 1)
    other_low = swap(far_low, "expert", 1)
    other_high = swap(far_high, "expert", 1)
    base = core * half
    other = half - base
    one, two, far = (me ^ 1) * rows, (me ^ 2) * rows, (me ^ 3) * rows
    starts = [me * rows, one + base, two + base, far + base, far + base + part]
    starts += [one + other, two + other, far + other, far + other + part]
    pieces = [shard, from_one, from_two, far_low, far_high]
    pieces += [other_one, other_two, other_low, other_high]
    return pieces, starts


def after(values, *marks):
    return lax.optimization_barrier((values, marks))[0]


def gather_rows(rows, first_mark, second_mark):
    groups = lax.axis_size("dp")
    rows_later = after(rows, first_mark)
    if groups != 4:
        return [rows] + [swap(rows_later, "dp", mask) for mask in range(1, groups)]
    half = rows.shape[0] // 2
    from_one = swap(rows_later, "dp", 1)
    from_two = swap(rows_later, "dp", 2)
    one, two = after((from_one, from_two), second_mark)
    return [rows, one, two, swap(one[:half], "dp", 2), swap(two[half:], "dp", 1)]


def exchange(blocks):
    return [blocks[0]] + [swap(blocks[mask], "expert", mask) for mask in range(1, len(blocks))]


def in_order(pieces, me, axis):
    stack = jnp.stack(pieces)
    return jnp.concatenate(
        [
            lax.dynamic_index_in_dim(stack, me ^ index, 0, keepdims=False)
            for index in range(len(pieces))
        ],
        axis=axis,
    )


VMEM = pl.BlockSpec(memory_space=pltpu.VMEM)
SMEM = pl.BlockSpec(memory_space=pltpu.SMEM)
NARROW = jnp.bfloat16
WIDE = jnp.float32
MIB = 1024 * 1024


def like(shape, dtype):
    return jax.ShapeDtypeStruct(shape, dtype)


def run(body, outs, operands, flops, moved, mib, scalars=0, scratch=(), name=None):
    return pl.pallas_call(
        body,
        out_shape=outs,
        in_specs=[SMEM] * scalars + [VMEM] * (len(operands) - scalars),
        out_specs=jax.tree.map(lambda _: VMEM, outs),
        scratch_shapes=list(scratch),
        compiler_params=pltpu.CompilerParams(vmem_limit_bytes=mib * MIB),
        cost_estimate=pl.CostEstimate(flops=1, bytes_accessed=1, transcendentals=0),
        name=name,
    )(*operands)


def mm(left, right):
    return jnp.dot(left, right, preferred_element_type=WIDE)


def mm_rows(left, right):
    return lax.dot_general(left, right, (((1,), (1,)), ((), ())), preferred_element_type=WIDE)


def mm_cols(left, right):
    return lax.dot_general(left, right, (((0,), (0,)), ((), ())), preferred_element_type=WIDE)


def head_masks(rows):
    lanes = lax.broadcasted_iota(jnp.int32, (rows, 2 * HEAD_DIM), 1)
    return [lanes < HEAD_DIM, lanes >= HEAD_DIM]


def join_body(count, *refs):
    out_ref, wide_ref = refs[count], refs[count + 1]
    at = 0
    for ref in refs[:count]:
        wide_ref[at : at + ref.shape[0], :] = ref[...].astype(WIDE)
        at += ref.shape[0]
    out_ref[...] = wide_ref[...].astype(NARROW)


def join(pieces):
    rows = sum(piece.shape[0] for piece in pieces)
    columns = pieces[0].shape[1]
    return run(
        functools.partial(join_body, len(pieces)),
        like((rows, columns), NARROW),
        pieces,
        rows * columns,
        4 * rows * columns,
        16,
        scratch=[pltpu.VMEM((rows, columns), WIDE)],
        name="join",
    )


def slot_rows(targets, total, tokens):
    ids = lax.broadcasted_iota(jnp.int32, (total, tokens), 0)
    return ids == targets[0:1, :], ids == targets[1:2, :]


def grad_slots_body(experts, d_ref, routes_ref, targets_ref, out_ref):
    tokens, width = d_ref.shape
    slots = out_ref.shape[1]
    first, second = slot_rows(targets_ref[...], experts * slots, tokens)
    first, second = first.astype(NARROW), second.astype(NARROW)
    rows = mm(first + second, d_ref[...]).astype(NARROW)
    lanes = lax.broadcasted_iota(jnp.int32, (tokens, 128), 1)
    other_first = (lanes == routes_ref[:, 1:2]).astype(NARROW)
    other_second = (lanes == routes_ref[:, 0:1]).astype(NARROW)
    marks = (mm(first, other_first) + mm(second, other_second)).astype(NARROW)
    for index in range(experts):
        out_ref[index, :, :width] = rows[index * slots : (index + 1) * slots, :]
        out_ref[index, :, width:] = marks[index * slots : (index + 1) * slots, :]


def order_body(me_ref, blocks_ref, out_ref, wide_ref):
    experts, slots, _ = blocks_ref.shape
    for index in range(experts):
        at = index * slots
        wide_ref[at : at + slots, :] = blocks_ref[me_ref[0] ^ index].astype(WIDE)
    out_ref[...] = wide_ref[...].astype(NARROW)


def attend_body(count, *refs):
    starts_ref, x_ref, columns_ref = refs[0], refs[1], refs[2]
    pieces = refs[3 : 3 + count]
    full_ref, proj_ref, vec_ref, qkv_ref, ctx_ref, lse_ref, keep_ref, give_ref = refs[
        3 + count : 11 + count
    ]
    side_ref = refs[11 + count]
    tokens, width = x_ref.shape
    for index, piece in enumerate(pieces):
        rows = piece.shape[0]
        at = starts_ref[index] if count > 1 else 0
        if count > 1:
            at = pl.multiple_of(at, 16)
        full_ref[pl.ds(at, rows), :] = piece[:, : 3 * width]
        proj_ref[pl.ds(at, rows), :] = piece[:, 3 * width : 4 * width]
        side_ref[pl.ds(at, rows), :] = piece[:, 4 * width :]
    side = jnp.transpose(side_ref[...].astype(WIDE))
    vec_ref[...] = side[: vec_ref.shape[0], :]
    bias_q, bias_v = vec_ref[0:1, :], vec_ref[1:2, :]
    gain, bias = vec_ref[3:4, :], vec_ref[4:5, :]
    normed, _ = normalize(x_ref[...].astype(WIDE))
    a_in = (normed * gain + bias).astype(NARROW)
    qkv_ref[:, :width] = (mm(a_in, full_ref[:, :width]) + bias_q).astype(NARROW)
    qkv_ref[:, width : 2 * width] = mm(a_in, full_ref[:, width : 2 * width]).astype(NARROW)
    qkv_ref[:, 2 * width :] = (
        mm(a_in, full_ref[:, 2 * width : 3 * width]) + bias_v
    ).astype(NARROW)
    masks = head_masks(tokens)
    lanes = lax.broadcasted_iota(jnp.int32, (tokens, 128), 1)
    lse_all = jnp.zeros((tokens, 128), WIDE)
    pair = 2 * HEAD_DIM
    for group in range(width // pair):
        at = group * pair
        query = qkv_ref[:, at : at + pair]
        keys = qkv_ref[:, width + at : width + at + pair]
        values = qkv_ref[:, 2 * width + at : 2 * width + at + pair]
        outs = []
        for index in range(2):
            scores = mm_rows(jnp.where(masks[index], query, 0), keys) * (
                1.0 / math.sqrt(HEAD_DIM)
            )
            top = jnp.max(scores, axis=-1, keepdims=True)
            exps = jnp.exp(scores - top)
            total = jnp.sum(exps, axis=-1, keepdims=True)
            lse_all = jnp.where(lanes == 2 * group + index, top + jnp.log(total), lse_all)
            outs.append(mm((exps / total).astype(NARROW), values))
        ctx_ref[:, at : at + pair] = jnp.where(masks[0], outs[0], outs[1]).astype(NARROW)
    lse_ref[...] = lse_all
    ids = lax.broadcasted_iota(jnp.int32, (width, columns_ref.shape[1]), 0)
    hot = (ids == columns_ref[0:1, :]).astype(NARROW)
    half = width // 2
    chosen = mm(a_in, hot).astype(NARROW)
    keep_ref[:, :half] = chosen[:, :half]
    give_ref[:, :half] = chosen[:, half:]
    chosen = mm(ctx_ref[...], hot).astype(NARROW)
    keep_ref[:, half:] = chosen[:, :half]
    give_ref[:, half:] = chosen[:, half:]


def middle_body(experts, ctx_ref, x_ref, vec_ref, targets_ref, full_ref, hidden_ref, y_ref, *outs):
    hidden = x_ref[...].astype(WIDE) + mm(ctx_ref[...], full_ref[...]) + vec_ref[2:3, :]
    hidden_ref[...] = hidden
    normed, _ = normalize(hidden)
    y_in = (normed * vec_ref[5:6, :] + vec_ref[6:7, :]).astype(NARROW)
    y_ref[...] = y_in
    slots = outs[0].shape[0]
    first, second = slot_rows(targets_ref[...], experts * slots, x_ref.shape[0])
    rows = mm((first | second).astype(NARROW), y_in).astype(NARROW)
    for index, out in enumerate(outs):
        out[...] = rows[index * slots : (index + 1) * slots, :]


def in_terms(values):
    high = values.astype(NARROW)
    rest = values - high.astype(WIDE)
    middle = rest.astype(NARROW)
    return high, middle, (rest - middle.astype(WIDE)).astype(NARROW)


def slot_gates(rows, marks, router, mine):
    logits = mm_rows(rows, router)
    lanes = lax.broadcasted_iota(jnp.int32, logits.shape, 1)
    own = jnp.sum(jnp.where(lanes == mine, logits, 0.0), axis=-1, keepdims=True)
    other = jnp.sum(
        marks[:, : logits.shape[1]].astype(WIDE) * logits, axis=-1, keepdims=True
    )
    return 1.0 / (1.0 + jnp.exp(other - own))


def gelu_parts(pre_act):
    half = 0.5 * (1.0 + lax.erf(pre_act * SQRT_HALF))
    slope = half + pre_act * INV_ROOT_TWO_PI * jnp.exp(-0.5 * pre_act * pre_act)
    return pre_act * half, slope


def expert_body(experts, spare, me_ref, rows_ref, marked_ref, vec_ref, in_ref, bin_ref, out_ref, bout_ref, *refs):
    fresh_ref = refs[0]
    back_ref, sent_ref, acc_ref, dacc_ref = refs[1:]
    step = pl.program_id(0)
    width = rows_ref.shape[1]

    @pl.when(step == 0)
    def _():
        router = vec_ref[8:32, :].astype(NARROW)
        gate = slot_gates(rows_ref[...], marked_ref[:, width:], router, me_ref[0])
        sent_ref[...] = (gate * marked_ref[:, :width].astype(WIDE)).astype(NARROW)
        acc_ref[...] = jnp.zeros_like(acc_ref)
        dacc_ref[...] = jnp.zeros_like(dacc_ref)

    weight_in, weight_out = in_ref[...], out_ref[...]
    pre_act = mm(rows_ref[...], weight_in) + bin_ref[...].astype(WIDE)
    act, slope = gelu_parts(pre_act)
    acc_ref[...] += mm(act.astype(NARROW), weight_out)
    d_pre = mm_rows(sent_ref[...], weight_out) * slope
    dacc_ref[...] += mm_rows(d_pre.astype(NARROW), weight_in)

    @pl.when(step == pl.num_programs(0) - 1)
    def _():
        bias = bout_ref[...].astype(WIDE)
        slots = back_ref.shape[1]
        lanes = lax.broadcasted_iota(jnp.int32, (slots, 128), 1)
        lines = lax.broadcasted_iota(jnp.int32, (slots, 128), 0)
        line_hot = (lanes == lines).astype(NARROW)
        spare_hot = ((lines == lanes + spare) & (lanes < 3)).astype(NARROW)
        grads = marked_ref[:, :width].astype(WIDE)
        fresh_all = (acc_ref[...] + bias).astype(NARROW).astype(WIDE)
        acc_ref[...] = fresh_all
        terms = [
            term.astype(WIDE)
            for term in in_terms(jnp.sum(grads * fresh_all, axis=-1, keepdims=True))
        ]
        for index in range(experts):
            at = index * slots
            fresh_ref[me_ref[0] ^ index] = acc_ref[at : at + slots, :].astype(NARROW)
            mine = jnp.zeros((slots, 128), WIDE)
            for place, term in enumerate(terms):
                mine = jnp.where(lanes == place, term[at : at + slots, :], mine)
            packed = mm(spare_hot, mm_cols(mine.astype(NARROW), line_hot).astype(NARROW))
            back_ref[me_ref[0] ^ index, :, :128] = (dacc_ref[at : at + slots, :128] + packed).astype(NARROW)
            back_ref[me_ref[0] ^ index, :, 128:] = dacc_ref[at : at + slots, 128:].astype(
                NARROW
            )


def expert(me, rows, marked, vec, weight_in, b_in, weight_out, b_out, experts, slots, spare, chunk):
    total, width = rows.shape
    hidden_units = weight_in.shape[1]
    whole = lambda array: pl.BlockSpec(array.shape, lambda step: (0, 0))
    block = like((experts, slots, width), NARROW)
    return pl.pallas_call(
        functools.partial(expert_body, experts, spare),
        grid=(hidden_units // chunk,),
        out_shape=[block, block],
        in_specs=[
            SMEM,
            whole(rows),
            whole(marked),
            whole(vec),
            pl.BlockSpec((width, chunk), lambda step: (0, step)),
            pl.BlockSpec((1, chunk), lambda step: (0, step)),
            pl.BlockSpec((chunk, width), lambda step: (step, 0)),
            whole(b_out),
        ],
        out_specs=[pl.BlockSpec((experts, slots, width), lambda step: (0, 0, 0))] * 2,
        scratch_shapes=[
            pltpu.VMEM((total, width), NARROW),
            pltpu.VMEM((total, width), WIDE),
            pltpu.VMEM((total, width), WIDE),
        ],
        compiler_params=pltpu.CompilerParams(vmem_limit_bytes=58 * MIB),
        cost_estimate=pl.CostEstimate(flops=1, bytes_accessed=1, transcendentals=0),
        name="expert",
    )(me, rows, marked, vec, weight_in, b_in, weight_out, b_out)


def weights_body(count, me_ref, vec_ref, in_ref, bin_ref, out_ref, *refs):
    rows_in, marked_in = refs[:count], refs[count : 2 * count]
    dout_ref, own_ref = refs[2 * count : 2 * count + 2]
    others = refs[2 * count + 2 : -5]
    dbin_ref, dbout_ref, rows_ref, sent_ref, din_ref = refs[-5:]
    width = in_ref.shape[0]

    @pl.when(pl.program_id(0) == 0)
    def _():
        router = vec_ref[8:32, :].astype(NARROW)
        at = 0
        total = jnp.zeros((1, width), WIDE)
        for rows, marked in zip(rows_in, marked_in):
            size = rows.shape[0]
            gate = slot_gates(rows[...], marked[:, width:], router, me_ref[0])
            sent = (gate * marked[:, :width].astype(WIDE)).astype(NARROW)
            rows_ref[at : at + size, :] = rows[...]
            sent_ref[at : at + size, :] = sent
            total += jnp.sum(sent.astype(WIDE), axis=0, keepdims=True)
            at += size
        dbout_ref[...] = total

    pre_act = mm(rows_ref[...], in_ref[...]) + bin_ref[...].astype(WIDE)
    act, slope = gelu_parts(pre_act)
    dout_ref[...] = mm_cols(act.astype(NARROW), sent_ref[...])
    d_pre = mm_rows(sent_ref[...], out_ref[...]) * slope
    dbin_ref[...] = jnp.sum(d_pre, axis=0, keepdims=True)
    din_ref[...] = mm_cols(rows_ref[...], d_pre.astype(NARROW))
    share = own_ref.shape[0]
    for mask, out in enumerate((own_ref,) + others):
        at = pl.multiple_of((me_ref[1] ^ mask) * share, 8)
        out[...] = din_ref[pl.ds(at, share), :].astype(out.dtype)


def expert_weights(me, vec, my_in, my_bias, my_out, rows, marked, groups, chunk):
    count = len(rows)
    width, units = my_in.shape
    share = width // groups
    total = sum(piece.shape[0] for piece in rows)
    whole = lambda array: pl.BlockSpec(array.shape, lambda step: (0, 0))
    return pl.pallas_call(
        functools.partial(weights_body, count),
        grid=(units // chunk,),
        out_shape=[
            like((units, width), WIDE),
            like((share, units), WIDE),
        ]
        + [like((share, units), NARROW)] * (groups - 1)
        + [
            like((1, units), WIDE),
            like((1, width), WIDE),
        ],
        in_specs=[
            SMEM,
            whole(vec),
            pl.BlockSpec((width, chunk), lambda step: (0, step)),
            pl.BlockSpec((1, chunk), lambda step: (0, step)),
            pl.BlockSpec((chunk, width), lambda step: (step, 0)),
        ]
        + [whole(piece) for piece in rows + marked],
        out_specs=[
            pl.BlockSpec((chunk, width), lambda step: (step, 0)),
        ]
        + [pl.BlockSpec((share, chunk), lambda step: (0, step))] * groups
        + [
            pl.BlockSpec((1, chunk), lambda step: (0, step)),
            pl.BlockSpec((1, width), lambda step: (0, 0)),
        ],
        scratch_shapes=[
            pltpu.VMEM((total, width), NARROW),
            pltpu.VMEM((total, width), NARROW),
            pltpu.VMEM((width, chunk), WIDE),
        ],
        compiler_params=pltpu.CompilerParams(vmem_limit_bytes=58 * MIB),
        cost_estimate=pl.CostEstimate(flops=1, bytes_accessed=1, transcendentals=0),
        name="expert_weights",
    )(me, vec, my_in, my_bias, my_out, *rows, *marked)


def combine_body(experts, spare, *refs):
    hidden_ref, y_ref, d_ref, vec_ref, full_ref, routes_ref, slot_ref, targets_ref = refs[:8]
    back_ref, gate_ref, dh_ref, dctx_ref, sums_ref, dret_ref = refs[8:]
    tokens, width = hidden_ref.shape
    slots = back_ref.shape[1]
    for index in range(experts):
        at = index * slots
        dret_ref[at : at + slots, :] = back_ref[index].astype(WIDE)
    d_returned = dret_ref[...].astype(NARROW)
    lanes = lax.broadcasted_iota(jnp.int32, (tokens, experts * slots), 1)
    places = lax.broadcasted_iota(jnp.int32, (tokens, 128), 1)
    d_gates = []
    for choice in range(2):
        target = targets_ref[:, choice : choice + 1]
        slot = slot_ref[:, choice : choice + 1]
        line = jnp.where(target < 0, -8, target - slot + spare)
        found = None
        for term in range(3):
            hot = (lanes == line + term).astype(NARROW)
            new = mm(hot, d_returned[:, :128])
            found = new if found is None else found + new
        d_gates.append(
            jnp.sum(jnp.where(places == slot, found, 0.0), axis=-1, keepdims=True)
        )
    router = vec_ref[8:32, :].astype(NARROW)
    y_in = y_ref[...]
    logits = mm_rows(y_in, router)
    names = lax.broadcasted_iota(jnp.int32, logits.shape, 1)
    hot_first = (names == routes_ref[:, 0:1]).astype(WIDE)
    hot_second = (names == routes_ref[:, 1:2]).astype(WIDE)
    chosen_first = jnp.sum(logits * hot_first, axis=-1, keepdims=True)
    chosen_second = jnp.sum(logits * hot_second, axis=-1, keepdims=True)
    gate_first = 1.0 / (1.0 + jnp.exp(chosen_second - chosen_first))
    gate_second = 1.0 - gate_first
    gate_ref[...] = jnp.broadcast_to(gate_first, gate_ref.shape)
    grad = d_ref[...].astype(WIDE)
    d_diff = (d_gates[0] - d_gates[1]) * gate_first * gate_second
    d_logits = (d_diff * (hot_first - hot_second)).astype(NARROW)
    sums_ref[8:32, :] = mm_cols(d_logits, y_in)
    hot = ((lanes == targets_ref[:, 0:1]) | (lanes == targets_ref[:, 1:2])).astype(NARROW)
    d_y = mm(hot, d_returned) + mm(d_logits, router)
    normed, inv_std = normalize(hidden_ref[...])
    d_hidden = grad + norm_back(d_y, normed, inv_std, vec_ref[5:6, :])
    sums_ref[0:8, :] = jnp.zeros((8, width), WIDE)
    sums_ref[0:1, :] = jnp.sum(d_hidden, axis=0, keepdims=True)
    sums_ref[1:2, :] = jnp.sum(d_y * normed, axis=0, keepdims=True)
    sums_ref[2:3, :] = jnp.sum(d_y, axis=0, keepdims=True)
    dh_ref[...] = d_hidden
    dctx_ref[...] = mm_rows(d_hidden.astype(NARROW), full_ref[...]).astype(NARROW)


def output_body(hidden_ref, gate_ref, targets_ref, fresh_ref, out_ref, ret_ref):
    tokens = hidden_ref.shape[0]
    experts, slots, _ = fresh_ref.shape
    for index in range(experts):
        at = index * slots
        ret_ref[at : at + slots, :] = fresh_ref[index].astype(WIDE)
    returned = ret_ref[...].astype(NARROW)
    lanes = lax.broadcasted_iota(jnp.int32, (tokens, experts * slots), 1)
    first = mm((lanes == targets_ref[:, 0:1]).astype(NARROW), returned)
    second = mm((lanes == targets_ref[:, 1:2]).astype(NARROW), returned)
    gate = gate_ref[:, 0:1]
    out_ref[...] = (hidden_ref[...] + (gate * first + (1.0 - gate) * second)).astype(NARROW)


def back_body(qkv_ref, dctx_ref, lse_ref, full_ref, x_ref, vec_ref, dh_ref, early_ref, dx_ref, out_ref):
    tokens, width = dctx_ref.shape
    masks = head_masks(tokens)
    lanes = lax.broadcasted_iota(jnp.int32, (tokens, 128), 1)
    pair = 2 * HEAD_DIM
    scale = 1.0 / math.sqrt(HEAD_DIM)
    out_ref[tokens:, :] = jnp.zeros((out_ref.shape[0] - tokens, out_ref.shape[1]), NARROW)
    out_ref[:tokens, :width] = dh_ref[...].astype(NARROW)
    sums_q, sums_v = [], []
    for group in range(width // pair):
        at = group * pair
        query = qkv_ref[:, at : at + pair]
        keys = qkv_ref[:, width + at : width + at + pair]
        values = qkv_ref[:, 2 * width + at : 2 * width + at + pair]
        grads = dctx_ref[:, at : at + pair]
        d_query = d_keys = d_values = None
        for index in range(2):
            zero = jnp.zeros_like(query)
            query_h = jnp.where(masks[index], query, zero)
            keys_h = jnp.where(masks[index], keys, zero)
            grads_h = jnp.where(masks[index], grads, zero)
            head = 2 * group + index
            lse = jnp.sum(jnp.where(lanes == head, lse_ref[...], 0.0), axis=-1, keepdims=True)
            probs = jnp.exp(mm_rows(query_h, keys) * scale - lse)
            d_probs = mm_rows(grads_h, values)
            delta = jnp.sum(probs * d_probs, axis=-1, keepdims=True)
            d_scores = (probs * (d_probs - delta) * scale).astype(NARROW)
            new_values = mm_cols(probs.astype(NARROW), grads_h)
            new_query = mm(d_scores, keys_h)
            new_keys = mm_cols(d_scores, query_h)
            d_values = new_values if d_values is None else d_values + new_values
            d_query = new_query if d_query is None else d_query + new_query
            d_keys = new_keys if d_keys is None else d_keys + new_keys
        out_ref[:tokens, width + at : width + at + pair] = d_query.astype(NARROW)
        out_ref[:tokens, 2 * width + at : 2 * width + at + pair] = d_keys.astype(NARROW)
        out_ref[:tokens, 3 * width + at : 3 * width + at + pair] = d_values.astype(NARROW)
        sums_q.append(jnp.sum(d_query, axis=0, keepdims=True))
        sums_v.append(jnp.sum(d_values, axis=0, keepdims=True))
    d_a = mm_rows(out_ref[:tokens, width:], full_ref[...])
    normed, inv_std = normalize(x_ref[...].astype(WIDE))
    dx_ref[...] = dh_ref[...] + norm_back(d_a, normed, inv_std, vec_ref[3:4, :])
    rows = lax.broadcasted_iota(jnp.int32, (32, width), 0)
    sums = early_ref[...]
    new_rows = (
        jnp.concatenate(sums_q, axis=1),
        jnp.concatenate(sums_v, axis=1),
        jnp.sum(d_a * normed, axis=0, keepdims=True),
        jnp.sum(d_a, axis=0, keepdims=True),
    )
    for place, new in enumerate(new_rows, 3):
        sums = jnp.where(rows == place, new, sums)
    base = out_ref.shape[0] - 32
    for place, term in enumerate(in_terms(sums)):
        out_ref[base:, place * width : (place + 1) * width] = term


def outer_body(groups, columns_ref, keep_ref, other_ref, own_d_ref, other_d_ref, own_ref, *refs):
    outs, turned_ref = refs[:-1], refs[-1]
    tokens = keep_ref.shape[0]
    width = keep_ref.shape[1]
    half = width // 2
    rows = own_ref.shape[0]
    base = own_d_ref.shape[0] - 32
    sums = jnp.zeros((32, width), WIDE)
    for ref in (own_d_ref, other_d_ref):
        mine = ref[base:, :width].astype(WIDE) + ref[base:, width : 2 * width].astype(WIDE)
        sums = sums + (mine + ref[base:, 2 * width : 3 * width].astype(WIDE))
    turned_ref[...] = jnp.zeros_like(turned_ref)
    turned_ref[0:32, :] = sums
    turned = jnp.transpose(turned_ref[...]).astype(NARROW)
    ids = lax.broadcasted_iota(jnp.int32, (width, half), 0)
    hot = (ids == columns_ref[0:1, :half]).astype(NARROW)
    blocks = (
        (0, width, half),
        (width, 4 * width, 0),
        (4 * width, 4 * width + 128, None),
    )
    for low, high, left in blocks:
        if left is None:
            total = mm_cols(hot, turned)
        else:
            total = mm_cols(keep_ref[:, left : left + half], own_d_ref[:tokens, low:high])
            total = total + mm_cols(
                other_ref[:, left : left + half], other_d_ref[:tokens, low:high]
            )
        own_ref[:, low:high] = total[:rows, :]
        for index in range(1, groups):
            outs[index - 1][:, low:high] = total[index * rows : (index + 1) * rows, :].astype(
                NARROW
            )


def sum_body(count, layers, own_ref, *refs):
    total = own_ref[...]
    for ref in refs[:count]:
        total = total + ref[...].astype(WIDE)
    part = own_ref.shape[0] // layers
    for index, out in enumerate(refs[count:]):
        out[...] = total[index * part : (index + 1) * part, :].astype(out.dtype)


def sum_blocks(own, others, layers, first):
    rows, columns = own.shape
    part = rows // layers
    return run(
        functools.partial(sum_body, len(others), layers),
        [like((part, columns), first)] + [like((part, columns), NARROW)] * (layers - 1),
        [own] + others,
        rows * columns,
        12 * rows * columns,
        16,
        name="sum_blocks",
    )


def ordered_body(experts, layers, width, place_ref, low_ref, high_ref, *outs):
    qkv_ref, proj_ref, router_ref = outs[:3]
    rows = qkv_ref.shape[0]
    half = rows // 2
    ids = lax.broadcasted_iota(jnp.int32, (rows, half), 0)
    hot_low = (ids == place_ref[0:1, :]).astype(NARROW)
    hot_high = (ids == place_ref[1:2, :]).astype(NARROW)

    def pick(low, high):
        return mm(hot_low, low_ref[:, low:high]) + mm(hot_high, high_ref[:, low:high])

    proj_ref[...] = pick(0, width)
    qkv_ref[...] = pick(width, 4 * width)
    side = pick(4 * width, 4 * width + 128)
    router_ref[...] = side[:, 8 : 8 + experts]
    lanes = lax.broadcasted_iota(jnp.int32, (rows, rows), 1)
    lines = lax.broadcasted_iota(jnp.int32, (rows, rows), 0)
    for index, out in enumerate(outs[3:]):
        out[...] = jnp.sum(
            jnp.where(lanes == lines, side[:, index : index + 1], 0.0), axis=0, keepdims=True
        )


def spread_body(me_ref, *refs):
    out_ref = refs[-1]
    units = refs[0].shape[1]
    for mask, ref in enumerate(refs[:-1]):
        at = pl.multiple_of((me_ref[1] ^ mask) * units, 128)
        out_ref[:, pl.ds(at, units)] = ref[...].astype(WIDE)


def pack_body(core_ref, qkv_ref, proj_ref, router_ref, vectors_ref, out_ref, mine_ref, mark_ref):
    share, width = proj_ref.shape
    lanes = lax.broadcasted_iota(jnp.int32, (share, share), 1)
    lines = lax.broadcasted_iota(jnp.int32, (share, share), 0)
    places = lax.broadcasted_iota(jnp.int32, (share, 128), 1)
    spread = (
        lax.broadcasted_iota(jnp.int32, (router_ref.shape[1], 128), 0) + 8
        == lax.broadcasted_iota(jnp.int32, (router_ref.shape[1], 128), 1)
    ).astype(NARROW)
    side = mm(router_ref[...], spread)
    for index in range(vectors_ref.shape[0]):
        line = vectors_ref[index : index + 1, :]
        column = jnp.sum(jnp.where(lanes == lines, line, 0.0), axis=-1, keepdims=True)
        side = jnp.where(places == index, column, side)
    out_ref[:, : 3 * width] = qkv_ref[...]
    out_ref[:, 3 * width : 4 * width] = proj_ref[...]
    out_ref[:, 4 * width :] = side.astype(NARROW)
    rows = mine_ref.shape[0]
    at = pl.multiple_of(core_ref[0] * rows, 8)
    mine_ref[...] = out_ref[pl.ds(at, rows), :]
    mark_ref[...] = jnp.zeros_like(mark_ref)


def expert_weights_plain(me, vec, my_in, my_bias, my_out, rows, marked):
    rows, marked = jnp.concatenate(rows, axis=0), jnp.concatenate(marked, axis=0)
    width = rows.shape[1]
    gate = slot_gates(rows, marked[:, width:], vec[8:32].astype(NARROW), me)
    sent = (gate * marked[:, :width].astype(WIDE)).astype(NARROW)
    act, slope = gelu_parts(mm(rows, my_in) + my_bias.astype(WIDE))
    d_pre = mm_rows(sent, my_out) * slope
    return (
        mm_cols(act.astype(NARROW), sent),
        mm_cols(rows, d_pre.astype(NARROW)),
        jnp.sum(d_pre, axis=0, keepdims=True),
        jnp.sum(sent.astype(WIDE), axis=0, keepdims=True),
    )


def per_device(
    block_input,
    w_qkv,
    b_q,
    b_v,
    w_proj,
    b_proj,
    ln1_gain,
    ln1_bias,
    ln2_gain,
    ln2_bias,
    w_router,
    w_in,
    b_in,
    w_out,
    b_out,
    routes,
    slot_index,
    d_out,
):
    tokens, width = block_input.shape
    hidden_units = w_in.shape[2]
    experts = w_in.shape[0] * lax.axis_size("expert")
    groups = lax.axis_size("dp")
    layers = lax.axis_size("expert") // 2
    capacity = 2 * tokens // experts
    slots = -(-(capacity + 3) // 8) * 8
    total = experts * slots
    share = width // groups
    half = width // 2
    dp_me = lax.axis_index("dp")
    expert_me = lax.axis_index("expert")
    core, layer = expert_me % 2, expert_me // 2
    me = jnp.stack([expert_me, dp_me]).astype(jnp.int32)
    vectors = jnp.stack([b_q, b_v, b_proj, ln1_gain, ln1_bias, ln2_gain, ln2_bias]).astype(WIDE)
    wide = 4 * width + 128
    shard, mine, mark = run(
        pack_body,
        [
            like((share, wide), NARROW),
            like((share // 2, wide), NARROW),
            like((16, 128), NARROW),
        ],
        [core.reshape(1).astype(jnp.int32), w_qkv, w_proj, w_router, vectors],
        0,
        6 * share * wide,
        58,
        scalars=1,
        name="pack",
    )
    pieces, starts = gather_shared(shard, mine)
    d_late, routes, slot_index = after(
        (d_out, routes, slot_index), swap(mark, "expert", 1)
    )
    targets = jnp.where(slot_index < capacity, (routes ^ expert_me) * slots + slot_index, -1)
    targets_row = targets.T
    device_targets = jnp.where(slot_index < capacity, routes * slots + slot_index, -1)
    part = share // (2 * layers)
    order = jnp.arange(half, dtype=jnp.int32)
    spot = (order // (share // 2) ^ dp_me) * share + (
        order // part % layers ^ layer
    ) * part + order % part
    chosen_columns = jnp.concatenate(
        [spot + core * (share // 2), spot + (1 - core) * (share // 2)]
    )[None].astype(jnp.int32)

    marked_blocks = run(
        functools.partial(grad_slots_body, experts),
        like((experts, slots, width + 128), NARROW),
        [d_late, routes, device_targets.T],
        2 * total * tokens * width,
        4 * total * width,
        16,
        name="grad_slots",
    )
    marked_blocks = lax.all_to_all(marked_blocks, "expert", 0, 0, tiled=True)
    marked = run(
        order_body,
        like((total, width + 128), NARROW),
        [me, marked_blocks],
        total * width,
        4 * total * width,
        16,
        scalars=1,
        scratch=[pltpu.VMEM((total, width + 128), WIDE)],
        name="order",
    )

    full_qkv, full_proj, vec, qkv, context, log_total, keep, give = run(
        functools.partial(attend_body, len(pieces)),
        [
            like((width, 3 * width), NARROW),
            like((width, width), NARROW),
            like((32, width), WIDE),
            like((tokens, 3 * width), NARROW),
            like((tokens, width), NARROW),
            like((tokens, 128), WIDE),
            like((tokens, width), NARROW),
            like((tokens, width), NARROW),
        ],
        [jnp.stack(starts).astype(jnp.int32), block_input, chosen_columns] + pieces,
        10 * tokens * width * width,
        4 * width * wide,
        58,
        scalars=1,
        scratch=[pltpu.VMEM((width, 128), NARROW)],
        name="attend",
    )
    middle = run(
        functools.partial(middle_body, experts),
        [like((tokens, width), WIDE), like((tokens, width), NARROW)]
        + [like((slots, width), NARROW)] * experts,
        [context, block_input, vec, targets_row, full_proj],
        4 * tokens * width * width,
        4 * width * width,
        58,
        name="middle",
    )
    hidden, y_in = middle[:2]
    rows = join(exchange(middle[2:]))
    weight_in, weight_out = w_in[0], w_out[0]
    results = expert(
        me, rows, marked, vec, weight_in, b_in, weight_out, b_out, experts, slots, capacity, 512
    )
    fresh, d_expert_in = results
    d_returned = lax.all_to_all(d_expert_in, "expert", 0, 0, tiled=True)
    other = swap(after(give, fresh), "expert", 1)
    units = hidden_units // groups
    my_in, my_out, my_bias = (
        lax.dynamic_slice_in_dim(array, dp_me * units, units, axis)
        for array, axis in zip(after((weight_in, weight_out, b_in), y_in), (1, 0, 1))
    )
    marked_all = gather_rows(marked, y_in, rows)
    rows_all = gather_rows(rows, rows, fresh)
    d_returned, rows_all, marked_all, my_in, my_out, my_bias, other = lax.optimization_barrier(
        (d_returned, rows_all, marked_all, my_in, my_out, my_bias, other)
    )

    gates, d_hidden, d_context, early_sums = run(
        functools.partial(combine_body, experts, capacity),
        [
            like((tokens, 128), WIDE),
            like((tokens, width), WIDE),
            like((tokens, width), NARROW),
            like((32, width), WIDE),
        ],
        [hidden, y_in, d_out, vec, full_proj, routes, slot_index, device_targets, d_returned],
        2 * tokens * total * width + 2 * tokens * width * width,
        4 * width * width,
        24,
        scratch=[pltpu.VMEM((total, width), WIDE)],
        name="combine",
    )
    d_input, d_all = run(
        back_body,
        [like((tokens, width), WIDE), like((240, 4 * width), NARROW)],
        [qkv, d_context, log_total, full_qkv, block_input, vec, d_hidden, early_sums],
        40 * tokens * 256 * width,
        8 * tokens * width,
        32,
        name="back",
    )
    d_other = swap(d_all, "expert", 1)
    sums = run(
        functools.partial(outer_body, groups),
        [like((share // 2, wide), WIDE)] + [like((share // 2, wide), NARROW)] * (groups - 1),
        [chosen_columns, keep, other, d_all, d_other],
        4 * tokens * half * wide,
        6 * half * wide,
        24,
        scratch=[pltpu.VMEM((128, width), WIDE)],
        name="outer",
    )
    rows_all, marked_all = after((rows_all, marked_all), sums[0])
    if groups == 4:
        grads = expert_weights(
            me, vec, my_in, my_bias, my_out, rows_all, marked_all, groups, 256
        )
        part_w_out, blocks, (part_b_in, sum_sent) = grads[0], grads[1:-2], grads[-2:]
    else:
        part_w_out, d_w_in, part_b_in, sum_sent = expert_weights_plain(
            expert_me, vec, my_in, my_bias, my_out, rows_all, marked_all
        )
        blocks = [
            lax.dynamic_slice_in_dim(d_w_in, (dp_me ^ mask) * share, share, 0).astype(
                NARROW if mask else WIDE
            )
            for mask in range(groups)
        ]
    part_b_out = lax.dynamic_slice_in_dim(sum_sent[0], dp_me * share, share, 0)
    returned = lax.all_to_all(after(fresh, sums[0]), "expert", 0, 0, tiled=True)
    returned = after(returned, part_b_in)
    block_out = run(
        output_body,
        like((tokens, width), NARROW),
        [hidden, gates, device_targets, returned],
        4 * tokens * total * width,
        8 * tokens * width,
        24,
        scratch=[pltpu.VMEM((total, width), WIDE)],
        name="output",
    )
    sums = [sums[0]] + [swap(sums[mask], "dp", mask) for mask in range(1, groups)]
    sums, block_out, part_b_in, part_b_out = lax.optimization_barrier(
        (sums, block_out, part_b_in, part_b_out)
    )
    sums = sum_blocks(sums[0], sums[1:], layers, WIDE)
    blocks = [blocks[0]] + [
        swap(after(blocks[mask], sums[0]), "dp", mask) for mask in range(1, groups)
    ]
    sums = [sums[0]] + [swap(sums[mask], "expert", 2 * mask) for mask in range(1, layers)]
    done = sum_blocks(sums[0], sums[1:], 1, NARROW)[0]
    if groups == 4:
        part_w_in = run(
            spread_body,
            like((share, hidden_units), WIDE),
            [me] + blocks,
            share * hidden_units,
            8 * share * hidden_units,
            24,
            scalars=1,
            name="spread",
        )
    else:
        part_w_in = in_order([block.astype(WIDE) for block in blocks], dp_me, 1)
    done_pieces = [done] + [swap(done, "expert", 2 * mask) for mask in range(1, layers)]
    done_pieces, part_w_in = lax.optimization_barrier((done_pieces, part_w_in))
    low = join(done_pieces)
    high = swap(low, "expert", 1)

    place = jnp.arange(share // 2, dtype=jnp.int32)
    place = (place // part ^ layer) * part + place % part
    place = jnp.stack([place + core * (share // 2), place + (1 - core) * (share // 2)])
    finals = run(
        functools.partial(ordered_body, experts, layers, width),
        [
            like((share, 3 * width), WIDE),
            like((share, width), WIDE),
            like((share, experts), WIDE),
        ]
        + [like((1, share), WIDE)] * 7,
        [place.astype(jnp.int32), low, high],
        2 * share * share * wide,
        8 * share * wide,
        24,
        name="ordered",
    )
    vector_sum = [value[0] for value in finals[3:]]
    return (
        block_out,
        d_input,
        finals[0],
        vector_sum[3],
        vector_sum[4],
        finals[1],
        vector_sum[0],
        vector_sum[5],
        vector_sum[6],
        vector_sum[1],
        vector_sum[2],
        finals[2],
        part_w_in[None],
        part_b_in,
        part_w_out[None],
        part_b_out[None],
    )


def solution(mesh):
    return jax.shard_map(
        per_device,
        mesh=mesh,
        in_specs=(
            P(("dp", "expert"), None),
            P("dp", None),
            P("dp"),
            P("dp"),
            P("dp", None),
            P("dp"),
            P("dp"),
            P("dp"),
            P("dp"),
            P("dp"),
            P("dp", None),
            P("expert", None, None),
            P("expert", None),
            P("expert", None, None),
            P("expert", None),
            P(("dp", "expert"), None),
            P(("dp", "expert"), None),
            P(("dp", "expert"), None),
        ),
        out_specs=(
            P(("dp", "expert"), None),
            P(("dp", "expert"), None),
            P("dp", None),
            P("dp"),
            P("dp"),
            P("dp", None),
            P("dp"),
            P("dp"),
            P("dp"),
            P("dp"),
            P("dp"),
            P("dp", None),
            P("expert", "dp", None),
            P("expert", "dp"),
            P("expert", "dp", None),
            P("expert", "dp"),
        ),
        check_vma=False,
    )
```

time: 309 us -> 224 us (0.72)
  starting transfers between devices: 109 us -> 58.9 us
  waiting for transfers between devices: 97.8 us -> 64.7 us
  Pallas kernels: 50.1 us -> 67.3 us
  local copies, waits for them, and re-layouts: 44.8 us -> 30 us
    ppermute x94 -> x38, starting transfers between devices: 109 us -> 42 us  [swap(): lax.ppermute(values, axis, [(index, index ^ mask) for index in range(size)])]
    ppermute x94 -> x38, waiting for transfers between devices: 97.8 us -> 64.7 us  [swap(): lax.ppermute(values, axis, [(index, index ^ mask) for index in range(size)])]
    unnamed x128 -> x68, local copies, waits for them, and re-layouts: 27.1 us -> 9.38 us
    all_to_all x0 -> x3, starting transfers between devices: none -> 16.9 us  [the longest x1 7.28 us: per_device(): d_returned = lax.all_to_all(d_expert_in, 'expert', 0, 0, tiled=True)]
    pallas_call x12 -> x15, Pallas kernels: 20.2 us -> 32.9 us  [run(): pl.pallas_call(body, out_shape=outs, in_specs=[SMEM] * scalars + [VMEM] *...]
  transfers between devices with their start and end apart: 94 -> 41, of which waited for: 31 -> 14; matrix products, arithmetic and copies ran while one was open for 4% -> 8% of each run, Pallas kernels for 12% -> 22%
where the time goes in v3:
time: 224 us; the launch traced here: 223 us
  Pallas kernels  67.3 us (30%)
  waiting for transfers between devices  64.7 us (29%)
  starting transfers between devices  58.9 us (26%)
  local copies, waits for them, and re-layouts  30 us (13%)
    ppermute x38, waiting for transfers between devices, swap(): lax.ppermute(values, axis, [(index, index ^ mask) for index in range(size)])  64.7 us
    ppermute x38, starting transfers between devices, swap(): lax.ppermute(values, axis, [(index, index ^ mask) for index in range(size)])  42 us
    pallas_call x15, Pallas kernels, run(): pl.pallas_call(body, out_shape=outs, in_specs=[SMEM] * scalars + [VMEM] *...  32.9 us
    pallas_call x1, Pallas kernels, expert_weights(): pl.pallas_call(functools.partial(weights_body, count), grid=(units // chu...  19.1 us
    pallas_call x1, Pallas kernels, expert(): pl.pallas_call(functools.partial(expert_body, experts, spare), grid=(hidd...  15.3 us
    unnamed x68, local copies, waits for them, and re-layouts  9.38 us
    all_to_all x1, starting transfers between devices, per_device(): d_returned = lax.all_to_all(d_expert_in, 'expert', 0, 0, tiled=True)  7.28 us
    all_to_all x1, starting transfers between devices, per_device(): marked_blocks = lax.all_to_all(marked_blocks, 'expert', 0, 0, tiled=True)  4.88 us
  transfers between devices with their start and end apart: 41, of which 14 were waited for; matrix products, arithmetic and copies ran while one was open for 8% of the time, Pallas kernels for 22%

profile of v3, /device:TPU:0, one launch (start us, length us, event | category | flops | bytes accessed | tf_op | source)
XLA Modules:
  0.0 223.5 jit_solution(17673427963145830317)
XLA Ops:
  7.4 2.8 %pack.1 = (bf16[192,3200]{1,0:T(8,128)(2,1)}, bf16[96,3200]{1,0:T(8,128)(2,1)}, bf16[16,128]{1,0:T(8,128)(2,1)}) custom-call(s32[1]{0:T(128)} %bitcast.9.core_ref, bf16[192,2304]{1,0:T(8,128)(2,1)} %qkv_ref.1, bf16[192,768]{1,0:T(8,128)(2,1)} %proj_ref.1, bf16[192,8]{1,0:T(8,128)(2,1)} %copy.49.router_ref, f32[7,192]{1,0:T(8,128)} %convert_element_type.3.vectors_ref), custom_call_target="tpu_custom_call" | custom-call | flops 1 | bytes 1 | tf_op jit(solution)/shard_map/pack/pallas_call | solution.py:118
  10.2 3.0 %collective-permute-start.1 = (bf16[96,3200]{1,0:T(8,128)(2,1)}, bf16[96,3200]{1,0:T(8,128)(2,1)S(1)}, u32[]{:S(2)}, u32[]{:S(2)}) collective-permute-start(bf16[96,3200]{1,0:T(8,128)(2,1)} %get-tuple-element.125), channel_id=1, source_target_pairs={{0,16},{8,24},{16,0},{24,8},{1,17},{9,25},{17,1},{25,9},{2,18},{10... | collective-permute-start | bytes 1843208 | tf_op jit(solution)/shard_map/ppermute | solution.py:45
  18.1 4.9 %all-to-all-start = ((bf16[8,56,896]{2,1,0:T(8,128)(2,1)}), bf16[8,56,896]{2,1,0:T(8,128)(2,1)S(1)}, u32[]{:S(2)}, u32[]{:S(2)}) async-start(bf16[8,56,896]{2,1,0:T(8,128)(2,1)} %grad_slots.1), calls=%async_computation | async-start | bytes 1605632 | tf_op jit(solution)/shard_map/all_to_all | solution.py:777
  23.0 4.2 %collective-permute-done.1.refs_5_ = bf16[96,3200]{1,0:T(8,128)(2,1)S(1)} collective-permute-done((bf16[96,3200]{1,0:T(8,128)(2,1)}, bf16[96,3200]{1,0:T(8,128)(2,1)S(1)}, u32[]{:S(2)}, u32[]{:S(2)}) %collective-permute-start.1) | collective-permute-done | bytes 614432 | tf_op jit(solution)/shard_map/ppermute | solution.py:45
  32.5 4.1 %collective-permute-done.3.refs_7_ = bf16[48,3200]{1,0:T(8,128)(2,1)S(1)} collective-permute-done((bf16[48,3200]{1,0:T(8,128)(2,1)}, bf16[48,3200]{1,0:T(8,128)(2,1)S(1)}, u32[]{:S(2)}, u32[]{:S(2)}) %collective-permute-start.3) | collective-permute-done | bytes 307232 | tf_op jit(solution)/shard_map/ppermute | solution.py:45
  40.7 7.0 %attend.1 = (bf16[768,2304]{1,0:T(8,128)(2,1)}, bf16[768,768]{1,0:T(8,128)(2,1)}, f32[32,768]{1,0:T(8,128)}, bf16[197,2304]{1,0:T(8,128)(2,1)}, bf16[197,768]{1,...) custom-call(s32[9]{0:T(128)} %stack.77.refs_0_, bf16[197,768]{1,0:T(8,128)(2,1)} %x_ref.3, ...), custom_call_target="tpu_custom_call" | custom-call | flops 1 | bytes 1 | tf_op jit(solution)/shard_map/attend/pallas_call | solution.py:118
  47.8 3.3 %middle.1 = (f32[197,768]{1,0:T(8,128)}, bf16[197,768]{1,0:T(8,128)(2,1)}, bf16[56,768]{1,0:T(8,128)(2,1)}, bf16[56,768]{1,0:T(8,128)(2,1)}, bf16[56,768]{1,0:T(...) custom-call(bf16[197,768]{1,0:T(8,128)(2,1)} %get-tuple-element.127., ...), custom_call_target="tpu_custom_call" | custom-call | flops 1 | bytes 1 | tf_op jit(solution)/shard_map/middle/pallas_call | solution.py:118
  53.2 2.6 %collective-permute-start.11 = (bf16[56,768]{1,0:T(8,128)(2,1)}, bf16[56,768]{1,0:T(8,128)(2,1)S(1)}, u32[]{:S(2)}, u32[]{:S(2)}) collective-permute-start(bf16[56,768]{1,0:T(8,128)(2,1)} %get-tuple-element.136), channel_id=1, source_target_pairs={{0,4},{1,5},{2,6},{3,7},{4,0},{5,1},{6,2},{7,3},{8,12},{9,13},{10,... | collective-permute-start | bytes 258056 | tf_op jit(solution)/shard_map/ppermute | solution.py:45
  56.0 3.6 %collective-permute-start.13 = (bf16[56,768]{1,0:T(8,128)(2,1)}, bf16[56,768]{1,0:T(8,128)(2,1)S(1)}, u32[]{:S(2)}, u32[]{:S(2)}) collective-permute-start(bf16[56,768]{1,0:T(8,128)(2,1)} %get-tuple-element.138), channel_id=1, source_target_pairs={{0,6},{1,7},{2,4},{3,5},{4,2},{5,3},{6,0},{7,1},{8,14},{9,15},{10,... | collective-permute-start | bytes 258056 | tf_op jit(solution)/shard_map/ppermute | solution.py:45
  60.5 8.3 %collective-permute-done.12.refs_5_ = bf16[56,768]{1,0:T(8,128)(2,1)S(1)} collective-permute-done((bf16[56,768]{1,0:T(8,128)(2,1)}, bf16[56,768]{1,0:T(8,128)(2,1)S(1)}, u32[]{:S(2)}, u32[]{:S(2)}) %collective-permute-start.12) | collective-permute-done | bytes 86048 | tf_op jit(solution)/shard_map/ppermute | solution.py:45
  73.3 15.3 %expert.1 = (bf16[8,56,768]{2,1,0:T(8,128)(2,1)}, bf16[8,56,768]{2,1,0:T(8,128)(2,1)}) custom-call(s32[2]{0:T(128)} %copy-done.18, bf16[448,768]{1,0:T(8,128)(2,1)} %copy-done.1, bf16[448,896]{1,0:T(8,128)(2,1)} %copy-done, f32[32,768]{1,0:T(8,128)} %get-tuple-element.128.vec_ref.refs_3_, bf16[768,3072]{1,0:T(8,128)(2,1)} %bitcast.28, ...), custom_call_target="tpu_custom_call" | custom-call | flops 1 | bytes 1 | tf_op jit(solution)/shard_map/expert/pallas_call | solution.py:348
  88.6 7.3 %all-to-all-start.1 = ((bf16[8,56,768]{2,1,0:T(8,128)(2,1)}), bf16[8,56,768]{2,1,0:T(8,128)(2,1)S(1)}, u32[]{:S(2)}, u32[]{:S(2)}) async-start(bf16[8,56,768]{2,1,0:T(8,128)(2,1)} %get-tuple-element.141), calls=%async_computation.1 | async-start | bytes 1376256 | tf_op jit(solution)/shard_map/all_to_all | solution.py:827
  103.6 10.6 %collective-permute-done.16.refs_2_ = bf16[448,768]{1,0:T(8,128)(2,1)S(1)} collective-permute-done((bf16[448,768]{1,0:T(8,128)(2,1)S(1)}, bf16[448,768]{1,0:T(8,128)(2,1)S(1)}, u32[]{:S(2)}, u32[]{:S(2)}) %collective-permute-start.16) | collective-permute-done | bytes 688160 | tf_op jit(solution)/shard_map/ppermute | solution.py:45
  120.7 3.3 %constant_dynamic-slice_fusion.2 = (bf16[768,768]{1,0:T(8,128)(2,1)}, bf16[768,768]{1,0:T(8,128)(2,1)}) fusion(bf16[3072,768]{1,0:T(8,128)(2,1)} %bitcast.31, s32[]{:T(128)S(6)} %select_n.87, bf16[768,3072]{1,0:T(8,128)(2,1)} %bitcast.29), kind=kLoop, calls=%fused_computation.40 | loop fusion | bytes 4718596 | tf_op jit(solution)/shard_map/dynamic_slice | solution.py:831
  124.1 5.9 %collective-permute-done.18.refs_4_ = bf16[224,768]{1,0:T(8,128)(2,1)} collective-permute-done((bf16[224,768]{1,0:T(8,128)(2,1)}, bf16[224,768]{1,0:T(8,128)(2,1)}, u32[]{:S(2)}, u32[]{:S(2)}) %collective-permute-start.18) | collective-permute-done | bytes 344096 | tf_op jit(solution)/shard_map/ppermute | solution.py:45
  135.1 6.0 %back.1 = (f32[197,768]{1,0:T(8,128)}, bf16[240,3072]{1,0:T(8,128)(2,1)S(1)}) custom-call(bf16[197,2304]{1,0:T(8,128)(2,1)S(1)} %copy-done.9, bf16[197,768]{1,0:T(8,128)(2,1)S(1)} %get-tuple-element.159.dctx_ref, f32[197,128]{1,0:T(8,128)S(1)} %copy-done.15, bf16[768,2304]{1,0:T(8,128)(2,1)S(1)} %copy-done.4, bf16[197,768]{1,0:T(8,128)(2,1)S(1)} %copy-done.5, ...), custom_call_target="tpu_custom_call" | custom-call | flops 1 | bytes 1 | tf_op jit(solution)/shard_map/back/pallas_call | solution.py:118
  141.1 3.3 %collective-permute-done.24.other_d_ref = bf16[240,3072]{1,0:T(8,128)(2,1)S(1)} collective-permute-done((bf16[240,3072]{1,0:T(8,128)(2,1)S(1)}, bf16[240,3072]{1,0:T(8,128)(2,1)S(1)}, u32[]{:S(2)}, u32[]{:S(2)}) %collective-permute-start.24) | collective-permute-done | bytes 1474592 | tf_op jit(solution)/shard_map/ppermute | solution.py:45
  144.4 2.6 %outer.1 = (f32[96,3200]{1,0:T(8,128)S(1)}, bf16[96,3200]{1,0:T(8,128)(2,1)S(1)}, bf16[96,3200]{1,0:T(8,128)(2,1)S(1)}, bf16[96,3200]{1,0:T(8,128)(2,1)S(1)}) custom-call(s32[1,768]{1,0:T(1,128)S(1)} %copy-done.17, bf16[197,768]{1,0:T(8,128)(2,1)S(1)} %copy-done.11, bf16[197,768]{1,0:T(8,128)(2,1)} %collective-permute-done.23.other_ref, ...), custom_call_target="tpu_custom_call" | custom-call | flops 1 | bytes 1 | tf_op jit(solution)/shard_map/outer/pallas_call | solution.py:118
  149.5 4.7 %all-to-all-start.2 = ((bf16[8,56,768]{2,1,0:T(8,128)(2,1)}), bf16[8,56,768]{2,1,0:T(8,128)(2,1)S(1)}, u32[]{:S(2)}, u32[]{:S(2)}) async-start(bf16[8,56,768]{2,1,0:T(8,128)(2,1)} %get-tuple-element.170), calls=%async_computation.2 | async-start | bytes 1376256 | tf_op jit(solution)/shard_map/all_to_all | solution.py:892
  157.7 19.1 %expert_weights.1 = (f32[768,768]{1,0:T(8,128)}, f32[192,768]{1,0:T(8,128)}, bf16[192,768]{1,0:T(8,128)(2,1)}, bf16[192,768]{1,0:T(8,128)(2,1)}, bf16[192,768]{1...) custom-call(s32[2]{0:T(128)} %copy-done.18, f32[32,768]{1,0:T(8,128)} %get-tuple-element.128.vec_ref.refs_3_, ...), custom_call_target="tpu_custom_call" | custom-call | flops 1 | bytes 1 | tf_op jit(solution)/shard_map/expert_weights/pallas_call | solution.py:414
  179.4 5.8 %collective-permute-done.26.refs_1_ = bf16[96,3200]{1,0:T(8,128)(2,1)} collective-permute-done((bf16[96,3200]{1,0:T(8,128)(2,1)}, bf16[96,3200]{1,0:T(8,128)(2,1)}, u32[]{:S(2)}, u32[]{:S(2)}) %collective-permute-start.26) | collective-permute-done | bytes 614432 | tf_op jit(solution)/shard_map/ppermute | solution.py:45
  194.9 8.3 %collective-permute-done.29.refs_1_ = bf16[24,3200]{1,0:T(8,128)(2,1)S(1)} collective-permute-done((bf16[24,3200]{1,0:T(8,128)(2,1)S(1)}, bf16[24,3200]{1,0:T(8,128)(2,1)S(1)}, u32[]{:S(2)}, u32[]{:S(2)}) %collective-permute-start.29) | collective-permute-done | bytes 153632 | tf_op jit(solution)/shard_map/ppermute | solution.py:45
  203.2 2.5 %collective-permute-start.33 = (bf16[24,3200]{1,0:T(8,128)(2,1)S(1)}, bf16[24,3200]{1,0:T(8,128)(2,1)S(1)}, u32[]{:S(2)}, u32[]{:S(2)}) collective-permute-start(bf16[24,3200]{1,0:T(8,128)(2,1)S(1)} %sum_blocks.3.refs_0_), channel_id=1, source_target_pairs={{0,6},{1,7},{2,4},{3,5},{4,2},{5,3},{6,0},{7,1},{8,14},{9,15},{10,... | collective-permute-start | bytes 460808 | tf_op jit(solution)/shard_map/ppermute | solution.py:45
  211.8 6.9 %collective-permute-done.32.refs_2_ = bf16[24,3200]{1,0:T(8,128)(2,1)S(1)} collective-permute-done((bf16[24,3200]{1,0:T(8,128)(2,1)S(1)}, bf16[24,3200]{1,0:T(8,128)(2,1)S(1)}, u32[]{:S(2)}, u32[]{:S(2)}) %collective-permute-start.32) | collective-permute-done | bytes 153632 | tf_op jit(solution)/shard_map/ppermute | solution.py:45
  (182 shorter events, 77.0 us)
Async XLA Ops:
  10.2 17.0 %collective-permute-start.1 = (bf16[96,3200]{1,0:T(8,128)(2,1)}, bf16[96,3200]{1,0:T(8,128)(2,1)S(1)}, u32[]{:S(2)}, u32[]{:S(2)}) collective-permute-start(bf16[96,3200]{1,0:T(8,128)(2,1)} %get-tuple-element.125), channel_id=1, source_target_pairs={{0,16},{8,24},{16,0},{24,8},{1,17},{9,25},{17,1},{25,9},{2,18},{10... | collective-permute-start | bytes 1843208 | tf_op jit(solution)/shard_map/ppermute | solution.py:45
  13.1 16.6 %collective-permute-start = (bf16[96,3200]{1,0:T(8,128)(2,1)}, bf16[96,3200]{1,0:T(8,128)(2,1)S(1)}, u32[]{:S(2)}, u32[]{:S(2)}) collective-permute-start(bf16[96,3200]{1,0:T(8,128)(2,1)} %get-tuple-element.125), channel_id=1, source_target_pairs={{0,8},{8,0},{16,24},{24,16},{1,9},{9,1},{17,25},{25,17},{2,10},{10... | collective-permute-start | bytes 1843208 | tf_op jit(solution)/shard_map/ppermute | solution.py:45
  18.1 52.5 %all-to-all-start = ((bf16[8,56,896]{2,1,0:T(8,128)(2,1)}), bf16[8,56,896]{2,1,0:T(8,128)(2,1)S(1)}, u32[]{:S(2)}, u32[]{:S(2)}) async-start(bf16[8,56,896]{2,1,0:T(8,128)(2,1)} %grad_slots.1), calls=%async_computation | async-start | bytes 1605632 | tf_op jit(solution)/shard_map/all_to_all | solution.py:777
  55.8 13.0 %collective-permute-start.12 = (bf16[56,768]{1,0:T(8,128)(2,1)}, bf16[56,768]{1,0:T(8,128)(2,1)S(1)}, u32[]{:S(2)}, u32[]{:S(2)}) collective-permute-start(bf16[56,768]{1,0:T(8,128)(2,1)} %get-tuple-element.137), channel_id=1, source_target_pairs={{0,5},{1,4},{2,7},{3,6},{4,1},{5,0},{6,3},{7,2},{8,13},{9,12},{10,... | collective-permute-start | bytes 258056 | tf_op jit(solution)/shard_map/ppermute | solution.py:45
  56.0 12.8 %collective-permute-start.13 = (bf16[56,768]{1,0:T(8,128)(2,1)}, bf16[56,768]{1,0:T(8,128)(2,1)S(1)}, u32[]{:S(2)}, u32[]{:S(2)}) collective-permute-start(bf16[56,768]{1,0:T(8,128)(2,1)} %get-tuple-element.138), channel_id=1, source_target_pairs={{0,6},{1,7},{2,4},{3,5},{4,2},{5,3},{6,0},{7,1},{8,14},{9,15},{10,... | collective-permute-start | bytes 258056 | tf_op jit(solution)/shard_map/ppermute | solution.py:45
  71.2 26.8 %collective-permute-start.20 = (bf16[448,896]{1,0:T(8,128)(2,1)S(1)}, bf16[448,896]{1,0:T(8,128)(2,1)}, u32[]{:S(2)}, u32[]{:S(2)}) collective-permute-start(bf16[448,896]{1,0:T(8,128)(2,1)S(1)} %order.1.marked_ref.refs_5_), channel_id=1, source_target_pairs={{0,16},{8,24},{16,0},{24,8},{1,17},{9,25},{17,1},{25,9},{2,18},{10... | collective-permute-start | bytes 2408456 | tf_op jit(solution)/shard_map/ppermute | solution.py:45
  72.8 25.2 %collective-permute-start.19 = (bf16[448,896]{1,0:T(8,128)(2,1)S(1)}, bf16[448,896]{1,0:T(8,128)(2,1)}, u32[]{:S(2)}, u32[]{:S(2)}) collective-permute-start(bf16[448,896]{1,0:T(8,128)(2,1)S(1)} %order.1.marked_ref.refs_5_), channel_id=1, source_target_pairs={{0,8},{8,0},{16,24},{24,16},{1,9},{9,1},{17,25},{25,17},{2,10},{10... | collective-permute-start | bytes 2408456 | tf_op jit(solution)/shard_map/ppermute | solution.py:45
  88.6 41.4 %all-to-all-start.1 = ((bf16[8,56,768]{2,1,0:T(8,128)(2,1)}), bf16[8,56,768]{2,1,0:T(8,128)(2,1)S(1)}, u32[]{:S(2)}, u32[]{:S(2)}) async-start(bf16[8,56,768]{2,1,0:T(8,128)(2,1)} %get-tuple-element.141), calls=%async_computation.1 | async-start | bytes 1376256 | tf_op jit(solution)/shard_map/all_to_all | solution.py:827
  95.8 18.3 %collective-permute-start.16 = (bf16[448,768]{1,0:T(8,128)(2,1)S(1)}, bf16[448,768]{1,0:T(8,128)(2,1)S(1)}, u32[]{:S(2)}, u32[]{:S(2)}) collective-permute-start(bf16[448,768]{1,0:T(8,128)(2,1)S(1)} %copy-done.2), channel_id=1, source_target_pairs={{0,16},{8,24},{16,0},{24,8},{1,17},{9,25},{17,1},{25,9},{2,18},{10... | collective-permute-start | bytes 2064392 | tf_op jit(solution)/shard_map/ppermute | solution.py:45
  96.4 18.3 %collective-permute-start.15 = (bf16[448,768]{1,0:T(8,128)(2,1)S(1)}, bf16[448,768]{1,0:T(8,128)(2,1)S(1)}, u32[]{:S(2)}, u32[]{:S(2)}) collective-permute-start(bf16[448,768]{1,0:T(8,128)(2,1)S(1)} %copy-done.2), channel_id=1, source_target_pairs={{0,8},{8,0},{16,24},{24,16},{1,9},{9,1},{17,25},{25,17},{2,10},{10... | collective-permute-start | bytes 2064392 | tf_op jit(solution)/shard_map/ppermute | solution.py:45
  101.6 28.4 %collective-permute-start.22 = (bf16[224,896]{1,0:T(8,128)(2,1)}, bf16[224,896]{1,0:T(8,128)(2,1)}, u32[]{:S(2)}, u32[]{:S(2)}) collective-permute-start(bf16[224,896]{1,0:T(8,128)(2,1)} %slice.23), channel_id=1, source_target_pairs={{0,8},{8,0},{16,24},{24,16},{1,9},{9,1},{17,25},{25,17},{2,10},{10... | collective-permute-start | bytes 1204232 | tf_op jit(solution)/shard_map/ppermute | solution.py:45
  102.0 28.0 %collective-permute-start.21 = (bf16[224,896]{1,0:T(8,128)(2,1)}, bf16[224,896]{1,0:T(8,128)(2,1)}, u32[]{:S(2)}, u32[]{:S(2)}) collective-permute-start(bf16[224,896]{1,0:T(8,128)(2,1)} %slice.22), channel_id=1, source_target_pairs={{0,16},{8,24},{16,0},{24,8},{1,17},{9,25},{17,1},{25,9},{2,18},{10... | collective-permute-start | bytes 1204232 | tf_op jit(solution)/shard_map/ppermute | solution.py:45
  116.3 13.7 %collective-permute-start.18 = (bf16[224,768]{1,0:T(8,128)(2,1)}, bf16[224,768]{1,0:T(8,128)(2,1)}, u32[]{:S(2)}, u32[]{:S(2)}) collective-permute-start(bf16[224,768]{1,0:T(8,128)(2,1)} %slice.21), channel_id=1, source_target_pairs={{0,8},{8,0},{16,24},{24,16},{1,9},{9,1},{17,25},{25,17},{2,10},{10... | collective-permute-start | bytes 1032200 | tf_op jit(solution)/shard_map/ppermute | solution.py:45
  117.8 12.2 %collective-permute-start.17 = (bf16[224,768]{1,0:T(8,128)(2,1)}, bf16[224,768]{1,0:T(8,128)(2,1)}, u32[]{:S(2)}, u32[]{:S(2)}) collective-permute-start(bf16[224,768]{1,0:T(8,128)(2,1)} %slice.20), channel_id=1, source_target_pairs={{0,16},{8,24},{16,0},{24,8},{1,17},{9,25},{17,1},{25,9},{2,18},{10... | collective-permute-start | bytes 1032200 | tf_op jit(solution)/shard_map/ppermute | solution.py:45
  149.5 28.6 %all-to-all-start.2 = ((bf16[8,56,768]{2,1,0:T(8,128)(2,1)}), bf16[8,56,768]{2,1,0:T(8,128)(2,1)S(1)}, u32[]{:S(2)}, u32[]{:S(2)}) async-start(bf16[8,56,768]{2,1,0:T(8,128)(2,1)} %get-tuple-element.170), calls=%async_computation.2 | async-start | bytes 1376256 | tf_op jit(solution)/shard_map/all_to_all | solution.py:892
  154.2 25.2 %collective-permute-start.25 = (bf16[96,3200]{1,0:T(8,128)(2,1)}, bf16[96,3200]{1,0:T(8,128)(2,1)S(1)}, u32[]{:S(2)}, u32[]{:S(2)}) collective-permute-start(bf16[96,3200]{1,0:T(8,128)(2,1)} %copy-done.22), channel_id=1, source_target_pairs={{0,8},{8,0},{16,24},{24,16},{1,9},{9,1},{17,25},{25,17},{2,10},{10... | collective-permute-start | bytes 1843208 | tf_op jit(solution)/shard_map/ppermute | solution.py:45
  155.8 29.5 %collective-permute-start.26 = (bf16[96,3200]{1,0:T(8,128)(2,1)}, bf16[96,3200]{1,0:T(8,128)(2,1)}, u32[]{:S(2)}, u32[]{:S(2)}) collective-permute-start(bf16[96,3200]{1,0:T(8,128)(2,1)} %copy-done.21), channel_id=1, source_target_pairs={{0,16},{8,24},{16,0},{24,8},{1,17},{9,25},{17,1},{25,9},{2,18},{10... | collective-permute-start | bytes 1843208 | tf_op jit(solution)/shard_map/ppermute | solution.py:45
  157.3 28.0 %collective-permute-start.27 = (bf16[96,3200]{1,0:T(8,128)(2,1)}, bf16[96,3200]{1,0:T(8,128)(2,1)}, u32[]{:S(2)}, u32[]{:S(2)}) collective-permute-start(bf16[96,3200]{1,0:T(8,128)(2,1)} %copy-done.20), channel_id=1, source_target_pairs={{0,24},{8,16},{16,8},{24,0},{1,25},{9,17},{17,9},{25,1},{2,26},{10... | collective-permute-start | bytes 1843208 | tf_op jit(solution)/shard_map/ppermute | solution.py:45
  188.6 18.8 %collective-permute-start.34 = (bf16[192,768]{1,0:T(8,128)(2,1)S(1)}, bf16[192,768]{1,0:T(8,128)(2,1)S(1)}, u32[]{:S(2)}, u32[]{:S(2)}) collective-permute-start(bf16[192,768]{1,0:T(8,128)(2,1)S(1)} %copy-done.32), channel_id=1, source_target_pairs={{0,8},{8,0},{16,24},{24,16},{1,9},{9,1},{17,25},{25,17},{2,10},{10... | collective-permute-start | bytes 884744 | tf_op jit(solution)/shard_map/ppermute | solution.py:45
  189.9 13.3 %collective-permute-start.29 = (bf16[24,3200]{1,0:T(8,128)(2,1)S(1)}, bf16[24,3200]{1,0:T(8,128)(2,1)S(1)}, u32[]{:S(2)}, u32[]{:S(2)}) collective-permute-start(bf16[24,3200]{1,0:T(8,128)(2,1)S(1)} %get-tuple-element.205), channel_id=1, source_target_pairs={{0,4},{1,5},{2,6},{3,7},{4,0},{5,1},{6,2},{7,3},{8,12},{9,13},{10,... | collective-permute-start | bytes 460808 | tf_op jit(solution)/shard_map/ppermute | solution.py:45
  192.6 15.1 %collective-permute-start.35 = (bf16[192,768]{1,0:T(8,128)(2,1)S(1)}, bf16[192,768]{1,0:T(8,128)(2,1)S(1)}, u32[]{:S(2)}, u32[]{:S(2)}) collective-permute-start(bf16[192,768]{1,0:T(8,128)(2,1)S(1)} %copy-done.31), channel_id=1, source_target_pairs={{0,16},{8,24},{16,0},{24,8},{1,17},{9,25},{17,1},{25,9},{2,18},{10... | collective-permute-start | bytes 884744 | tf_op jit(solution)/shard_map/ppermute | solution.py:45
  193.4 14.3 %collective-permute-start.36 = (bf16[192,768]{1,0:T(8,128)(2,1)S(1)}, bf16[192,768]{1,0:T(8,128)(2,1)S(1)}, u32[]{:S(2)}, u32[]{:S(2)}) collective-permute-start(bf16[192,768]{1,0:T(8,128)(2,1)S(1)} %copy-done.30), channel_id=1, source_target_pairs={{0,24},{8,16},{16,8},{24,0},{1,25},{9,17},{17,9},{25,1},{2,26},{10... | collective-permute-start | bytes 884744 | tf_op jit(solution)/shard_map/ppermute | solution.py:45
  205.7 12.9 %collective-permute-start.32 = (bf16[24,3200]{1,0:T(8,128)(2,1)S(1)}, bf16[24,3200]{1,0:T(8,128)(2,1)S(1)}, u32[]{:S(2)}, u32[]{:S(2)}) collective-permute-start(bf16[24,3200]{1,0:T(8,128)(2,1)S(1)} %sum_blocks.3.refs_0_), channel_id=1, source_target_pairs={{0,4},{1,5},{2,6},{3,7},{4,0},{5,1},{6,2},{7,3},{8,12},{9,13},{10,... | collective-permute-start | bytes 460808 | tf_op jit(solution)/shard_map/ppermute | solution.py:45
  207.5 11.2 %collective-permute-start.31 = (bf16[24,3200]{1,0:T(8,128)(2,1)S(1)}, bf16[24,3200]{1,0:T(8,128)(2,1)S(1)}, u32[]{:S(2)}, u32[]{:S(2)}) collective-permute-start(bf16[24,3200]{1,0:T(8,128)(2,1)S(1)} %sum_blocks.3.refs_0_), channel_id=1, source_target_pairs={{0,2},{1,3},{2,0},{3,1},{4,6},{5,7},{6,4},{7,5},{8,10},{9,11},{10,... | collective-permute-start | bytes 460808 | tf_op jit(solution)/shard_map/ppermute | solution.py:45
  (50 other events, 387.0 us)

commit v4 on v3

--- a/solution.py
+++ b/solution.py
@@ -72,20 +72,17 @@
     return pieces, starts
 
 
-def after(values, *marks):
-    return lax.optimization_barrier((values, marks))[0]
-
-
-def gather_rows(rows, first_mark, second_mark):
+def gather_near(rows):
     groups = lax.axis_size("dp")
-    rows_later = after(rows, first_mark)
-    if groups != 4:
-        return [rows] + [swap(rows_later, "dp", mask) for mask in range(1, groups)]
-    half = rows.shape[0] // 2
-    from_one = swap(rows_later, "dp", 1)
-    from_two = swap(rows_later, "dp", 2)
-    one, two = after((from_one, from_two), second_mark)
-    return [rows, one, two, swap(one[:half], "dp", 2), swap(two[half:], "dp", 1)]
+    return [swap(rows, "dp", mask) for mask in ((1, 2) if groups == 4 else range(1, groups))]
+
+
+def gather_far(near):
+    if lax.axis_size("dp") != 4:
+        return []
+    one, two = near
+    half = one.shape[0] // 2
+    return [swap(one[:half], "dp", 2), swap(two[half:], "dp", 1)]
 
 
 def exchange(blocks):
@@ -114,17 +111,27 @@
     return jax.ShapeDtypeStruct(shape, dtype)
 
 
-def run(body, outs, operands, flops, moved, mib, scalars=0, scratch=(), name=None):
+def run(
+    body, outs, operands, flops, moved, mib, scalars=0, scratch=(), out_specs=None, name=None, marks=()
+):
+    marks = list(marks)
+    count = len(operands)
+
+    def marked_body(*refs):
+        body(*refs[:count], *refs[count + len(marks) :])
+
     return pl.pallas_call(
-        body,
+        marked_body,
         out_shape=outs,
-        in_specs=[SMEM] * scalars + [VMEM] * (len(operands) - scalars),
-        out_specs=jax.tree.map(lambda _: VMEM, outs),
+        in_specs=[SMEM] * scalars
+        + [VMEM] * (count - scalars)
+        + [pl.BlockSpec(memory_space=pl.ANY)] * len(marks),
+        out_specs=out_specs or jax.tree.map(lambda _: VMEM, outs),
         scratch_shapes=list(scratch),
         compiler_params=pltpu.CompilerParams(vmem_limit_bytes=mib * MIB),
         cost_estimate=pl.CostEstimate(flops=1, bytes_accessed=1, transcendentals=0),
         name=name,
-    )(*operands)
+    )(*operands, *marks)
 
 
 def mm(left, right):
@@ -188,21 +195,20 @@
         out_ref[index, :, width:] = marks[index * slots : (index + 1) * slots, :]
 
 
-def order_body(me_ref, blocks_ref, out_ref, wide_ref):
-    experts, slots, _ = blocks_ref.shape
-    for index in range(experts):
-        at = index * slots
-        wide_ref[at : at + slots, :] = blocks_ref[me_ref[0] ^ index].astype(WIDE)
+def order_body(me_ref, *refs):
+    out_ref, wide_ref = refs[-2:]
+    slots = refs[0].shape[0]
+    for mask, ref in enumerate(refs[:-2]):
+        at = pl.multiple_of((me_ref[0] ^ mask) * slots, 8)
+        wide_ref[pl.ds(at, slots), :] = ref[...].astype(WIDE)
     out_ref[...] = wide_ref[...].astype(NARROW)
 
 
 def attend_body(count, *refs):
     starts_ref, x_ref, columns_ref = refs[0], refs[1], refs[2]
     pieces = refs[3 : 3 + count]
-    full_ref, proj_ref, vec_ref, qkv_ref, ctx_ref, lse_ref, keep_ref, give_ref = refs[
-        3 + count : 11 + count
-    ]
-    side_ref = refs[11 + count]
+    full_ref, vec_ref, qkv_ref, ctx_ref, lse_ref, keep_ref, give_ref = refs[3 + count : 10 + count]
+    side_ref = refs[10 + count]
     tokens, width = x_ref.shape
     for index, piece in enumerate(pieces):
         rows = piece.shape[0]
@@ -210,8 +216,7 @@
         if count > 1:
             at = pl.multiple_of(at, 16)
         full_ref[pl.ds(at, rows), :] = piece[:, : 3 * width]
-        proj_ref[pl.ds(at, rows), :] = piece[:, 3 * width : 4 * width]
-        side_ref[pl.ds(at, rows), :] = piece[:, 4 * width :]
+        side_ref[pl.ds(at, rows), :] = piece[:, 3 * width :]
     side = jnp.transpose(side_ref[...].astype(WIDE))
     vec_ref[...] = side[: vec_ref.shape[0], :]
     bias_q, bias_v = vec_ref[0:1, :], vec_ref[1:2, :]
@@ -255,7 +260,12 @@
     give_ref[:, half:] = chosen[:, half:]
 
 
-def middle_body(experts, ctx_ref, x_ref, vec_ref, targets_ref, full_ref, hidden_ref, y_ref, *outs):
+def middle_body(experts, count, starts_ref, ctx_ref, x_ref, vec_ref, targets_ref, *refs):
+    full_ref, hidden_ref, y_ref = refs[count : count + 3]
+    outs = refs[count + 3 :]
+    for index, piece in enumerate(refs[:count]):
+        at = pl.multiple_of(starts_ref[index], 16) if count > 1 else 0
+        full_ref[pl.ds(at, piece.shape[0]), :] = piece[...]
     hidden = x_ref[...].astype(WIDE) + mm(ctx_ref[...], full_ref[...]) + vec_ref[2:3, :]
     hidden_ref[...] = hidden
     normed, _ = normalize(hidden)
@@ -329,13 +339,13 @@
         ]
         for index in range(experts):
             at = index * slots
-            fresh_ref[me_ref[0] ^ index] = acc_ref[at : at + slots, :].astype(NARROW)
+            fresh_ref[index] = acc_ref[at : at + slots, :].astype(NARROW)
             mine = jnp.zeros((slots, 128), WIDE)
             for place, term in enumerate(terms):
                 mine = jnp.where(lanes == place, term[at : at + slots, :], mine)
             packed = mm(spare_hot, mm_cols(mine.astype(NARROW), line_hot).astype(NARROW))
-            back_ref[me_ref[0] ^ index, :, :128] = (dacc_ref[at : at + slots, :128] + packed).astype(NARROW)
-            back_ref[me_ref[0] ^ index, :, 128:] = dacc_ref[at : at + slots, 128:].astype(
+            back_ref[index, :, :128] = (dacc_ref[at : at + slots, :128] + packed).astype(NARROW)
+            back_ref[index, :, 128:] = dacc_ref[at : at + slots, 128:].astype(
                 NARROW
             )
 
@@ -371,10 +381,10 @@
     )(me, rows, marked, vec, weight_in, b_in, weight_out, b_out)
 
 
-def weights_body(count, me_ref, vec_ref, in_ref, bin_ref, out_ref, *refs):
-    rows_in, marked_in = refs[:count], refs[count : 2 * count]
-    dout_ref, own_ref = refs[2 * count : 2 * count + 2]
-    others = refs[2 * count + 2 : -5]
+def weights_body(count, me_ref, mark_ref, vec_ref, in_ref, bin_ref, out_ref, *refs):
+    rows_in, marked_in = refs[: count[0]], refs[count[0] : sum(count)]
+    dout_ref, own_ref = refs[sum(count) : sum(count) + 2]
+    others = refs[sum(count) + 2 : -5]
     dbin_ref, dbout_ref, rows_ref, sent_ref, din_ref = refs[-5:]
     width = in_ref.shape[0]
 
@@ -382,12 +392,15 @@
     def _():
         router = vec_ref[8:32, :].astype(NARROW)
         at = 0
+        for rows in rows_in:
+            rows_ref[at : at + rows.shape[0], :] = rows[...]
+            at += rows.shape[0]
+        at = 0
         total = jnp.zeros((1, width), WIDE)
-        for rows, marked in zip(rows_in, marked_in):
-            size = rows.shape[0]
-            gate = slot_gates(rows[...], marked[:, width:], router, me_ref[0])
+        for marked in marked_in:
+            size = marked.shape[0]
+            gate = slot_gates(rows_ref[at : at + size, :], marked[:, width:], router, me_ref[0])
             sent = (gate * marked[:, :width].astype(WIDE)).astype(NARROW)
-            rows_ref[at : at + size, :] = rows[...]
             sent_ref[at : at + size, :] = sent
             total += jnp.sum(sent.astype(WIDE), axis=0, keepdims=True)
             at += size
@@ -405,49 +418,44 @@
         out[...] = din_ref[pl.ds(at, share), :].astype(out.dtype)
 
 
-def expert_weights(me, vec, my_in, my_bias, my_out, rows, marked, groups, chunk):
-    count = len(rows)
-    width, units = my_in.shape
+def expert_weights(me, mark, vec, weight_in, b_in, weight_out, rows, marked, groups, chunk):
+    count = len(rows), len(marked)
+    width, hidden_units = weight_in.shape
+    units = hidden_units // groups
     share = width // groups
+    steps = units // chunk
     total = sum(piece.shape[0] for piece in rows)
-    whole = lambda array: pl.BlockSpec(array.shape, lambda step: (0, 0))
+    whole = lambda array: pl.BlockSpec(array.shape, lambda step, at: (0, 0))
+    wide = lambda size: pl.BlockSpec((size, chunk), lambda step, at: (0, step))
     return pl.pallas_call(
         functools.partial(weights_body, count),
-        grid=(units // chunk,),
-        out_shape=[
-            like((units, width), WIDE),
-            like((share, units), WIDE),
-        ]
+        grid_spec=pltpu.PrefetchScalarGridSpec(
+            num_scalar_prefetch=1,
+            grid=(steps,),
+            in_specs=[
+                pl.BlockSpec(memory_space=pl.ANY),
+                whole(vec),
+                pl.BlockSpec((width, chunk), lambda step, at: (0, at[1] * steps + step)),
+                pl.BlockSpec((1, chunk), lambda step, at: (0, at[1] * steps + step)),
+                pl.BlockSpec((chunk, width), lambda step, at: (at[1] * steps + step, 0)),
+            ]
+            + [whole(piece) for piece in rows + marked],
+            out_specs=[pl.BlockSpec((chunk, width), lambda step, at: (step, 0))]
+            + [wide(share)] * groups
+            + [wide(1), pl.BlockSpec((1, width), lambda step, at: (0, 0))],
+            scratch_shapes=[
+                pltpu.VMEM((total, width), NARROW),
+                pltpu.VMEM((total, width), NARROW),
+                pltpu.VMEM((width, chunk), WIDE),
+            ],
+        ),
+        out_shape=[like((units, width), WIDE), like((share, units), WIDE)]
         + [like((share, units), NARROW)] * (groups - 1)
-        + [
-            like((1, units), WIDE),
-            like((1, width), WIDE),
-        ],
-        in_specs=[
-            SMEM,
-            whole(vec),
-            pl.BlockSpec((width, chunk), lambda step: (0, step)),
-            pl.BlockSpec((1, chunk), lambda step: (0, step)),
-            pl.BlockSpec((chunk, width), lambda step: (step, 0)),
-        ]
-        + [whole(piece) for piece in rows + marked],
-        out_specs=[
-            pl.BlockSpec((chunk, width), lambda step: (step, 0)),
-        ]
-        + [pl.BlockSpec((share, chunk), lambda step: (0, step))] * groups
-        + [
-            pl.BlockSpec((1, chunk), lambda step: (0, step)),
-            pl.BlockSpec((1, width), lambda step: (0, 0)),
-        ],
-        scratch_shapes=[
-            pltpu.VMEM((total, width), NARROW),
-            pltpu.VMEM((total, width), NARROW),
-            pltpu.VMEM((width, chunk), WIDE),
-        ],
+        + [like((1, units), WIDE), like((1, width), WIDE)],
         compiler_params=pltpu.CompilerParams(vmem_limit_bytes=58 * MIB),
         cost_estimate=pl.CostEstimate(flops=1, bytes_accessed=1, transcendentals=0),
         name="expert_weights",
-    )(me, vec, my_in, my_bias, my_out, *rows, *marked)
+    )(me, mark, vec, weight_in, b_in, weight_out, *rows, *marked)
 
 
 def combine_body(experts, spare, *refs):
@@ -571,8 +579,23 @@
         out_ref[base:, place * width : (place + 1) * width] = term
 
 
+def backward_body(experts, spare, *refs):
+    inputs = refs[:8]
+    d_returned_ref, qkv_ref, lse_ref, qkv_weight_ref, x_ref = refs[8:13]
+    gate_ref, dx_ref, all_ref, dret_ref, dh_ref, dctx_ref, sums_ref = refs[13:]
+    vec_ref = refs[3]
+    combine_body(
+        experts, spare, *inputs, d_returned_ref, gate_ref, dh_ref, dctx_ref, sums_ref, dret_ref
+    )
+    back_body(
+        qkv_ref, dctx_ref, lse_ref, qkv_weight_ref, x_ref, vec_ref, dh_ref, sums_ref, dx_ref, all_ref
+    )
+
+
 def outer_body(groups, columns_ref, keep_ref, other_ref, own_d_ref, other_d_ref, own_ref, *refs):
-    outs, turned_ref = refs[:-1], refs[-1]
+    peers = refs[: groups - 1]
+    turned_ref, sems = refs[groups - 1 : groups + 1]
+    outs = refs[groups + 1 :]
     tokens = keep_ref.shape[0]
     width = keep_ref.shape[1]
     half = width // 2
@@ -605,6 +628,14 @@
             outs[index - 1][:, low:high] = total[index * rows : (index + 1) * rows, :].astype(
                 NARROW
             )
+    copies = [
+        pltpu.make_async_copy(out, peer, sems.at[index])
+        for index, (out, peer) in enumerate(zip(outs, peers))
+    ]
+    for copy in copies:
+        copy.start()
+    for copy in copies:
+        copy.wait()
 
 
 def sum_body(count, layers, own_ref, *refs):
@@ -661,27 +692,26 @@
         out_ref[:, pl.ds(at, units)] = ref[...].astype(WIDE)
 
 
-def pack_body(core_ref, qkv_ref, proj_ref, router_ref, vectors_ref, out_ref, mine_ref, mark_ref):
-    share, width = proj_ref.shape
+def pack_body(core_ref, qkv_ref, router_ref, *refs):
+    out_ref, mine_ref = refs[7:]
+    share, width = qkv_ref.shape[0], qkv_ref.shape[1] // 3
     lanes = lax.broadcasted_iota(jnp.int32, (share, share), 1)
     lines = lax.broadcasted_iota(jnp.int32, (share, share), 0)
     places = lax.broadcasted_iota(jnp.int32, (share, 128), 1)
     spread = (
-        lax.broadcasted_iota(jnp.int32, (router_ref.shape[1], 128), 0) + 8
-        == lax.broadcasted_iota(jnp.int32, (router_ref.shape[1], 128), 1)
+        lax.broadcasted_iota(jnp.int32, (router_ref.shape[0], 128), 0) + 8
+        == lax.broadcasted_iota(jnp.int32, (router_ref.shape[0], 128), 1)
     ).astype(NARROW)
-    side = mm(router_ref[...], spread)
-    for index in range(vectors_ref.shape[0]):
-        line = vectors_ref[index : index + 1, :]
+    side = mm_cols(router_ref[...], spread)
+    for index in range(7):
+        line = refs[index][...].astype(WIDE).reshape(1, share)
         column = jnp.sum(jnp.where(lanes == lines, line, 0.0), axis=-1, keepdims=True)
         side = jnp.where(places == index, column, side)
     out_ref[:, : 3 * width] = qkv_ref[...]
-    out_ref[:, 3 * width : 4 * width] = proj_ref[...]
-    out_ref[:, 4 * width :] = side.astype(NARROW)
+    out_ref[:, 3 * width :] = side.astype(NARROW)
     rows = mine_ref.shape[0]
     at = pl.multiple_of(core_ref[0] * rows, 8)
     mine_ref[...] = out_ref[pl.ds(at, rows), :]
-    mark_ref[...] = jnp.zeros_like(mark_ref)
 
 
 def expert_weights_plain(me, vec, my_in, my_bias, my_out, rows, marked):
@@ -733,16 +763,15 @@
     expert_me = lax.axis_index("expert")
     core, layer = expert_me % 2, expert_me // 2
     me = jnp.stack([expert_me, dp_me]).astype(jnp.int32)
-    vectors = jnp.stack([b_q, b_v, b_proj, ln1_gain, ln1_bias, ln2_gain, ln2_bias]).astype(WIDE)
+    vectors = [b_q, b_v, b_proj, ln1_gain, ln1_bias, ln2_gain, ln2_bias]
     wide = 4 * width + 128
-    shard, mine, mark = run(
+    shard, mine = run(
         pack_body,
         [
-            like((share, wide), NARROW),
-            like((share // 2, wide), NARROW),
-            like((16, 128), NARROW),
+            like((share, 3 * width + 128), NARROW),
+            like((share // 2, 3 * width + 128), NARROW),
         ],
-        [core.reshape(1).astype(jnp.int32), w_qkv, w_proj, w_router, vectors],
+        [core.reshape(1).astype(jnp.int32), w_qkv, w_router.T] + vectors,
         0,
         6 * share * wide,
         58,
@@ -750,9 +779,13 @@
         name="pack",
     )
     pieces, starts = gather_shared(shard, mine)
-    d_late, routes, slot_index = after(
-        (d_out, routes, slot_index), swap(mark, "expert", 1)
-    )
+    if groups == 4:
+        later, pieces[3] = lax.optimization_barrier((w_proj, pieces[3]))
+        proj_pieces = [later] + [swap(later, "dp", mask) for mask in range(1, groups)]
+        proj_starts = jnp.stack([(dp_me ^ mask) * share for mask in range(groups)])
+    else:
+        proj_pieces = [lax.all_gather(w_proj, "dp", axis=0, tiled=True)]
+        proj_starts = jnp.zeros((1,), jnp.int32)
     targets = jnp.where(slot_index < capacity, (routes ^ expert_me) * slots + slot_index, -1)
     targets_row = targets.T
     device_targets = jnp.where(slot_index < capacity, routes * slots + slot_index, -1)
@@ -768,30 +801,20 @@
     marked_blocks = run(
         functools.partial(grad_slots_body, experts),
         like((experts, slots, width + 128), NARROW),
-        [d_late, routes, device_targets.T],
+        [d_out, routes, device_targets.T],
         2 * total * tokens * width,
         4 * total * width,
         16,
         name="grad_slots",
+        marks=pieces[1:3],
     )
     marked_blocks = lax.all_to_all(marked_blocks, "expert", 0, 0, tiled=True)
-    marked = run(
-        order_body,
-        like((total, width + 128), NARROW),
-        [me, marked_blocks],
-        total * width,
-        4 * total * width,
-        16,
-        scalars=1,
-        scratch=[pltpu.VMEM((total, width + 128), WIDE)],
-        name="order",
-    )
-
-    full_qkv, full_proj, vec, qkv, context, log_total, keep, give = run(
+    marked = marked_blocks.reshape(total, width + 128)
+
+    full_qkv, vec, qkv, context, log_total, keep, give = run(
         functools.partial(attend_body, len(pieces)),
         [
             like((width, 3 * width), NARROW),
-            like((width, width), NARROW),
             like((32, width), WIDE),
             like((tokens, 3 * width), NARROW),
             like((tokens, width), NARROW),
@@ -808,77 +831,92 @@
         name="attend",
     )
     middle = run(
-        functools.partial(middle_body, experts),
-        [like((tokens, width), WIDE), like((tokens, width), NARROW)]
+        functools.partial(middle_body, experts, len(proj_pieces)),
+        [like((width, width), NARROW), like((tokens, width), WIDE), like((tokens, width), NARROW)]
         + [like((slots, width), NARROW)] * experts,
-        [context, block_input, vec, targets_row, full_proj],
+        [proj_starts.astype(jnp.int32), context, block_input, vec, targets_row] + proj_pieces,
         4 * tokens * width * width,
         4 * width * width,
         58,
+        scalars=1,
         name="middle",
     )
-    hidden, y_in = middle[:2]
-    rows = join(exchange(middle[2:]))
+    full_proj, hidden, y_in = middle[:3]
+    marked, y_in = lax.optimization_barrier((marked, y_in))
     weight_in, weight_out = w_in[0], w_out[0]
+    units = hidden_units // groups
+    arrived, marked_near = lax.optimization_barrier((exchange(middle[3:]), gather_near(marked)))
+    rows = run(
+        order_body,
+        like((total, width), NARROW),
+        [me] + arrived,
+        0,
+        0,
+        16,
+        scalars=1,
+        scratch=[pltpu.VMEM((total, width), WIDE)],
+        name="order",
+    )
     results = expert(
-        me, rows, marked, vec, weight_in, b_in, weight_out, b_out, experts, slots, capacity, 512
+        me, rows, marked, vec, weight_in, b_in, weight_out, b_out, experts, slots, capacity, 1024
     )
     fresh, d_expert_in = results
+    d_expert_in, rows_near, marked_near = lax.optimization_barrier(
+        (d_expert_in, gather_near(rows), marked_near)
+    )
     d_returned = lax.all_to_all(d_expert_in, "expert", 0, 0, tiled=True)
-    other = swap(after(give, fresh), "expert", 1)
-    units = hidden_units // groups
-    my_in, my_out, my_bias = (
-        lax.dynamic_slice_in_dim(array, dp_me * units, units, axis)
-        for array, axis in zip(after((weight_in, weight_out, b_in), y_in), (1, 0, 1))
-    )
-    marked_all = gather_rows(marked, y_in, rows)
-    rows_all = gather_rows(rows, rows, fresh)
-    d_returned, rows_all, marked_all, my_in, my_out, my_bias, other = lax.optimization_barrier(
-        (d_returned, rows_all, marked_all, my_in, my_out, my_bias, other)
-    )
-
-    gates, d_hidden, d_context, early_sums = run(
-        functools.partial(combine_body, experts, capacity),
+    fresh, give = lax.optimization_barrier((fresh, give))
+    other = swap(give, "expert", 1)
+    d_returned, other = lax.optimization_barrier((d_returned, other))
+    rows_all = [rows] + rows_near + gather_far(rows_near)
+    marked_all = [marked] + marked_near + gather_far(marked_near)
+    gates, d_input, d_all = run(
+        functools.partial(backward_body, experts, capacity),
         [
             like((tokens, 128), WIDE),
             like((tokens, width), WIDE),
-            like((tokens, width), NARROW),
-            like((32, width), WIDE),
+            like((240, 4 * width), NARROW),
         ],
-        [hidden, y_in, d_out, vec, full_proj, routes, slot_index, device_targets, d_returned],
-        2 * tokens * total * width + 2 * tokens * width * width,
-        4 * width * width,
-        24,
-        scratch=[pltpu.VMEM((total, width), WIDE)],
-        name="combine",
-    )
-    d_input, d_all = run(
-        back_body,
-        [like((tokens, width), WIDE), like((240, 4 * width), NARROW)],
-        [qkv, d_context, log_total, full_qkv, block_input, vec, d_hidden, early_sums],
-        40 * tokens * 256 * width,
-        8 * tokens * width,
-        32,
-        name="back",
+        [hidden, y_in, d_out, vec, full_proj, routes, slot_index, device_targets, d_returned]
+        + [qkv, log_total, full_qkv, block_input],
+        0,
+        0,
+        58,
+        scratch=[
+            pltpu.VMEM((total, width), WIDE),
+            pltpu.VMEM((tokens, width), WIDE),
+            pltpu.VMEM((tokens, width), NARROW),
+            pltpu.VMEM((32, width), WIDE),
+        ],
+        name="backward",
+    )
+    d_all, fresh, rows_all, marked_all = lax.optimization_barrier(
+        (d_all, fresh, rows_all, marked_all)
     )
     d_other = swap(d_all, "expert", 1)
+    returned = lax.all_to_all(fresh, "expert", 0, 0, tiled=True)
     sums = run(
         functools.partial(outer_body, groups),
         [like((share // 2, wide), WIDE)] + [like((share // 2, wide), NARROW)] * (groups - 1),
         [chosen_columns, keep, other, d_all, d_other],
         4 * tokens * half * wide,
         6 * half * wide,
-        24,
-        scratch=[pltpu.VMEM((128, width), WIDE)],
+        58,
+        scratch=[pltpu.VMEM((128, width), WIDE), pltpu.SemaphoreType.DMA((groups - 1,))]
+        + [pltpu.VMEM((share // 2, wide), NARROW)] * (groups - 1),
+        out_specs=[VMEM] + [pl.BlockSpec(memory_space=pltpu.HBM)] * (groups - 1),
         name="outer",
     )
-    rows_all, marked_all = after((rows_all, marked_all), sums[0])
     if groups == 4:
         grads = expert_weights(
-            me, vec, my_in, my_bias, my_out, rows_all, marked_all, groups, 256
+            me, sums[1], vec, weight_in, b_in, weight_out, rows_all, marked_all, groups, 384
         )
         part_w_out, blocks, (part_b_in, sum_sent) = grads[0], grads[1:-2], grads[-2:]
     else:
+        my_in, my_out, my_bias = (
+            lax.dynamic_slice_in_dim(array, dp_me * units, units, axis)
+            for array, axis in zip((weight_in, weight_out, b_in), (1, 0, 1))
+        )
         part_w_out, d_w_in, part_b_in, sum_sent = expert_weights_plain(
             expert_me, vec, my_in, my_bias, my_out, rows_all, marked_all
         )
@@ -889,8 +927,15 @@
             for mask in range(groups)
         ]
     part_b_out = lax.dynamic_slice_in_dim(sum_sent[0], dp_me * share, share, 0)
-    returned = lax.all_to_all(after(fresh, sums[0]), "expert", 0, 0, tiled=True)
-    returned = after(returned, part_b_in)
+    sums = [sums[0]] + [swap(sums[mask], "dp", mask) for mask in range(1, groups)]
+    sums, part_b_in, part_b_out, returned = lax.optimization_barrier(
+        (sums, part_b_in, part_b_out, returned)
+    )
+    sums = sum_blocks(sums[0], sums[1:], layers, WIDE)
+    sums, blocks = lax.optimization_barrier((sums, blocks))
+    sums = [sums[0]] + [swap(sums[mask], "expert", 2 * mask) for mask in range(1, layers)]
+    blocks = [blocks[0]] + [swap(blocks[mask], "dp", mask) for mask in range(1, groups)]
+    done = sum_blocks(sums[0], sums[1:], 1, NARROW)[0]
     block_out = run(
         output_body,
         like((tokens, width), NARROW),
@@ -900,17 +945,8 @@
         24,
         scratch=[pltpu.VMEM((total, width), WIDE)],
         name="output",
-    )
-    sums = [sums[0]] + [swap(sums[mask], "dp", mask) for mask in range(1, groups)]
-    sums, block_out, part_b_in, part_b_out = lax.optimization_barrier(
-        (sums, block_out, part_b_in, part_b_out)
-    )
-    sums = sum_blocks(sums[0], sums[1:], layers, WIDE)
-    blocks = [blocks[0]] + [
-        swap(after(blocks[mask], sums[0]), "dp", mask) for mask in range(1, groups)
-    ]
-    sums = [sums[0]] + [swap(sums[mask], "expert", 2 * mask) for mask in range(1, layers)]
-    done = sum_blocks(sums[0], sums[1:], 1, NARROW)[0]
+        marks=[done],
+    )
     if groups == 4:
         part_w_in = run(
             spread_body,
@@ -921,11 +957,14 @@
             24,
             scalars=1,
             name="spread",
+            marks=[done],
         )
     else:
         part_w_in = in_order([block.astype(WIDE) for block in blocks], dp_me, 1)
     done_pieces = [done] + [swap(done, "expert", 2 * mask) for mask in range(1, layers)]
-    done_pieces, part_w_in = lax.optimization_barrier((done_pieces, part_w_in))
+    done_pieces, part_w_in, block_out = lax.optimization_barrier(
+        (done_pieces, part_w_in, block_out)
+    )
     low = join(done_pieces)
     high = swap(low, "expert", 1)
 

time: 224 us -> 216 us (0.964)
  local copies, waits for them, and re-layouts: 30 us -> 14.9 us
  Pallas kernels: 67.3 us -> 72.9 us
  waiting for transfers between devices: 64.7 us -> 62 us
  starting transfers between devices: 58.9 us -> 61.4 us
    ppermute x38 -> x41, waiting for transfers between devices: 64.7 us -> 51.1 us  [swap(): lax.ppermute(values, axis, [(index, index ^ mask) for index in range(size)])]
    all_to_all x1, waiting for transfers between devices: 0.01 us -> 10.9 us  [per_device(): d_returned = lax.all_to_all(d_expert_in, 'expert', 0, 0, tiled=True)]
    pallas_call x16 -> x14, Pallas kernels: 52 us -> 58.5 us  [the longest x13 39.6 us: run(): pl.pallas_call(marked_body, out_shape=outs, in_specs=[SMEM] * scalars + [...]
    another operation x8 -> x0, local copies, waits for them, and re-layouts: 4.67 us -> none  [per_device(): jnp.stack([b_q, b_v, b_proj, ln1_gain, ln1_bias, ln2_gain, ln2_bias])]
    ppermute x38 -> x41, starting transfers between devices: 42 us -> 46.6 us  [swap(): lax.ppermute(values, axis, [(index, index ^ mask) for index in range(size)])]
    dynamic_slice x2 -> x0, local copies, waits for them, and re-layouts: 4.61 us -> none  [per_device(): lax.dynamic_slice_in_dim(array, dp_me * units, units, axis)]
    slice x4, local copies, waits for them, and re-layouts: 5.14 us -> 1.84 us  [gather_far(): return [swap(one[:half], 'dp', 2), swap(two[half:], 'dp', 1)]]
    unnamed x68 -> x67, local copies, waits for them, and re-layouts: 9.38 us -> 8.52 us
  transfers between devices with their start and end apart: 41 -> 44, of which waited for: 14 -> 20; matrix products, arithmetic and copies ran while one was open for 8% -> 5% of each run, Pallas kernels for 22% -> 30%
where the time goes in v4:
time: 216 us; the launch traced here: 215 us
  Pallas kernels  72.9 us (34%)
  waiting for transfers between devices  62 us (29%)
  starting transfers between devices  61.4 us (28%)
  local copies, waits for them, and re-layouts  14.9 us (7%)
  other arithmetic  2.89 us (1%)
    ppermute x41, waiting for transfers between devices, swap(): lax.ppermute(values, axis, [(index, index ^ mask) for index in range(size)])  51.1 us
    ppermute x41, starting transfers between devices, swap(): lax.ppermute(values, axis, [(index, index ^ mask) for index in range(size)])  46.6 us
    pallas_call x13, Pallas kernels, run(): pl.pallas_call(marked_body, out_shape=outs, in_specs=[SMEM] * scalars + [...  39.6 us
    pallas_call x1, Pallas kernels, expert_weights(): pl.pallas_call(functools.partial(weights_body, count), grid_spec=pltpu.Pr...  19 us
    pallas_call x1, Pallas kernels, expert(): pl.pallas_call(functools.partial(expert_body, experts, spare), grid=(hidd...  14.4 us
    all_to_all x1, waiting for transfers between devices, per_device(): d_returned = lax.all_to_all(d_expert_in, 'expert', 0, 0, tiled=True)  10.9 us
    unnamed x67, local copies, waits for them, and re-layouts  8.52 us
    all_to_all x1, starting transfers between devices, per_device(): d_returned = lax.all_to_all(d_expert_in, 'expert', 0, 0, tiled=True)  6.12 us
  transfers between devices with their start and end apart: 44, of which 20 were waited for; matrix products, arithmetic and copies ran while one was open for 5% of the time, Pallas kernels for 30%

profile of v4, /device:TPU:0, one launch (start us, length us, event | category | flops | bytes accessed | tf_op | source)
XLA Modules:
  0.0 215.2 jit_solution(15160153726547617352)
XLA Ops:
  0.7 2.6 %pack.1 = (bf16[192,2432]{1,0:T(8,128)(2,1)}, bf16[96,2432]{1,0:T(8,128)(2,1)}) custom-call(s32[1]{0:T(128)} %bitcast.9.refs_0_, bf16[192,2304]{1,0:T(8,128)(2,1)} %refs_1_.3, bf16[8,192]{1,0:T(8,128)(2,1)} %bitcast.43, bf16[192]{0:T(256)(128)(2,1)} %refs_3_.1, bf16[192]{0:T(256)(128)(2,1)} %refs_4_.1, bf16[192]{0:T(256)(128)(2,1)} %refs_5_.2, ...), custom_call_target="tpu_custom_call" | custom-call | flops 1 | bytes 1 | tf_op jit(solution)/shard_map/pack/pallas_call | solution.py:123
  3.3 3.0 %collective-permute-start.1 = (bf16[96,2432]{1,0:T(8,128)(2,1)}, bf16[96,2432]{1,0:T(8,128)(2,1)S(1)}, u32[]{:S(2)}, u32[]{:S(2)}) collective-permute-start(bf16[96,2432]{1,0:T(8,128)(2,1)} %get-tuple-element.123), channel_id=1, source_target_pairs={{0,16},{8,24},{16,0},{24,8},{1,17},{9,25},{17,1},{25,9},{2,18},{10... | collective-permute-start | bytes 1400840 | tf_op jit(solution)/shard_map/ppermute | solution.py:45
  12.1 5.1 %collective-permute-done.1.refs_5_.refs_4_ = bf16[96,2432]{1,0:T(8,128)(2,1)S(1)} collective-permute-done((bf16[96,2432]{1,0:T(8,128)(2,1)}, bf16[96,2432]{1,0:T(8,128)(2,1)S(1)}, u32[]{:S(2)}, u32[]{:S(2)}) %collective-permute-start.1) | collective-permute-done | bytes 466976 | tf_op jit(solution)/shard_map/ppermute | solution.py:45
  20.1 4.9 %all-to-all-start = ((bf16[8,56,896]{2,1,0:T(8,128)(2,1)}), bf16[8,56,896]{2,1,0:T(8,128)(2,1)S(1)}, u32[]{:S(2)}, u32[]{:S(2)}) async-start(bf16[8,56,896]{2,1,0:T(8,128)(2,1)} %grad_slots.1), calls=%async_computation | async-start | bytes 1605632 | tf_op jit(solution)/shard_map/all_to_all | solution.py:811
  28.0 5.3 %collective-permute-done.3.refs_7_ = bf16[48,2432]{1,0:T(8,128)(2,1)} collective-permute-done((bf16[48,2432]{1,0:T(8,128)(2,1)S(1)}, bf16[48,2432]{1,0:T(8,128)(2,1)}, u32[]{:S(2)}, u32[]{:S(2)}) %collective-permute-start.3) | collective-permute-done | bytes 233504 | tf_op jit(solution)/shard_map/ppermute | solution.py:45
  42.6 6.7 %attend.1 = (bf16[768,2304]{1,0:T(8,128)(2,1)}, f32[32,768]{1,0:T(8,128)}, bf16[197,2304]{1,0:T(8,128)(2,1)}, bf16[197,768]{1,0:T(8,128)(2,1)}, f32[197,128]{1,0...) custom-call(s32[9]{0:T(128)} %stack.66.refs_0_, bf16[197,768]{1,0:T(8,128)(2,1)} %refs_12_.1, ...), custom_call_target="tpu_custom_call" | custom-call | flops 1 | bytes 1 | tf_op jit(solution)/shard_map/attend/pallas_call | solution.py:123
  50.7 3.3 %middle.1 = (bf16[768,768]{1,0:T(8,128)(2,1)}, f32[197,768]{1,0:T(8,128)}, bf16[197,768]{1,0:T(8,128)(2,1)}, bf16[56,768]{1,0:T(8,128)(2,1)}, bf16[56,768]{1,0:T...) custom-call(s32[4]{0:T(128)} %pad_add_fusion.3.refs_0_, ...), custom_call_target="tpu_custom_call" | custom-call | flops 1 | bytes 1 | tf_op jit(solution)/shard_map/middle/pallas_call | solution.py:123
  56.0 2.3 %collective-permute-start.12 = (bf16[56,768]{1,0:T(8,128)(2,1)}, bf16[56,768]{1,0:T(8,128)(2,1)S(1)}, u32[]{:S(2)}, u32[]{:S(2)}) collective-permute-start(bf16[56,768]{1,0:T(8,128)(2,1)} %get-tuple-element.131), channel_id=1, source_target_pairs={{0,2},{1,3},{2,0},{3,1},{4,6},{5,7},{6,4},{7,5},{8,10},{9,11},{10,... | collective-permute-start | bytes 258056 | tf_op jit(solution)/shard_map/ppermute | solution.py:45
  58.4 2.6 %collective-permute-start.14 = (bf16[56,768]{1,0:T(8,128)(2,1)}, bf16[56,768]{1,0:T(8,128)(2,1)S(1)}, u32[]{:S(2)}, u32[]{:S(2)}) collective-permute-start(bf16[56,768]{1,0:T(8,128)(2,1)} %get-tuple-element.133), channel_id=1, source_target_pairs={{0,4},{1,5},{2,6},{3,7},{4,0},{5,1},{6,2},{7,3},{8,12},{9,13},{10,... | collective-permute-start | bytes 258056 | tf_op jit(solution)/shard_map/ppermute | solution.py:45
  65.1 2.8 %collective-permute-start.16 = (bf16[56,768]{1,0:T(8,128)(2,1)}, bf16[56,768]{1,0:T(8,128)(2,1)S(1)}, u32[]{:S(2)}, u32[]{:S(2)}) collective-permute-start(bf16[56,768]{1,0:T(8,128)(2,1)} %get-tuple-element.135), channel_id=1, source_target_pairs={{0,6},{1,7},{2,4},{3,5},{4,2},{5,3},{6,0},{7,1},{8,14},{9,15},{10,... | collective-permute-start | bytes 258056 | tf_op jit(solution)/shard_map/ppermute | solution.py:45
  68.7 4.1 %collective-permute-done.15.refs_6_ = bf16[56,768]{1,0:T(8,128)(2,1)S(1)} collective-permute-done((bf16[56,768]{1,0:T(8,128)(2,1)}, bf16[56,768]{1,0:T(8,128)(2,1)S(1)}, u32[]{:S(2)}, u32[]{:S(2)}) %collective-permute-start.15) | collective-permute-done | bytes 86048 | tf_op jit(solution)/shard_map/ppermute | solution.py:45
  78.7 14.4 %expert.1 = (bf16[8,56,768]{2,1,0:T(8,128)(2,1)}, bf16[8,56,768]{2,1,0:T(8,128)(2,1)}) custom-call(s32[2]{0:T(128)} %copy-done.12, bf16[448,768]{1,0:T(8,128)(2,1)} %copy-done, bf16[448,896]{1,0:T(8,128)(2,1)} %bitcast.40, f32[32,768]{1,0:T(8,128)} %get-tuple-element.127.refs_3_.vec_ref, bf16[768,3072]{1,0:T(8,128)(2,1)} %bitcast.34, ...), custom_call_target="tpu_custom_call" | custom-call | flops 1 | bytes 1 | tf_op jit(solution)/shard_map/expert/pallas_call | solution.py:358
  96.0 6.1 %all-to-all-start.1 = ((bf16[8,56,768]{2,1,0:T(8,128)(2,1)}), bf16[8,56,768]{2,1,0:T(8,128)(2,1)S(1)}, u32[]{:S(2)}, u32[]{:S(2)}) async-start(bf16[8,56,768]{2,1,0:T(8,128)(2,1)} %get-tuple-element.150), calls=%async_computation.1 | async-start | bytes 1376256 | tf_op jit(solution)/shard_map/all_to_all | solution.py:867
  110.0 10.9 %all-to-all-done.1.refs_8_ = bf16[8,56,768]{2,1,0:T(8,128)(2,1)S(1)} async-done(((bf16[8,56,768]{2,1,0:T(8,128)(2,1)}), bf16[8,56,768]{2,1,0:T(8,128)(2,1)S(1)}, u32[]{:S(2)}, u32[]{:S(2)}) %all-to-all-start.1) | async-done | bytes 688160 | tf_op jit(solution)/shard_map/all_to_all | solution.py:867
  121.8 11.8 %backward.1 = (f32[197,128]{1,0:T(8,128)}, f32[197,768]{1,0:T(8,128)}, bf16[240,3072]{1,0:T(8,128)(2,1)}) custom-call(f32[197,768]{1,0:T(8,128)} %get-tuple-element.155.refs_0_, bf16[197,768]{1,0:T(8,128)(2,1)} %get-tuple-element.156.refs_1_, bf16[197,768]{1,0:T(8,128)(2,1)} %refs_2_.3, f32[32,768]{1,0:T(8,128)} %get-tuple-element.127.refs_3_.vec_ref, ...), custom_call_target="tpu_custom_call" | custom-call | flops 1 | bytes 1 | tf_op jit(solution)/shard_map/backward/pallas_call | solution.py:123
  135.2 3.8 %all-to-all-start.2 = ((bf16[8,56,768]{2,1,0:T(8,128)(2,1)}), bf16[8,56,768]{2,1,0:T(8,128)(2,1)S(1)}, u32[]{:S(2)}, u32[]{:S(2)}) async-start(bf16[8,56,768]{2,1,0:T(8,128)(2,1)} %get-tuple-element.185), calls=%async_computation.2 | async-start | bytes 1376256 | tf_op jit(solution)/shard_map/all_to_all | solution.py:897
  140.1 5.8 %outer.1 = (f32[96,3200]{1,0:T(8,128)}, bf16[96,3200]{1,0:T(8,128)(2,1)}, bf16[96,3200]{1,0:T(8,128)(2,1)}, bf16[96,3200]{1,0:T(8,128)(2,1)}) custom-call(s32[1,768]{1,0:T(1,128)} %broadcast_in_dim.17.refs_2_.refs_0_, bf16[197,768]{1,0:T(8,128)(2,1)} %get-tuple-element.125.refs_1_, bf16[197,768]{1,0:T(8,128)(2,1)} %collective-permute-done.22.refs_2_, ...), custom_call_target="tpu_custom_call" | custom-call | flops 1 | bytes 1 | tf_op jit(solution)/shard_map/outer/pallas_call | solution.py:123
  149.5 19.0 %expert_weights.1 = (f32[768,768]{1,0:T(8,128)}, f32[192,768]{1,0:T(8,128)}, bf16[192,768]{1,0:T(8,128)(2,1)}, bf16[192,768]{1,0:T(8,128)(2,1)}, bf16[192,768]{1...) custom-call(s32[2]{0:T(128)} %copy-done.12, bf16[96,3200]{1,0:T(8,128)(2,1)} %get-tuple-element.170.mark_ref, ...), custom_call_target="tpu_custom_call" | custom-call | flops 1 | bytes 1 | tf_op jit(solution)/shard_map/expert_weights/pallas_call | solution.py:430
  169.9 5.7 %collective-permute-done.29.refs_2_ = bf16[96,3200]{1,0:T(8,128)(2,1)S(1)} collective-permute-done((bf16[96,3200]{1,0:T(8,128)(2,1)}, bf16[96,3200]{1,0:T(8,128)(2,1)S(1)}, u32[]{:S(2)}, u32[]{:S(2)}) %collective-permute-start.29) | collective-permute-done | bytes 614432 | tf_op jit(solution)/shard_map/ppermute | solution.py:45
  180.8 2.4 %collective-permute-start.32 = (bf16[24,3200]{1,0:T(8,128)(2,1)S(1)}, bf16[24,3200]{1,0:T(8,128)(2,1)S(1)}, u32[]{:S(2)}, u32[]{:S(2)}) collective-permute-start(bf16[24,3200]{1,0:T(8,128)(2,1)S(1)} %get-tuple-element.200), channel_id=1, source_target_pairs={{0,4},{1,5},{2,6},{3,7},{4,0},{5,1},{6,2},{7,3},{8,12},{9,13},{10,... | collective-permute-start | bytes 460808 | tf_op jit(solution)/shard_map/ppermute | solution.py:45
  187.2 7.0 %collective-permute-done.32.refs_2_ = bf16[24,3200]{1,0:T(8,128)(2,1)S(1)} collective-permute-done((bf16[24,3200]{1,0:T(8,128)(2,1)S(1)}, bf16[24,3200]{1,0:T(8,128)(2,1)S(1)}, u32[]{:S(2)}, u32[]{:S(2)}) %collective-permute-start.32) | collective-permute-done | bytes 153632 | tf_op jit(solution)/shard_map/ppermute | solution.py:45
  194.3 2.5 %collective-permute-start.36 = (bf16[24,3200]{1,0:T(8,128)(2,1)S(1)}, bf16[24,3200]{1,0:T(8,128)(2,1)S(1)}, u32[]{:S(2)}, u32[]{:S(2)}) collective-permute-start(bf16[24,3200]{1,0:T(8,128)(2,1)S(1)} %sum_blocks.3.refs_5_.refs_4_.refs_0_), channel_id=1, source_target_pairs={{0,6},{1,7},{2,4},{3,5},{4,2},{5,3},{6,0},{7,1},{8,14},{9,15},{10,... | collective-permute-start | bytes 460808 | tf_op jit(solution)/shard_map/ppermute | solution.py:45
  196.8 2.9 %collective-permute-start.35 = (bf16[24,3200]{1,0:T(8,128)(2,1)S(1)}, bf16[24,3200]{1,0:T(8,128)(2,1)S(1)}, u32[]{:S(2)}, u32[]{:S(2)}) collective-permute-start(bf16[24,3200]{1,0:T(8,128)(2,1)S(1)} %sum_blocks.3.refs_5_.refs_4_.refs_0_), channel_id=1, source_target_pairs={{0,4},{1,5},{2,6},{3,7},{4,0},{5,1},{6,2},{7,3},{8,12},{9,13},{10,... | collective-permute-start | bytes 460808 | tf_op jit(solution)/shard_map/ppermute | solution.py:45
  203.2 7.2 %collective-permute-done.35.refs_2_ = bf16[24,3200]{1,0:T(8,128)(2,1)S(1)} collective-permute-done((bf16[24,3200]{1,0:T(8,128)(2,1)S(1)}, bf16[24,3200]{1,0:T(8,128)(2,1)S(1)}, u32[]{:S(2)}, u32[]{:S(2)}) %collective-permute-start.35) | collective-permute-done | bytes 153632 | tf_op jit(solution)/shard_map/ppermute | solution.py:45
  (174 shorter events, 71.9 us)
Async XLA Ops:
  3.3 13.9 %collective-permute-start.1 = (bf16[96,2432]{1,0:T(8,128)(2,1)}, bf16[96,2432]{1,0:T(8,128)(2,1)S(1)}, u32[]{:S(2)}, u32[]{:S(2)}) collective-permute-start(bf16[96,2432]{1,0:T(8,128)(2,1)} %get-tuple-element.123), channel_id=1, source_target_pairs={{0,16},{8,24},{16,0},{24,8},{1,17},{9,25},{17,1},{25,9},{2,18},{10... | collective-permute-start | bytes 1400840 | tf_op jit(solution)/shard_map/ppermute | solution.py:45
  20.1 34.0 %all-to-all-start = ((bf16[8,56,896]{2,1,0:T(8,128)(2,1)}), bf16[8,56,896]{2,1,0:T(8,128)(2,1)S(1)}, u32[]{:S(2)}, u32[]{:S(2)}) async-start(bf16[8,56,896]{2,1,0:T(8,128)(2,1)} %grad_slots.1), calls=%async_computation | async-start | bytes 1605632 | tf_op jit(solution)/shard_map/all_to_all | solution.py:811
  26.6 12.6 %collective-permute-start.5 = (bf16[96,2432]{1,0:T(8,128)(2,1)S(1)}, bf16[96,2432]{1,0:T(8,128)(2,1)S(1)}, u32[]{:S(2)}, u32[]{:S(2)}) collective-permute-start(bf16[96,2432]{1,0:T(8,128)(2,1)S(1)} %collective-permute-done.1.refs_5_.refs_4_), channel_id=1, source_target_pairs={{0,1},{1,0},{2,3},{3,2},{4,5},{5,4},{6,7},{7,6},{8,9},{9,8},{10,11... | collective-permute-start | bytes 1400840 | tf_op jit(solution)/shard_map/ppermute | solution.py:45
  35.7 13.6 %collective-permute-start.10 = (bf16[192,768]{1,0:T(8,128)(2,1)S(1)}, bf16[192,768]{1,0:T(8,128)(2,1)S(1)}, u32[]{:S(2)}, u32[]{:S(2)}) collective-permute-start(bf16[192,768]{1,0:T(8,128)(2,1)S(1)} %copy-done.26), channel_id=1, source_target_pairs={{0,24},{8,16},{16,8},{24,0},{1,25},{9,17},{17,9},{25,1},{2,26},{10... | collective-permute-start | bytes 884744 | tf_op jit(solution)/shard_map/ppermute | solution.py:45
  36.2 14.5 %collective-permute-start.9 = (bf16[192,768]{1,0:T(8,128)(2,1)S(1)}, bf16[192,768]{1,0:T(8,128)(2,1)}, u32[]{:S(2)}, u32[]{:S(2)}) collective-permute-start(bf16[192,768]{1,0:T(8,128)(2,1)S(1)} %copy-done.26), channel_id=1, source_target_pairs={{0,16},{8,24},{16,0},{24,8},{1,17},{9,25},{17,1},{25,9},{2,18},{10... | collective-permute-start | bytes 884744 | tf_op jit(solution)/shard_map/ppermute | solution.py:45
  37.7 13.0 %collective-permute-start.8 = (bf16[192,768]{1,0:T(8,128)(2,1)S(1)}, bf16[192,768]{1,0:T(8,128)(2,1)}, u32[]{:S(2)}, u32[]{:S(2)}) collective-permute-start(bf16[192,768]{1,0:T(8,128)(2,1)S(1)} %copy-done.26), channel_id=1, source_target_pairs={{0,8},{8,0},{16,24},{24,16},{1,9},{9,1},{17,25},{25,17},{2,10},{10... | collective-permute-start | bytes 884744 | tf_op jit(solution)/shard_map/ppermute | solution.py:45
  54.1 20.3 %collective-permute-start.19 = (bf16[448,896]{1,0:T(8,128)(2,1)S(1)}, bf16[448,896]{1,0:T(8,128)(2,1)S(1)}, u32[]{:S(2)}, u32[]{:S(2)}) collective-permute-start(bf16[448,896]{1,0:T(8,128)(2,1)S(1)} %bitcast.38), channel_id=1, source_target_pairs={{0,16},{8,24},{16,0},{24,8},{1,17},{9,25},{17,1},{25,9},{2,18},{10... | collective-permute-start | bytes 2408456 | tf_op jit(solution)/shard_map/ppermute | solution.py:45
  55.5 19.4 %collective-permute-start.18 = (bf16[448,896]{1,0:T(8,128)(2,1)S(1)}, bf16[448,896]{1,0:T(8,128)(2,1)S(1)}, u32[]{:S(2)}, u32[]{:S(2)}) collective-permute-start(bf16[448,896]{1,0:T(8,128)(2,1)S(1)} %bitcast.39), channel_id=1, source_target_pairs={{0,8},{8,0},{16,24},{24,16},{1,9},{9,1},{17,25},{25,17},{2,10},{10... | collective-permute-start | bytes 2408456 | tf_op jit(solution)/shard_map/ppermute | solution.py:45
  76.6 17.3 %collective-permute-start.21 = (bf16[448,768]{1,0:T(8,128)(2,1)S(1)}, bf16[448,768]{1,0:T(8,128)(2,1)S(1)}, u32[]{:S(2)}, u32[]{:S(2)}) collective-permute-start(bf16[448,768]{1,0:T(8,128)(2,1)S(1)} %order.1.rows_ref.refs_0_), channel_id=1, source_target_pairs={{0,16},{8,24},{16,0},{24,8},{1,17},{9,25},{17,1},{25,9},{2,18},{10... | collective-permute-start | bytes 2064392 | tf_op jit(solution)/shard_map/ppermute | solution.py:45
  77.6 17.4 %collective-permute-start.20 = (bf16[448,768]{1,0:T(8,128)(2,1)S(1)}, bf16[448,768]{1,0:T(8,128)(2,1)S(1)}, u32[]{:S(2)}, u32[]{:S(2)}) collective-permute-start(bf16[448,768]{1,0:T(8,128)(2,1)S(1)} %order.1.rows_ref.refs_0_), channel_id=1, source_target_pairs={{0,8},{8,0},{16,24},{24,16},{1,9},{9,1},{17,25},{25,17},{2,10},{10... | collective-permute-start | bytes 2064392 | tf_op jit(solution)/shard_map/ppermute | solution.py:45
  96.0 25.0 %all-to-all-start.1 = ((bf16[8,56,768]{2,1,0:T(8,128)(2,1)}), bf16[8,56,768]{2,1,0:T(8,128)(2,1)S(1)}, u32[]{:S(2)}, u32[]{:S(2)}) async-start(bf16[8,56,768]{2,1,0:T(8,128)(2,1)} %get-tuple-element.150), calls=%async_computation.1 | async-start | bytes 1376256 | tf_op jit(solution)/shard_map/all_to_all | solution.py:867
  102.9 30.7 %collective-permute-start.26 = (bf16[224,896]{1,0:T(8,128)(2,1)}, bf16[224,896]{1,0:T(8,128)(2,1)S(1)}, u32[]{:S(2)}, u32[]{:S(2)}) collective-permute-start(bf16[224,896]{1,0:T(8,128)(2,1)} %slice.23), channel_id=1, source_target_pairs={{0,8},{8,0},{16,24},{24,16},{1,9},{9,1},{17,25},{25,17},{2,10},{10... | collective-permute-start | bytes 1204232 | tf_op jit(solution)/shard_map/ppermute | solution.py:45
  103.7 30.0 %collective-permute-start.25 = (bf16[224,896]{1,0:T(8,128)(2,1)S(1)}, bf16[224,896]{1,0:T(8,128)(2,1)S(1)}, u32[]{:S(2)}, u32[]{:S(2)}) collective-permute-start(bf16[224,896]{1,0:T(8,128)(2,1)S(1)} %slice.22), channel_id=1, source_target_pairs={{0,16},{8,24},{16,0},{24,8},{1,17},{9,25},{17,1},{25,9},{2,18},{10... | collective-permute-start | bytes 1204232 | tf_op jit(solution)/shard_map/ppermute | solution.py:45
  106.1 27.6 %collective-permute-start.24 = (bf16[224,768]{1,0:T(8,128)(2,1)S(1)}, bf16[224,768]{1,0:T(8,128)(2,1)}, u32[]{:S(2)}, u32[]{:S(2)}) collective-permute-start(bf16[224,768]{1,0:T(8,128)(2,1)S(1)} %slice.21), channel_id=1, source_target_pairs={{0,8},{8,0},{16,24},{24,16},{1,9},{9,1},{17,25},{25,17},{2,10},{10... | collective-permute-start | bytes 1032200 | tf_op jit(solution)/shard_map/ppermute | solution.py:45
  106.6 27.0 %collective-permute-start.23 = (bf16[224,768]{1,0:T(8,128)(2,1)S(1)}, bf16[224,768]{1,0:T(8,128)(2,1)}, u32[]{:S(2)}, u32[]{:S(2)}) collective-permute-start(bf16[224,768]{1,0:T(8,128)(2,1)S(1)} %slice.20), channel_id=1, source_target_pairs={{0,16},{8,24},{16,0},{24,8},{1,17},{9,25},{17,1},{25,9},{2,18},{10... | collective-permute-start | bytes 1032200 | tf_op jit(solution)/shard_map/ppermute | solution.py:45
  135.2 34.7 %all-to-all-start.2 = ((bf16[8,56,768]{2,1,0:T(8,128)(2,1)}), bf16[8,56,768]{2,1,0:T(8,128)(2,1)S(1)}, u32[]{:S(2)}, u32[]{:S(2)}) async-start(bf16[8,56,768]{2,1,0:T(8,128)(2,1)} %get-tuple-element.185), calls=%async_computation.2 | async-start | bytes 1376256 | tf_op jit(solution)/shard_map/all_to_all | solution.py:897
  145.9 29.7 %collective-permute-start.29 = (bf16[96,3200]{1,0:T(8,128)(2,1)}, bf16[96,3200]{1,0:T(8,128)(2,1)S(1)}, u32[]{:S(2)}, u32[]{:S(2)}) collective-permute-start(bf16[96,3200]{1,0:T(8,128)(2,1)} %get-tuple-element.171), channel_id=1, source_target_pairs={{0,16},{8,24},{16,0},{24,8},{1,17},{9,25},{17,1},{25,9},{2,18},{10... | collective-permute-start | bytes 1843208 | tf_op jit(solution)/shard_map/ppermute | solution.py:45
  146.6 29.0 %collective-permute-start.30 = (bf16[96,3200]{1,0:T(8,128)(2,1)}, bf16[96,3200]{1,0:T(8,128)(2,1)}, u32[]{:S(2)}, u32[]{:S(2)}) collective-permute-start(bf16[96,3200]{1,0:T(8,128)(2,1)} %get-tuple-element.172), channel_id=1, source_target_pairs={{0,24},{8,16},{16,8},{24,0},{1,25},{9,17},{17,9},{25,1},{2,26},{10... | collective-permute-start | bytes 1843208 | tf_op jit(solution)/shard_map/ppermute | solution.py:45
  148.2 28.7 %collective-permute-start.28 = (bf16[96,3200]{1,0:T(8,128)(2,1)}, bf16[96,3200]{1,0:T(8,128)(2,1)}, u32[]{:S(2)}, u32[]{:S(2)}) collective-permute-start(bf16[96,3200]{1,0:T(8,128)(2,1)} %get-tuple-element.170.mark_ref), channel_id=1, source_target_pairs={{0,8},{8,0},{16,24},{24,16},{1,9},{9,1},{17,25},{25,17},{2,10},{10... | collective-permute-start | bytes 1843208 | tf_op jit(solution)/shard_map/ppermute | solution.py:45
  180.0 19.8 %collective-permute-start.37 = (bf16[192,768]{1,0:T(8,128)(2,1)S(1)}, bf16[192,768]{1,0:T(8,128)(2,1)S(1)}, u32[]{:S(2)}, u32[]{:S(2)}) collective-permute-start(bf16[192,768]{1,0:T(8,128)(2,1)S(1)} %copy-done.31), channel_id=1, source_target_pairs={{0,8},{8,0},{16,24},{24,16},{1,9},{9,1},{17,25},{25,17},{2,10},{10... | collective-permute-start | bytes 884744 | tf_op jit(solution)/shard_map/ppermute | solution.py:45
  180.8 13.4 %collective-permute-start.32 = (bf16[24,3200]{1,0:T(8,128)(2,1)S(1)}, bf16[24,3200]{1,0:T(8,128)(2,1)S(1)}, u32[]{:S(2)}, u32[]{:S(2)}) collective-permute-start(bf16[24,3200]{1,0:T(8,128)(2,1)S(1)} %get-tuple-element.200), channel_id=1, source_target_pairs={{0,4},{1,5},{2,6},{3,7},{4,0},{5,1},{6,2},{7,3},{8,12},{9,13},{10,... | collective-permute-start | bytes 460808 | tf_op jit(solution)/shard_map/ppermute | solution.py:45
  183.8 17.3 %collective-permute-start.38 = (bf16[192,768]{1,0:T(8,128)(2,1)S(1)}, bf16[192,768]{1,0:T(8,128)(2,1)S(1)}, u32[]{:S(2)}, u32[]{:S(2)}) collective-permute-start(bf16[192,768]{1,0:T(8,128)(2,1)S(1)} %copy-done.30), channel_id=1, source_target_pairs={{0,16},{8,24},{16,0},{24,8},{1,17},{9,25},{17,1},{25,9},{2,18},{10... | collective-permute-start | bytes 884744 | tf_op jit(solution)/shard_map/ppermute | solution.py:45
  185.5 15.6 %collective-permute-start.39 = (bf16[192,768]{1,0:T(8,128)(2,1)S(1)}, bf16[192,768]{1,0:T(8,128)(2,1)S(1)}, u32[]{:S(2)}, u32[]{:S(2)}) collective-permute-start(bf16[192,768]{1,0:T(8,128)(2,1)S(1)} %copy-done.29), channel_id=1, source_target_pairs={{0,24},{8,16},{16,8},{24,0},{1,25},{9,17},{17,9},{25,1},{2,26},{10... | collective-permute-start | bytes 884744 | tf_op jit(solution)/shard_map/ppermute | solution.py:45
  196.8 13.6 %collective-permute-start.35 = (bf16[24,3200]{1,0:T(8,128)(2,1)S(1)}, bf16[24,3200]{1,0:T(8,128)(2,1)S(1)}, u32[]{:S(2)}, u32[]{:S(2)}) collective-permute-start(bf16[24,3200]{1,0:T(8,128)(2,1)S(1)} %sum_blocks.3.refs_5_.refs_4_.refs_0_), channel_id=1, source_target_pairs={{0,4},{1,5},{2,6},{3,7},{4,0},{5,1},{6,2},{7,3},{8,12},{9,13},{10,... | collective-permute-start | bytes 460808 | tf_op jit(solution)/shard_map/ppermute | solution.py:45
  (52 other events, 600.2 us)

commit v5 on v4

--- a/solution.py
+++ b/solution.py
@@ -779,10 +779,11 @@
         name="pack",
     )
     pieces, starts = gather_shared(shard, mine)
+    starts = jnp.stack(starts).astype(jnp.int32)
     if groups == 4:
         later, pieces[3] = lax.optimization_barrier((w_proj, pieces[3]))
         proj_pieces = [later] + [swap(later, "dp", mask) for mask in range(1, groups)]
-        proj_starts = jnp.stack([(dp_me ^ mask) * share for mask in range(groups)])
+        proj_starts = (jnp.arange(groups, dtype=jnp.int32) ^ dp_me) * share
     else:
         proj_pieces = [lax.all_gather(w_proj, "dp", axis=0, tiled=True)]
         proj_starts = jnp.zeros((1,), jnp.int32)
@@ -806,7 +807,7 @@
         4 * total * width,
         16,
         name="grad_slots",
-        marks=pieces[1:3],
+        marks=pieces[1:3] + [starts, proj_starts, chosen_columns, targets_row],
     )
     marked_blocks = lax.all_to_all(marked_blocks, "expert", 0, 0, tiled=True)
     marked = marked_blocks.reshape(total, width + 128)
@@ -822,7 +823,7 @@
             like((tokens, width), NARROW),
             like((tokens, width), NARROW),
         ],
-        [jnp.stack(starts).astype(jnp.int32), block_input, chosen_columns] + pieces,
+        [starts, block_input, chosen_columns] + pieces,
         10 * tokens * width * width,
         4 * width * wide,
         58,
@@ -834,7 +835,7 @@
         functools.partial(middle_body, experts, len(proj_pieces)),
         [like((width, width), NARROW), like((tokens, width), WIDE), like((tokens, width), NARROW)]
         + [like((slots, width), NARROW)] * experts,
-        [proj_starts.astype(jnp.int32), context, block_input, vec, targets_row] + proj_pieces,
+        [proj_starts, context, block_input, vec, targets_row] + proj_pieces,
         4 * tokens * width * width,
         4 * width * width,
         58,

time: 216 us -> 215 us (level)
  waiting for transfers between devices: 62 us -> 64.6 us
  local copies, waits for them, and re-layouts: 14.9 us -> 12.7 us
    ppermute x41, waiting for transfers between devices: 51.1 us -> 53.7 us  [swap(): lax.ppermute(values, axis, [(index, index ^ mask) for index in range(size)])]
    unnamed x67 -> x85, local copies, waits for them, and re-layouts: 8.52 us -> 8.74 us
  transfers between devices with their start and end apart: 44 -> 44, of which waited for: 20 -> 21; matrix products, arithmetic and copies ran while one was open for 5% -> 4% of each run, Pallas kernels for 30% -> 30%
where the time goes in v5:
time: 215 us; the launch traced here: 214 us
  Pallas kernels  72.9 us (34%)
  waiting for transfers between devices  64.6 us (30%)
  starting transfers between devices  60.7 us (28%)
  local copies, waits for them, and re-layouts  12.7 us (6%)
  other arithmetic  2.31 us (1%)
    ppermute x41, waiting for transfers between devices, swap(): lax.ppermute(values, axis, [(index, index ^ mask) for index in range(size)])  53.7 us
    ppermute x41, starting transfers between devices, swap(): lax.ppermute(values, axis, [(index, index ^ mask) for index in range(size)])  46 us
    pallas_call x13, Pallas kernels, run(): pl.pallas_call(marked_body, out_shape=outs, in_specs=[SMEM] * scalars + [...  39.6 us
    pallas_call x1, Pallas kernels, expert_weights(): pl.pallas_call(functools.partial(weights_body, count), grid_spec=pltpu.Pr...  19 us
    pallas_call x1, Pallas kernels, expert(): pl.pallas_call(functools.partial(expert_body, experts, spare), grid=(hidd...  14.4 us
    all_to_all x1, waiting for transfers between devices, per_device(): d_returned = lax.all_to_all(d_expert_in, 'expert', 0, 0, tiled=True)  10.9 us
    unnamed x85, local copies, waits for them, and re-layouts  8.74 us
    all_to_all x1, starting transfers between devices, per_device(): d_returned = lax.all_to_all(d_expert_in, 'expert', 0, 0, tiled=True)  6.09 us
  transfers between devices with their start and end apart: 44, of which 21 were waited for; matrix products, arithmetic and copies ran while one was open for 4% of the time, Pallas kernels for 30%

profile of v5, /device:TPU:0, one launch (start us, length us, event | category | flops | bytes accessed | tf_op | source)
XLA Modules:
  0.0 214.4 jit_solution(17855343075214768698)
XLA Ops:
  0.7 2.6 %pack.1 = (bf16[192,2432]{1,0:T(8,128)(2,1)}, bf16[96,2432]{1,0:T(8,128)(2,1)}) custom-call(s32[1]{0:T(128)} %bitcast.9.refs_0_, bf16[192,2304]{1,0:T(8,128)(2,1)} %refs_1_.3, bf16[8,192]{1,0:T(8,128)(2,1)} %bitcast.40, bf16[192]{0:T(256)(128)(2,1)} %refs_3_.1, bf16[192]{0:T(256)(128)(2,1)} %refs_4_.1, bf16[192]{0:T(256)(128)(2,1)} %refs_5_.2, ...), custom_call_target="tpu_custom_call" | custom-call | flops 1 | bytes 1 | tf_op jit(solution)/shard_map/pack/pallas_call | solution.py:123
  3.3 3.0 %collective-permute-start.1 = (bf16[96,2432]{1,0:T(8,128)(2,1)}, bf16[96,2432]{1,0:T(8,128)(2,1)S(1)}, u32[]{:S(2)}, u32[]{:S(2)}) collective-permute-start(bf16[96,2432]{1,0:T(8,128)(2,1)} %get-tuple-element.123), channel_id=1, source_target_pairs={{0,16},{8,24},{16,0},{24,8},{1,17},{9,25},{17,1},{25,9},{2,18},{10... | collective-permute-start | bytes 1400840 | tf_op jit(solution)/shard_map/ppermute | solution.py:45
  12.4 4.7 %collective-permute-done.1.refs_5_.refs_4_ = bf16[96,2432]{1,0:T(8,128)(2,1)S(1)} collective-permute-done((bf16[96,2432]{1,0:T(8,128)(2,1)}, bf16[96,2432]{1,0:T(8,128)(2,1)S(1)}, u32[]{:S(2)}, u32[]{:S(2)}) %collective-permute-start.1) | collective-permute-done | bytes 466976 | tf_op jit(solution)/shard_map/ppermute | solution.py:45
  20.1 4.9 %all-to-all-start = ((bf16[8,56,896]{2,1,0:T(8,128)(2,1)}), bf16[8,56,896]{2,1,0:T(8,128)(2,1)S(1)}, u32[]{:S(2)}, u32[]{:S(2)}) async-start(bf16[8,56,896]{2,1,0:T(8,128)(2,1)} %grad_slots.1), calls=%async_computation | async-start | bytes 1605632 | tf_op jit(solution)/shard_map/all_to_all | solution.py:812
  27.4 5.8 %collective-permute-done.3.refs_7_ = bf16[48,2432]{1,0:T(8,128)(2,1)S(1)} collective-permute-done((bf16[48,2432]{1,0:T(8,128)(2,1)S(1)}, bf16[48,2432]{1,0:T(8,128)(2,1)S(1)}, u32[]{:S(2)}, u32[]{:S(2)}) %collective-permute-start.3) | collective-permute-done | bytes 233504 | tf_op jit(solution)/shard_map/ppermute | solution.py:45
  40.6 6.6 %attend.1 = (bf16[768,2304]{1,0:T(8,128)(2,1)}, f32[32,768]{1,0:T(8,128)}, bf16[197,2304]{1,0:T(8,128)(2,1)}, bf16[197,768]{1,0:T(8,128)(2,1)}, f32[197,128]{1,0...) custom-call(s32[9]{0:T(128)} %copy-done.16, bf16[197,768]{1,0:T(8,128)(2,1)} %refs_12_.1, ...), custom_call_target="tpu_custom_call" | custom-call | flops 1 | bytes 1 | tf_op jit(solution)/shard_map/attend/pallas_call | solution.py:123
  47.3 2.9 %collective-permute-done.9.refs_7_ = bf16[192,768]{1,0:T(8,128)(2,1)S(1)} collective-permute-done((bf16[192,768]{1,0:T(8,128)(2,1)S(1)}, bf16[192,768]{1,0:T(8,128)(2,1)S(1)}, u32[]{:S(2)}, u32[]{:S(2)}) %collective-permute-start.9) | collective-permute-done | bytes 294944 | tf_op jit(solution)/shard_map/ppermute | solution.py:45
  51.0 3.4 %middle.1 = (bf16[768,768]{1,0:T(8,128)(2,1)}, f32[197,768]{1,0:T(8,128)}, bf16[197,768]{1,0:T(8,128)(2,1)}, bf16[56,768]{1,0:T(8,128)(2,1)}, bf16[56,768]{1,0:T...) custom-call(s32[4]{0:T(128)} %copy-done.17, ...), custom_call_target="tpu_custom_call" | custom-call | flops 1 | bytes 1 | tf_op jit(solution)/shard_map/middle/pallas_call | solution.py:123
  58.1 2.6 %collective-permute-start.14 = (bf16[56,768]{1,0:T(8,128)(2,1)}, bf16[56,768]{1,0:T(8,128)(2,1)S(1)}, u32[]{:S(2)}, u32[]{:S(2)}) collective-permute-start(bf16[56,768]{1,0:T(8,128)(2,1)} %get-tuple-element.133), channel_id=1, source_target_pairs={{0,4},{1,5},{2,6},{3,7},{4,0},{5,1},{6,2},{7,3},{8,12},{9,13},{10,... | collective-permute-start | bytes 258056 | tf_op jit(solution)/shard_map/ppermute | solution.py:45
  64.8 2.8 %collective-permute-start.16 = (bf16[56,768]{1,0:T(8,128)(2,1)}, bf16[56,768]{1,0:T(8,128)(2,1)S(1)}, u32[]{:S(2)}, u32[]{:S(2)}) collective-permute-start(bf16[56,768]{1,0:T(8,128)(2,1)} %get-tuple-element.135), channel_id=1, source_target_pairs={{0,6},{1,7},{2,4},{3,5},{4,2},{5,3},{6,0},{7,1},{8,14},{9,15},{10,... | collective-permute-start | bytes 258056 | tf_op jit(solution)/shard_map/ppermute | solution.py:45
  68.4 4.1 %collective-permute-done.15.refs_6_ = bf16[56,768]{1,0:T(8,128)(2,1)S(1)} collective-permute-done((bf16[56,768]{1,0:T(8,128)(2,1)}, bf16[56,768]{1,0:T(8,128)(2,1)S(1)}, u32[]{:S(2)}, u32[]{:S(2)}) %collective-permute-start.15) | collective-permute-done | bytes 86048 | tf_op jit(solution)/shard_map/ppermute | solution.py:45
  78.5 14.4 %expert.1 = (bf16[8,56,768]{2,1,0:T(8,128)(2,1)}, bf16[8,56,768]{2,1,0:T(8,128)(2,1)}) custom-call(s32[2]{0:T(128)} %copy-done.14, bf16[448,768]{1,0:T(8,128)(2,1)} %copy-done, bf16[448,896]{1,0:T(8,128)(2,1)} %bitcast.37, f32[32,768]{1,0:T(8,128)} %get-tuple-element.127.refs_3_.vec_ref, bf16[768,3072]{1,0:T(8,128)(2,1)} %bitcast.31, ...), custom_call_target="tpu_custom_call" | custom-call | flops 1 | bytes 1 | tf_op jit(solution)/shard_map/expert/pallas_call | solution.py:358
  95.8 6.1 %all-to-all-start.1 = ((bf16[8,56,768]{2,1,0:T(8,128)(2,1)}), bf16[8,56,768]{2,1,0:T(8,128)(2,1)S(1)}, u32[]{:S(2)}, u32[]{:S(2)}) async-start(bf16[8,56,768]{2,1,0:T(8,128)(2,1)} %get-tuple-element.150), calls=%async_computation.1 | async-start | bytes 1376256 | tf_op jit(solution)/shard_map/all_to_all | solution.py:868
  109.8 10.9 %all-to-all-done.1.refs_8_ = bf16[8,56,768]{2,1,0:T(8,128)(2,1)S(1)} async-done(((bf16[8,56,768]{2,1,0:T(8,128)(2,1)}), bf16[8,56,768]{2,1,0:T(8,128)(2,1)S(1)}, u32[]{:S(2)}, u32[]{:S(2)}) %all-to-all-start.1) | async-done | bytes 688160 | tf_op jit(solution)/shard_map/all_to_all | solution.py:868
  121.6 11.8 %backward.1 = (f32[197,128]{1,0:T(8,128)}, f32[197,768]{1,0:T(8,128)}, bf16[240,3072]{1,0:T(8,128)(2,1)}) custom-call(f32[197,768]{1,0:T(8,128)} %get-tuple-element.155.refs_0_, bf16[197,768]{1,0:T(8,128)(2,1)} %get-tuple-element.156.refs_1_, bf16[197,768]{1,0:T(8,128)(2,1)} %refs_2_.3, f32[32,768]{1,0:T(8,128)} %get-tuple-element.127.refs_3_.vec_ref, ...), custom_call_target="tpu_custom_call" | custom-call | flops 1 | bytes 1 | tf_op jit(solution)/shard_map/backward/pallas_call | solution.py:123
  134.4 3.8 %all-to-all-start.2 = ((bf16[8,56,768]{2,1,0:T(8,128)(2,1)}), bf16[8,56,768]{2,1,0:T(8,128)(2,1)S(1)}, u32[]{:S(2)}, u32[]{:S(2)}) async-start(bf16[8,56,768]{2,1,0:T(8,128)(2,1)} %get-tuple-element.185), calls=%async_computation.2 | async-start | bytes 1376256 | tf_op jit(solution)/shard_map/all_to_all | solution.py:898
  139.3 5.9 %outer.1 = (f32[96,3200]{1,0:T(8,128)}, bf16[96,3200]{1,0:T(8,128)(2,1)}, bf16[96,3200]{1,0:T(8,128)(2,1)}, bf16[96,3200]{1,0:T(8,128)(2,1)}) custom-call(s32[1,768]{1,0:T(1,128)} %copy-done.12, bf16[197,768]{1,0:T(8,128)(2,1)} %get-tuple-element.125.refs_1_, bf16[197,768]{1,0:T(8,128)(2,1)} %collective-permute-done.22.refs_2_, ...), custom_call_target="tpu_custom_call" | custom-call | flops 1 | bytes 1 | tf_op jit(solution)/shard_map/outer/pallas_call | solution.py:123
  148.7 19.0 %expert_weights.1 = (f32[768,768]{1,0:T(8,128)}, f32[192,768]{1,0:T(8,128)}, bf16[192,768]{1,0:T(8,128)(2,1)}, bf16[192,768]{1,0:T(8,128)(2,1)}, bf16[192,768]{1...) custom-call(s32[2]{0:T(128)} %copy-done.14, bf16[96,3200]{1,0:T(8,128)(2,1)} %get-tuple-element.170.mark_ref, ...), custom_call_target="tpu_custom_call" | custom-call | flops 1 | bytes 1 | tf_op jit(solution)/shard_map/expert_weights/pallas_call | solution.py:430
  169.1 5.6 %collective-permute-done.29.refs_2_ = bf16[96,3200]{1,0:T(8,128)(2,1)S(1)} collective-permute-done((bf16[96,3200]{1,0:T(8,128)(2,1)}, bf16[96,3200]{1,0:T(8,128)(2,1)S(1)}, u32[]{:S(2)}, u32[]{:S(2)}) %collective-permute-start.29) | collective-permute-done | bytes 614432 | tf_op jit(solution)/shard_map/ppermute | solution.py:45
  180.0 2.4 %collective-permute-start.32 = (bf16[24,3200]{1,0:T(8,128)(2,1)S(1)}, bf16[24,3200]{1,0:T(8,128)(2,1)S(1)}, u32[]{:S(2)}, u32[]{:S(2)}) collective-permute-start(bf16[24,3200]{1,0:T(8,128)(2,1)S(1)} %get-tuple-element.200), channel_id=1, source_target_pairs={{0,4},{1,5},{2,6},{3,7},{4,0},{5,1},{6,2},{7,3},{8,12},{9,13},{10,... | collective-permute-start | bytes 460808 | tf_op jit(solution)/shard_map/ppermute | solution.py:45
  186.2 7.3 %collective-permute-done.32.refs_2_ = bf16[24,3200]{1,0:T(8,128)(2,1)S(1)} collective-permute-done((bf16[24,3200]{1,0:T(8,128)(2,1)S(1)}, bf16[24,3200]{1,0:T(8,128)(2,1)S(1)}, u32[]{:S(2)}, u32[]{:S(2)}) %collective-permute-start.32) | collective-permute-done | bytes 153632 | tf_op jit(solution)/shard_map/ppermute | solution.py:45
  193.5 2.5 %collective-permute-start.36 = (bf16[24,3200]{1,0:T(8,128)(2,1)S(1)}, bf16[24,3200]{1,0:T(8,128)(2,1)S(1)}, u32[]{:S(2)}, u32[]{:S(2)}) collective-permute-start(bf16[24,3200]{1,0:T(8,128)(2,1)S(1)} %sum_blocks.3.refs_5_.refs_4_.refs_0_), channel_id=1, source_target_pairs={{0,6},{1,7},{2,4},{3,5},{4,2},{5,3},{6,0},{7,1},{8,14},{9,15},{10,... | collective-permute-start | bytes 460808 | tf_op jit(solution)/shard_map/ppermute | solution.py:45
  196.0 2.9 %collective-permute-start.35 = (bf16[24,3200]{1,0:T(8,128)(2,1)S(1)}, bf16[24,3200]{1,0:T(8,128)(2,1)S(1)}, u32[]{:S(2)}, u32[]{:S(2)}) collective-permute-start(bf16[24,3200]{1,0:T(8,128)(2,1)S(1)} %sum_blocks.3.refs_5_.refs_4_.refs_0_), channel_id=1, source_target_pairs={{0,4},{1,5},{2,6},{3,7},{4,0},{5,1},{6,2},{7,3},{8,12},{9,13},{10,... | collective-permute-start | bytes 460808 | tf_op jit(solution)/shard_map/ppermute | solution.py:45
  202.4 7.2 %collective-permute-done.35.refs_2_ = bf16[24,3200]{1,0:T(8,128)(2,1)S(1)} collective-permute-done((bf16[24,3200]{1,0:T(8,128)(2,1)S(1)}, bf16[24,3200]{1,0:T(8,128)(2,1)S(1)}, u32[]{:S(2)}, u32[]{:S(2)}) %collective-permute-start.35) | collective-permute-done | bytes 153632 | tf_op jit(solution)/shard_map/ppermute | solution.py:45
  (192 shorter events, 70.2 us)
Async XLA Ops:
  3.3 13.9 %collective-permute-start.1 = (bf16[96,2432]{1,0:T(8,128)(2,1)}, bf16[96,2432]{1,0:T(8,128)(2,1)S(1)}, u32[]{:S(2)}, u32[]{:S(2)}) collective-permute-start(bf16[96,2432]{1,0:T(8,128)(2,1)} %get-tuple-element.123), channel_id=1, source_target_pairs={{0,16},{8,24},{16,0},{24,8},{1,17},{9,25},{17,1},{25,9},{2,18},{10... | collective-permute-start | bytes 1400840 | tf_op jit(solution)/shard_map/ppermute | solution.py:45
  6.3 12.4 %collective-permute-start = (bf16[96,2432]{1,0:T(8,128)(2,1)}, bf16[96,2432]{1,0:T(8,128)(2,1)S(1)}, u32[]{:S(2)}, u32[]{:S(2)}) collective-permute-start(bf16[96,2432]{1,0:T(8,128)(2,1)} %get-tuple-element.123), channel_id=1, source_target_pairs={{0,8},{8,0},{16,24},{24,16},{1,9},{9,1},{17,25},{25,17},{2,10},{10... | collective-permute-start | bytes 1400840 | tf_op jit(solution)/shard_map/ppermute | solution.py:45
  20.1 34.2 %all-to-all-start = ((bf16[8,56,896]{2,1,0:T(8,128)(2,1)}), bf16[8,56,896]{2,1,0:T(8,128)(2,1)S(1)}, u32[]{:S(2)}, u32[]{:S(2)}) async-start(bf16[8,56,896]{2,1,0:T(8,128)(2,1)} %grad_slots.1), calls=%async_computation | async-start | bytes 1605632 | tf_op jit(solution)/shard_map/all_to_all | solution.py:812
  34.8 12.5 %collective-permute-start.10 = (bf16[192,768]{1,0:T(8,128)(2,1)S(1)}, bf16[192,768]{1,0:T(8,128)(2,1)S(1)}, u32[]{:S(2)}, u32[]{:S(2)}) collective-permute-start(bf16[192,768]{1,0:T(8,128)(2,1)S(1)} %copy-done.30), channel_id=1, source_target_pairs={{0,24},{8,16},{16,8},{24,0},{1,25},{9,17},{17,9},{25,1},{2,26},{10... | collective-permute-start | bytes 884744 | tf_op jit(solution)/shard_map/ppermute | solution.py:45
  35.2 14.9 %collective-permute-start.9 = (bf16[192,768]{1,0:T(8,128)(2,1)S(1)}, bf16[192,768]{1,0:T(8,128)(2,1)S(1)}, u32[]{:S(2)}, u32[]{:S(2)}) collective-permute-start(bf16[192,768]{1,0:T(8,128)(2,1)S(1)} %copy-done.30), channel_id=1, source_target_pairs={{0,16},{8,24},{16,0},{24,8},{1,17},{9,25},{17,1},{25,9},{2,18},{10... | collective-permute-start | bytes 884744 | tf_op jit(solution)/shard_map/ppermute | solution.py:45
  36.8 13.4 %collective-permute-start.8 = (bf16[192,768]{1,0:T(8,128)(2,1)S(1)}, bf16[192,768]{1,0:T(8,128)(2,1)S(1)}, u32[]{:S(2)}, u32[]{:S(2)}) collective-permute-start(bf16[192,768]{1,0:T(8,128)(2,1)S(1)} %copy-done.30), channel_id=1, source_target_pairs={{0,8},{8,0},{16,24},{24,16},{1,9},{9,1},{17,25},{25,17},{2,10},{10... | collective-permute-start | bytes 884744 | tf_op jit(solution)/shard_map/ppermute | solution.py:45
  54.3 19.7 %collective-permute-start.19 = (bf16[448,896]{1,0:T(8,128)(2,1)S(1)}, bf16[448,896]{1,0:T(8,128)(2,1)S(1)}, u32[]{:S(2)}, u32[]{:S(2)}) collective-permute-start(bf16[448,896]{1,0:T(8,128)(2,1)S(1)} %bitcast.35), channel_id=1, source_target_pairs={{0,16},{8,24},{16,0},{24,8},{1,17},{9,25},{17,1},{25,9},{2,18},{10... | collective-permute-start | bytes 2408456 | tf_op jit(solution)/shard_map/ppermute | solution.py:45
  55.1 19.5 %collective-permute-start.18 = (bf16[448,896]{1,0:T(8,128)(2,1)S(1)}, bf16[448,896]{1,0:T(8,128)(2,1)S(1)}, u32[]{:S(2)}, u32[]{:S(2)}) collective-permute-start(bf16[448,896]{1,0:T(8,128)(2,1)S(1)} %bitcast.36), channel_id=1, source_target_pairs={{0,8},{8,0},{16,24},{24,16},{1,9},{9,1},{17,25},{25,17},{2,10},{10... | collective-permute-start | bytes 2408456 | tf_op jit(solution)/shard_map/ppermute | solution.py:45
  76.4 17.2 %collective-permute-start.21 = (bf16[448,768]{1,0:T(8,128)(2,1)S(1)}, bf16[448,768]{1,0:T(8,128)(2,1)S(1)}, u32[]{:S(2)}, u32[]{:S(2)}) collective-permute-start(bf16[448,768]{1,0:T(8,128)(2,1)S(1)} %order.1.rows_ref.refs_0_), channel_id=1, source_target_pairs={{0,16},{8,24},{16,0},{24,8},{1,17},{9,25},{17,1},{25,9},{2,18},{10... | collective-permute-start | bytes 2064392 | tf_op jit(solution)/shard_map/ppermute | solution.py:45
  77.5 17.3 %collective-permute-start.20 = (bf16[448,768]{1,0:T(8,128)(2,1)S(1)}, bf16[448,768]{1,0:T(8,128)(2,1)S(1)}, u32[]{:S(2)}, u32[]{:S(2)}) collective-permute-start(bf16[448,768]{1,0:T(8,128)(2,1)S(1)} %order.1.rows_ref.refs_0_), channel_id=1, source_target_pairs={{0,8},{8,0},{16,24},{24,16},{1,9},{9,1},{17,25},{25,17},{2,10},{10... | collective-permute-start | bytes 2064392 | tf_op jit(solution)/shard_map/ppermute | solution.py:45
  95.8 25.0 %all-to-all-start.1 = ((bf16[8,56,768]{2,1,0:T(8,128)(2,1)}), bf16[8,56,768]{2,1,0:T(8,128)(2,1)S(1)}, u32[]{:S(2)}, u32[]{:S(2)}) async-start(bf16[8,56,768]{2,1,0:T(8,128)(2,1)} %get-tuple-element.150), calls=%async_computation.1 | async-start | bytes 1376256 | tf_op jit(solution)/shard_map/all_to_all | solution.py:868
  102.7 30.8 %collective-permute-start.26 = (bf16[224,896]{1,0:T(8,128)(2,1)}, bf16[224,896]{1,0:T(8,128)(2,1)S(1)}, u32[]{:S(2)}, u32[]{:S(2)}) collective-permute-start(bf16[224,896]{1,0:T(8,128)(2,1)} %slice.23), channel_id=1, source_target_pairs={{0,8},{8,0},{16,24},{24,16},{1,9},{9,1},{17,25},{25,17},{2,10},{10... | collective-permute-start | bytes 1204232 | tf_op jit(solution)/shard_map/ppermute | solution.py:45
  103.5 30.0 %collective-permute-start.25 = (bf16[224,896]{1,0:T(8,128)(2,1)S(1)}, bf16[224,896]{1,0:T(8,128)(2,1)S(1)}, u32[]{:S(2)}, u32[]{:S(2)}) collective-permute-start(bf16[224,896]{1,0:T(8,128)(2,1)S(1)} %slice.22), channel_id=1, source_target_pairs={{0,16},{8,24},{16,0},{24,8},{1,17},{9,25},{17,1},{25,9},{2,18},{10... | collective-permute-start | bytes 1204232 | tf_op jit(solution)/shard_map/ppermute | solution.py:45
  105.7 27.7 %collective-permute-start.24 = (bf16[224,768]{1,0:T(8,128)(2,1)S(1)}, bf16[224,768]{1,0:T(8,128)(2,1)}, u32[]{:S(2)}, u32[]{:S(2)}) collective-permute-start(bf16[224,768]{1,0:T(8,128)(2,1)S(1)} %slice.21), channel_id=1, source_target_pairs={{0,8},{8,0},{16,24},{24,16},{1,9},{9,1},{17,25},{25,17},{2,10},{10... | collective-permute-start | bytes 1032200 | tf_op jit(solution)/shard_map/ppermute | solution.py:45
  106.3 27.1 %collective-permute-start.23 = (bf16[224,768]{1,0:T(8,128)(2,1)S(1)}, bf16[224,768]{1,0:T(8,128)(2,1)}, u32[]{:S(2)}, u32[]{:S(2)}) collective-permute-start(bf16[224,768]{1,0:T(8,128)(2,1)S(1)} %slice.20), channel_id=1, source_target_pairs={{0,16},{8,24},{16,0},{24,8},{1,17},{9,25},{17,1},{25,9},{2,18},{10... | collective-permute-start | bytes 1032200 | tf_op jit(solution)/shard_map/ppermute | solution.py:45
  134.4 34.7 %all-to-all-start.2 = ((bf16[8,56,768]{2,1,0:T(8,128)(2,1)}), bf16[8,56,768]{2,1,0:T(8,128)(2,1)S(1)}, u32[]{:S(2)}, u32[]{:S(2)}) async-start(bf16[8,56,768]{2,1,0:T(8,128)(2,1)} %get-tuple-element.185), calls=%async_computation.2 | async-start | bytes 1376256 | tf_op jit(solution)/shard_map/all_to_all | solution.py:898
  145.2 29.6 %collective-permute-start.29 = (bf16[96,3200]{1,0:T(8,128)(2,1)}, bf16[96,3200]{1,0:T(8,128)(2,1)S(1)}, u32[]{:S(2)}, u32[]{:S(2)}) collective-permute-start(bf16[96,3200]{1,0:T(8,128)(2,1)} %get-tuple-element.171), channel_id=1, source_target_pairs={{0,16},{8,24},{16,0},{24,8},{1,17},{9,25},{17,1},{25,9},{2,18},{10... | collective-permute-start | bytes 1843208 | tf_op jit(solution)/shard_map/ppermute | solution.py:45
  145.8 29.0 %collective-permute-start.30 = (bf16[96,3200]{1,0:T(8,128)(2,1)}, bf16[96,3200]{1,0:T(8,128)(2,1)}, u32[]{:S(2)}, u32[]{:S(2)}) collective-permute-start(bf16[96,3200]{1,0:T(8,128)(2,1)} %get-tuple-element.172), channel_id=1, source_target_pairs={{0,24},{8,16},{16,8},{24,0},{1,25},{9,17},{17,9},{25,1},{2,26},{10... | collective-permute-start | bytes 1843208 | tf_op jit(solution)/shard_map/ppermute | solution.py:45
  147.5 28.6 %collective-permute-start.28 = (bf16[96,3200]{1,0:T(8,128)(2,1)}, bf16[96,3200]{1,0:T(8,128)(2,1)}, u32[]{:S(2)}, u32[]{:S(2)}) collective-permute-start(bf16[96,3200]{1,0:T(8,128)(2,1)} %get-tuple-element.170.mark_ref), channel_id=1, source_target_pairs={{0,8},{8,0},{16,24},{24,16},{1,9},{9,1},{17,25},{25,17},{2,10},{10... | collective-permute-start | bytes 1843208 | tf_op jit(solution)/shard_map/ppermute | solution.py:45
  179.2 19.7 %collective-permute-start.37 = (bf16[192,768]{1,0:T(8,128)(2,1)S(1)}, bf16[192,768]{1,0:T(8,128)(2,1)S(1)}, u32[]{:S(2)}, u32[]{:S(2)}) collective-permute-start(bf16[192,768]{1,0:T(8,128)(2,1)S(1)} %copy-done.40), channel_id=1, source_target_pairs={{0,8},{8,0},{16,24},{24,16},{1,9},{9,1},{17,25},{25,17},{2,10},{10... | collective-permute-start | bytes 884744 | tf_op jit(solution)/shard_map/ppermute | solution.py:45
  180.0 13.4 %collective-permute-start.32 = (bf16[24,3200]{1,0:T(8,128)(2,1)S(1)}, bf16[24,3200]{1,0:T(8,128)(2,1)S(1)}, u32[]{:S(2)}, u32[]{:S(2)}) collective-permute-start(bf16[24,3200]{1,0:T(8,128)(2,1)S(1)} %get-tuple-element.200), channel_id=1, source_target_pairs={{0,4},{1,5},{2,6},{3,7},{4,0},{5,1},{6,2},{7,3},{8,12},{9,13},{10,... | collective-permute-start | bytes 460808 | tf_op jit(solution)/shard_map/ppermute | solution.py:45
  182.9 17.3 %collective-permute-start.38 = (bf16[192,768]{1,0:T(8,128)(2,1)S(1)}, bf16[192,768]{1,0:T(8,128)(2,1)S(1)}, u32[]{:S(2)}, u32[]{:S(2)}) collective-permute-start(bf16[192,768]{1,0:T(8,128)(2,1)S(1)} %copy-done.39), channel_id=1, source_target_pairs={{0,16},{8,24},{16,0},{24,8},{1,17},{9,25},{17,1},{25,9},{2,18},{10... | collective-permute-start | bytes 884744 | tf_op jit(solution)/shard_map/ppermute | solution.py:45
  184.5 15.8 %collective-permute-start.39 = (bf16[192,768]{1,0:T(8,128)(2,1)S(1)}, bf16[192,768]{1,0:T(8,128)(2,1)S(1)}, u32[]{:S(2)}, u32[]{:S(2)}) collective-permute-start(bf16[192,768]{1,0:T(8,128)(2,1)S(1)} %copy-done.38), channel_id=1, source_target_pairs={{0,24},{8,16},{16,8},{24,0},{1,25},{9,17},{17,9},{25,1},{2,26},{10... | collective-permute-start | bytes 884744 | tf_op jit(solution)/shard_map/ppermute | solution.py:45
  196.0 13.6 %collective-permute-start.35 = (bf16[24,3200]{1,0:T(8,128)(2,1)S(1)}, bf16[24,3200]{1,0:T(8,128)(2,1)S(1)}, u32[]{:S(2)}, u32[]{:S(2)}) collective-permute-start(bf16[24,3200]{1,0:T(8,128)(2,1)S(1)} %sum_blocks.3.refs_5_.refs_4_.refs_0_), channel_id=1, source_target_pairs={{0,4},{1,5},{2,6},{3,7},{4,0},{5,1},{6,2},{7,3},{8,12},{9,13},{10,... | collective-permute-start | bytes 460808 | tf_op jit(solution)/shard_map/ppermute | solution.py:45
  (61 other events, 699.0 us)
